TPU v7x, 256 devices: a whole 4x4x8 slice. The times are simulated.
256 devices in a mesh: ens: 8 (over x, core), lat: 32 (over z, y).
Axes of the slice: x: 4, y: 4, z: 8, core: 2. Of those that a mesh axis runs over, the one named last changes fastest.
Arguments:
- fields: bfloat16 [16, 24, 192, 1440], P('ens', None, 'lat'), may hold values from -6 to 6
- depth_kernel: float32 [24, 7, 7], replicated, may hold values from -0.875 to 0.875
- mix_weight: bfloat16 [24, 24], replicated, may hold values from -1.25 to 1.25
- legendre: bfloat16 [192, 160, 160], P('lat'), may hold values from -0.875 to 0.875
- truth: bfloat16 [24, 2, 160, 160], replicated, may hold values from -6 to 6
- degree_order: int32 [160], replicated, may hold values from 0 to 159, each once
Outputs:
- grad_fields: bfloat16 [16, 24, 192, 1440], P('ens', None, 'lat')
- score_grad: float32 [16, 24, 2, 160, 160], P('ens', None, None, None, 'lat')
Inputs may be any that keep to these rules, and one draw needn't show every extreme that they name: `degree_order`: each degree appears once.
All inputs are finite; a program needn't handle non-finite values.
Results may differ from a plain program's by a relative error of at most 0.02.
Values may be sent and summed in bfloat16 or wider, within the bound.
A program may use at most 128 MiB of HBM per device.

v0:
```python
import math

import jax
import jax.numpy as jnp
from jax import lax
from jax.sharding import PartitionSpec as P

NLON = 1440
M = 160
L = 160


smooth_width = 0.5


def padded_2(block, sides, width):
    for axis, dim in sides:
        count = lax.axis_size(axis)
        forward = [(i, i + 1) for i in range(count - 1)]
        backward = [(target, source) for source, target in forward]
        low = lax.ppermute(
            lax.slice_in_dim(block, block.shape[dim] - width, None, axis=dim), axis, forward
        )
        high = lax.ppermute(lax.slice_in_dim(block, 0, width, axis=dim), axis, backward)
        block = jnp.concatenate([low, block, high], axis=dim)
    return block


def wave_table():
    columns = jnp.arange(NLON, dtype=jnp.int32)
    orders = jnp.arange(M, dtype=jnp.int32)
    angles = (columns[:, None] * orders[None, :] % NLON).astype(jnp.float32) * (
        2.0 * math.pi / NLON
    )
    return (jnp.concatenate([jnp.cos(angles), -jnp.sin(angles)], axis=1) / math.sqrt(NLON)).astype(
        jnp.bfloat16
    )


def depthwise(padded, kernel):
    height = padded.shape[-2] - 6
    breadth = padded.shape[-1]
    widened = jnp.concatenate([padded[..., -3:], padded, padded[..., :3]], axis=-1)
    running = jnp.zeros(padded.shape[:-2] + (height, breadth), jnp.float32)
    for row_off in range(7):
        for col_off in range(7):
            running = (
                running
                + kernel[:, row_off, col_off][:, None, None]
                * widened[..., row_off : row_off + height, col_off : col_off + breadth]
            )
    return running


def soft_sign(gaps):
    return gaps / jnp.sqrt(gaps * gaps + smooth_width * smooth_width)


def member_score(own_coeff, everyone, target):
    ens_count = everyone.shape[0]
    pair_sum = jnp.sum(soft_sign(own_coeff[:, None] - everyone[None]), axis=1)
    return soft_sign(own_coeff - target[None]) / ens_count - pair_sum / (
        ens_count * (ens_count - 1)
    )


def local(fields, depth_kernel, mix_weight, legendre, truth, degree_order):
    table = wave_table()
    per_owner = L // lax.axis_size("lat")
    owned = lax.dynamic_slice_in_dim(degree_order, lax.axis_index("lat") * per_owner, per_owner)
    ordered = jnp.take(legendre, degree_order, axis=2)
    padded = padded_2(fields, (("lat", 2),), 3).astype(jnp.float32)
    hidden = padded[:, :, 3:-3] + depthwise(padded, depth_kernel)
    activation = jax.nn.gelu(hidden).astype(jnp.bfloat16)
    mixed_out = jnp.einsum(
        "oc,bcij->boij", mix_weight, activation, preferred_element_type=jnp.float32
    ).astype(jnp.bfloat16)
    spectral = jnp.dot(mixed_out, table, preferred_element_type=jnp.float32).astype(jnp.bfloat16)
    spectral = spectral.reshape(spectral.shape[:3] + (2, M))
    partial_sum = jnp.einsum(
        "bcirm,iml->bcrml", spectral, ordered, preferred_element_type=jnp.float32
    )
    coeff = lax.psum_scatter(
        partial_sum.astype(jnp.bfloat16), "lat", scatter_dimension=4, tiled=True
    ).astype(jnp.float32)
    target = jnp.take(truth, owned, axis=3).astype(jnp.float32)
    share = coeff.shape[1] // lax.axis_size("ens")
    pooled = lax.all_to_all(
        coeff.astype(jnp.bfloat16), "ens", split_axis=1, concat_axis=0, tiled=True
    ).astype(coeff.dtype)
    piece_target = lax.dynamic_slice_in_dim(target, lax.axis_index("ens") * share, share, 0)
    pooled_grad = member_score(pooled, pooled, piece_target)
    gradient = lax.all_to_all(
        pooled_grad.astype(jnp.bfloat16), "ens", split_axis=0, concat_axis=1, tiled=True
    ).astype(pooled_grad.dtype)
    sent = gradient.astype(jnp.bfloat16)
    all_degrees = lax.all_gather(sent, "lat", axis=4, tiled=True)
    spec_grad = jnp.einsum(
        "bcrml,iml->bcirm", all_degrees, ordered, preferred_element_type=jnp.float32
    ).astype(jnp.bfloat16)
    spec_grad = spec_grad.reshape(spec_grad.shape[:3] + (2 * M,))
    mix_grad = jnp.dot(spec_grad, table.T, preferred_element_type=jnp.float32).astype(jnp.bfloat16)
    act_grad = jnp.einsum("oc,boij->bcij", mix_weight, mix_grad, preferred_element_type=jnp.float32)
    hid_grad = jax.vjp(jax.nn.gelu, hidden)[1](act_grad)[0]
    padded_grad = padded_2(hid_grad.astype(jnp.bfloat16), (("lat", 2),), 3).astype(hid_grad.dtype)
    grad_fields = (hid_grad + depthwise(padded_grad, depth_kernel[:, ::-1, ::-1])).astype(
        jnp.bfloat16
    )
    return (grad_fields, gradient)


def solution(mesh):
    placed = (P("ens", None, "lat", None), P(), P(), P("lat", None, None), P(), P())
    return jax.shard_map(
        local,
        mesh=mesh,
        in_specs=placed,
        out_specs=(P("ens", None, "lat", None), P("ens", None, None, None, "lat")),
        check_vma=False,
    )
```

profile of v0, /device:TPU:1, one launch (start us, length us, event | category | flops | bytes accessed | tf_op | source)
XLA Modules:
  0.0 520.9 jit_solution(14257302760006477700)
XLA Ops:
  7.3 1.3 fusion.317
  8.5 4.8 collective-permute-start
  13.4 1.3 collective-permute-start.1
  14.7 0.6 slice_bitcast_fusion.48
  15.3 0.7 slice_bitcast_fusion.47
  16.0 0.5 copy.82
  16.5 0.7 gather_fusion
  17.3 0.2 select_bitcast_fusion
  17.5 0.9 copy.106
  18.4 0.6 slice_bitcast_fusion.46
  19.0 5.7 %sine_negate_fusion = (f32[1440,160]{0,1:T(8,128)}, f32[1440,160]{0,1:T(8,128)}) fusion(), kind=kLoop, calls=%fused_computation.463 | loop fusion | flops 2304000 | bytes 1843200 | tf_op jit(solution)/shard_map/neg | solution.py:35
  25.0 1.1 collective-permute-done.1
  26.1 1.4 maximum_convert_fusion
  27.5 0.2 fusion.315
  27.9 26.7 %fusion.145 = f32[2,24,6,1440]{3,1,2,0:T(8,128)S(1)} fusion(f32[2,24,12,3]{3,1,2,0:T(8,128)S(1)} %get-tuple-element.9, f32[2,24,12,1440]{3,1,2,0:T(8,128)S(1)} %maximum_convert_fusion, f32[2,24,12,3]{3,1,2,0:T(8,128)S(1)} %get-tuple-element.8, f32[24]{0:T(128)} %get-tuple-element.61, f32[24]{0:T(128)} %get-tuple-element.62, f32[24]{0:T(128)S(1)} %get-tuple-element.15, ...), kind=kLoop, calls=%fused_computation.236 | loop fusion | flops 58060800 | bytes 18195296 | tf_op jit(solution)/shard_map/add | solution.py:73
  54.7 3.3 fusion.276
  58.0 0.1 reshape.133
  58.1 1.2 copy.84
  59.3 4.4 convert_bitcast_fusion
  63.6 15.1 %copy.85 = bf16[2,24,2,160,160]{3,1,2,0,4:T(8,128)(2,1)} copy(bf16[2,24,2,160,160]{4,1,2,0,3:T(8,128)(2,1)} %convert_bitcast_fusion) | data formatting | bytes 9830400 | tf_op jit(solution)/shard_map/convert_element_type | solution.py:84
  78.8 7.1 %copy.90 = bf16[24,2,160,160]{2,0,1,3:T(8,128)(2,1)} copy(bf16[24,2,160,160]{3,2,1,0:T(8,128)(2,1)} %param.10) | data formatting | bytes 4915200 | tf_op args[4]
  85.9 2.7 gather_fusion.1
  88.6 218.9 %reduce-scatter.2.cloned.1.call-done = bf16[2,24,2,160,5]{3,1,2,0,4:T(8,128)(2,1)} async-done(((bf16[2,24,2,160,160]{3,1,2,0,4:T(8,128)(2,1)}), bf16[2,24,2,160,5]{3,1,2,0,4:T(8,128)(2,1)}) %reduce-scatter.2.cloned.1.call-update) | async-done | bytes 153616 | tf_op jit(solution)/shard_map/reduce_scatter | solution.py:83
  307.5 1.8 copy.86
  309.3 8.9 %all-to-all-start = ((bf16[2,24,2,160,5]{3,2,4,0,1:T(2,128)(2,1)}), bf16[2,24,2,160,5]{3,2,4,0,1:T(2,128)(2,1)S(1)}, u32[]{:S(2)}, u32[]{:S(2)}) async-start(bf16[2,24,2,160,5]{3,2,4,0,1:T(2,128)(2,1)} %copy.86), calls=%async_computation.1 | async-start | bytes 491520 | tf_op jit(solution)/shard_map/all_to_all | solution.py:88
  318.3 6.3 %all-to-all-done = bf16[2,24,2,160,5]{3,2,4,0,1:T(2,128)(2,1)S(1)} async-done(((bf16[2,24,2,160,5]{3,2,4,0,1:T(2,128)(2,1)}), bf16[2,24,2,160,5]{3,2,4,0,1:T(2,128)(2,1)S(1)}, u32[]{:S(2)}, u32[]{:S(2)}) %all-to-all-start) | async-done | bytes 153632 | tf_op jit(solution)/shard_map/all_to_all | solution.py:88
  324.6 0.3 copy.88
  324.9 0.2 copy.89
  325.2 2.9 fusion.2
  328.1 0.4 fusion.293
  328.6 0.2 copy.96
  328.8 9.8 %all_to_all.27 = bf16[16,3,2,160,5]{3,2,4,1,0:T(2,128)(2,1)S(1)} all-to-all(bf16[16,3,2,160,5]{3,2,4,1,0:T(2,128)(2,1)S(1)} %copy.96), channel_id=1, replica_groups=mesh['ens'=8,'lat'=32] {'ens'}, dimensions={0} | all-to-all | bytes 307200 | tf_op jit(solution)/shard_map/all_to_all | solution.py:93
  338.5 0.2 copy.97
  338.7 0.7 copy.98
  339.4 92.4 %all-gather.2.cloned.1.call-done = bf16[2,24,2,160,160]{3,1,2,0,4:T(8,128)(2,1)} async-done(((bf16[2,24,2,160,5]{3,1,2,0,4:T(8,128)(2,1)}), bf16[2,24,2,160,160]{3,1,2,0,4:T(8,128)(2,1)}) %all-gather.2.cloned.1.call-update) | async-done | bytes 4915216 | tf_op jit(solution)/shard_map/all_gather | solution.py:97
  431.8 25.4 %copy.100 = bf16[2,24,2,160,160]{1,4,2,0,3:T(8,128)(2,1)} copy(bf16[2,24,2,160,160]{3,1,2,0,4:T(8,128)(2,1)} %all-gather.2.cloned.1.call-done) | data formatting | bytes 9830400 | tf_op jit(solution)/shard_map/all_gather | solution.py:97
  457.3 10.2 %fusion.274 = bf16[2,24,6,2,160]{1,2,3,0,4:T(8,128)(2,1)S(1)} fusion(bf16[6,160,160,1,1]{2,0,4,3,1:T(8,128)(2,1)S(1)} %copy.106, bf16[2,24,2,160,160]{1,4,2,0,3:T(8,128)(2,1)} %copy.100), kind=kOutput, calls=%fused_computation.457 | convolution fusion | flops 29583360 | bytes 5406720 | tf_op jit(solution)/shard_map/bcrml,iml->bcirm/dot_general | solution.py:98
  467.5 1.0 copy.101
  468.5 0.2 reshape.134
  468.7 3.9 fusion.318
  472.7 1.9 collective-permute-start.2
  474.6 1.3 collective-permute-start.3
  475.9 0.9 convert_element_type.100
  476.9 6.0 %collective-permute-done.2 = bf16[2,24,3,1440]{3,1,2,0:T(8,128)(2,1)S(1)} collective-permute-done((bf16[2,24,3,1440]{3,1,2,0:T(8,128)(2,1)S(1)}, bf16[2,24,3,1440]{3,1,2,0:T(8,128)(2,1)S(1)}, u32[]{:S(2)}, u32[]{:S(2)}) %collective-permute-start.2) | collective-permute-done | bytes 414752 | tf_op jit(solution)/shard_map/ppermute | solution.py:21
  482.9 3.9 collective-permute-done.3
  486.8 0.3 maximum_convert_fusion.1
  487.1 0.2 fusion.314
  487.3 26.8 %fusion.16 = bf16[2,24,6,1440]{3,1,2,0:T(8,128)(2,1)} fusion(f32[2,24,6,1440]{3,1,2,0:T(8,128)S(1)} %get-tuple-element.64, f32[2,24,12,3]{3,1,2,0:T(8,128)S(1)} %get-tuple-element.7, f32[2,24,12,1440]{3,1,2,0:T(8,128)S(1)} %maximum_convert_fusion.1, f32[2,24,12,3]{3,1,2,0:T(8,128)S(1)} %get-tuple-element.6, f32[24]{0:T(128)S(1)} %copy-done.35, ...), kind=kLoop, calls=%fused_computation.107 | loop fusion | flops 58475520 | bytes 19139072 | tf_op jit(solution)/shard_map/convert_element_type | solution.py:106
  (94 shorter events, 0.7 us)
Async XLA Ops:
  7.2 47.5 %copy-start = (bf16[24,24]{1,0:T(8,128)(2,1)S(1)}, bf16[24,24]{1,0:T(8,128)(2,1)}, u32[]{:S(2)}) copy-start(bf16[24,24]{1,0:T(8,128)(2,1)} %param.8) | copy-start | bytes 3460
  7.2 7.5 %copy-start.4 = (f32[24,7,7]{0,2,1:T(8,128)S(1)}, f32[24,7,7]{0,2,1:T(8,128)}, u32[]{:S(2)}) copy-start(f32[24,7,7]{0,2,1:T(8,128)} %param.7) | copy-start | bytes 14116
  7.2 8.7 %copy-start.37 = (s32[160]{0:T(256)S(1)}, s32[160]{0:T(256)}, u32[]{:S(2)}) copy-start(s32[160]{0:T(256)} %param.11) | copy-start | bytes 1924
  7.2 8.8 %copy-start.3 = (bf16[6,160,160]{2,1,0:T(8,128)(2,1)S(1)}, bf16[6,160,160]{2,1,0:T(8,128)(2,1)}, u32[]{:S(2)}) copy-start(bf16[6,160,160]{2,1,0:T(8,128)(2,1)} %param.9) | copy-start | bytes 921604
  7.2 300.2 %reduce-scatter.2.cloned.1.call-start = ((), (), s32[]{:S(2)}) async-start(), calls=%async_computation.3 | async-start | bytes 8110080 | tf_op jit(solution)/shard_map/reduce_scatter | solution.py:83
  8.5 16.3 %collective-permute-start = (bf16[2,24,3,1440]{3,1,2,0:T(8,128)(2,1)S(1)}, bf16[2,24,3,1440]{3,1,2,0:T(8,128)(2,1)}, u32[]{:S(2)}, u32[]{:S(2)}) collective-permute-start(bf16[2,24,3,1440]{3,1,2,0:T(8,128)(2,1)S(1)} %get-tuple-element.12), channel_id=1, source_target_pairs={{0,1},{1,2},{2,3},{3,4},{4,5},{5,6},{6,7},{7,8},{8,9},{9,10},{10,1... | collective-permute-start | bytes 1244168 | tf_op jit(solution)/shard_map/ppermute | solution.py:21
  13.4 12.7 %collective-permute-start.1 = (bf16[2,24,3,1440]{3,1,2,0:T(8,128)(2,1)S(1)}, bf16[2,24,3,1440]{3,1,2,0:T(8,128)(2,1)}, u32[]{:S(2)}, u32[]{:S(2)}) collective-permute-start(bf16[2,24,3,1440]{3,1,2,0:T(8,128)(2,1)S(1)} %get-tuple-element.13), channel_id=1, source_target_pairs={{1,0},{2,1},{3,2},{4,3},{5,4},{6,5},{7,6},{8,7},{9,8},{10,9},{11,1... | collective-permute-start | bytes 1244168 | tf_op jit(solution)/shard_map/ppermute | solution.py:24
  17.5 8.5 %copy-start.1 = (bf16[2,24,6,1440]{3,1,2,0:T(8,128)(2,1)S(1)}, bf16[2,24,6,1440]{3,1,2,0:T(8,128)(2,1)}, u32[]{:S(2)}) copy-start(bf16[2,24,6,1440]{3,1,2,0:T(8,128)(2,1)} %param.6) | copy-start | bytes 2488324
  24.8 2.9 copy-start.5
  24.8 2.9 copy-start.6
  24.8 2.9 copy-start.7
  24.8 2.9 copy-start.8
  24.8 2.9 copy-start.9
  24.8 2.9 copy-start.10
  24.8 2.9 copy-start.11
  24.8 2.9 copy-start.12
  24.8 2.9 copy-start.13
  24.8 2.9 copy-start.14
  24.8 2.9 copy-start.15
  24.9 2.9 copy-start.16
  24.9 2.9 copy-start.17
  24.9 2.9 copy-start.18
  24.9 2.9 copy-start.19
  24.9 2.9 copy-start.20
  24.9 2.9 copy-start.21
  24.9 2.9 copy-start.22
  24.9 2.9 copy-start.23
  24.9 2.9 copy-start.24
  24.9 2.9 copy-start.25
  25.0 2.9 copy-start.26
  25.0 2.9 copy-start.27
  54.6 3.3 copy-start.2
  78.7 7.1 %copy-start.38 = (s32[160]{0:T(256)S(1)}, s32[160]{0:T(256)}, u32[]{:S(2)}) copy-start(s32[160]{0:T(256)} %param.11) | copy-start | bytes 1924
  309.3 15.3 %all-to-all-start = ((bf16[2,24,2,160,5]{3,2,4,0,1:T(2,128)(2,1)}), bf16[2,24,2,160,5]{3,2,4,0,1:T(2,128)(2,1)S(1)}, u32[]{:S(2)}, u32[]{:S(2)}) async-start(bf16[2,24,2,160,5]{3,2,4,0,1:T(2,128)(2,1)} %copy.86), calls=%async_computation.1 | async-start | bytes 491520 | tf_op jit(solution)/shard_map/all_to_all | solution.py:88
  318.2 113.6 %all-gather.2.cloned.1.call-start = ((), (), s32[]{:S(2)}) async-start(), calls=%async_computation.4 | async-start | bytes 8110080 | tf_op jit(solution)/shard_map/all_gather | solution.py:97
  472.7 10.2 %collective-permute-start.2 = (bf16[2,24,3,1440]{3,1,2,0:T(8,128)(2,1)S(1)}, bf16[2,24,3,1440]{3,1,2,0:T(8,128)(2,1)S(1)}, u32[]{:S(2)}, u32[]{:S(2)}) collective-permute-start(bf16[2,24,3,1440]{3,1,2,0:T(8,128)(2,1)S(1)} %get-tuple-element.10), channel_id=1, source_target_pairs={{0,1},{1,2},{2,3},{3,4},{4,5},{5,6},{6,7},{7,8},{8,9},{9,10},{10,1... | collective-permute-start | bytes 1244168 | tf_op jit(solution)/shard_map/ppermute | solution.py:21
  474.6 12.2 %collective-permute-start.3 = (bf16[2,24,3,1440]{3,1,2,0:T(8,128)(2,1)S(1)}, bf16[2,24,3,1440]{3,1,2,0:T(8,128)(2,1)S(1)}, u32[]{:S(2)}, u32[]{:S(2)}) collective-permute-start(bf16[2,24,3,1440]{3,1,2,0:T(8,128)(2,1)S(1)} %get-tuple-element.11), channel_id=1, source_target_pairs={{1,0},{2,1},{3,2},{4,3},{5,4},{6,5},{7,6},{8,7},{9,8},{10,9},{11,1... | collective-permute-start | bytes 1244168 | tf_op jit(solution)/shard_map/ppermute | solution.py:24
  476.8 10.4 %copy-start.28 = (f32[24]{0:T(128)S(1)}, f32[24]{0:T(128)}, u32[]{:S(2)}) copy-start(f32[24]{0:T(128)} %get-tuple-element.54) | copy-start | bytes 292
  476.8 10.4 %copy-start.29 = (f32[24]{0:T(128)S(1)}, f32[24]{0:T(128)}, u32[]{:S(2)}) copy-start(f32[24]{0:T(128)} %get-tuple-element.55) | copy-start | bytes 292
  476.8 10.4 %copy-start.30 = (f32[24]{0:T(128)S(1)}, f32[24]{0:T(128)}, u32[]{:S(2)}) copy-start(f32[24]{0:T(128)} %get-tuple-element.56) | copy-start | bytes 292
  476.8 10.4 %copy-start.31 = (f32[24]{0:T(128)S(1)}, f32[24]{0:T(128)}, u32[]{:S(2)}) copy-start(f32[24]{0:T(128)} %get-tuple-element.57) | copy-start | bytes 292
  476.8 10.4 %copy-start.32 = (f32[24]{0:T(128)S(1)}, f32[24]{0:T(128)}, u32[]{:S(2)}) copy-start(f32[24]{0:T(128)} %get-tuple-element.58) | copy-start | bytes 292
  476.9 10.4 %copy-start.33 = (f32[24]{0:T(128)S(1)}, f32[24]{0:T(128)}, u32[]{:S(2)}) copy-start(f32[24]{0:T(128)} %get-tuple-element.59) | copy-start | bytes 292
  476.9 10.4 %copy-start.34 = (f32[24]{0:T(128)S(1)}, f32[24]{0:T(128)}, u32[]{:S(2)}) copy-start(f32[24]{0:T(128)} %get-tuple-element.60) | copy-start | bytes 292
  476.9 10.4 %copy-start.35 = (f32[24]{0:T(128)S(1)}, f32[24]{0:T(128)}, u32[]{:S(2)}) copy-start(f32[24]{0:T(128)} %get-tuple-element.61) | copy-start | bytes 292
  476.9 10.4 %copy-start.36 = (f32[24]{0:T(128)S(1)}, f32[24]{0:T(128)}, u32[]{:S(2)}) copy-start(f32[24]{0:T(128)} %get-tuple-element.62) | copy-start | bytes 292
Sparse Core Ops, SparseCore 0:
  78.9 228.5 reduce-scatter.1
  339.6 92.2 all-gather.1
where the time goes:
time: 525 us; the launch traced here: 521 us
  waiting for transfers between devices  329 us (63%)
  other arithmetic  65.7 us (13%)
  local copies, waits for them, and re-layouts  62.1 us (12%)
  matrix products  21.8 us (4%)
  starting transfers between devices  18.2 us (3%)
  between operations  14.8 us (3%)
  blocking collectives  9.77 us (2%)
    reduce_scatter x1, waiting for transfers between devices, local(): lax.psum_scatter(partial_sum.astype(jnp.bfloat16), 'lat', scatter_dimensi...  219 us
    all_gather x1, waiting for transfers between devices, local(): all_degrees = lax.all_gather(sent, 'lat', axis=4, tiled=True)  92.4 us
    convert_element_type x1, other arithmetic, local(): (hid_grad + depthwise(padded_grad, depth_kernel[:, ::-1, ::-1])).astype(j...  26.8 us
    add x1, other arithmetic, local(): hidden = padded[:, :, 3:-3] + depthwise(padded, depth_kernel)  26.7 us
    all_gather x1, local copies, waits for them, and re-layouts, local(): all_degrees = lax.all_gather(sent, 'lat', axis=4, tiled=True)  25.4 us
    convert_element_type x1, local copies, waits for them, and re-layouts, local(): partial_sum.astype(jnp.bfloat16)  15.1 us
  transfers between devices with their start and end apart: 7, of which 6 were waited for; matrix products, arithmetic and copies ran while one was open for 4% of the time, Pallas kernels for 0%

commit v1 on v0

v1 whole, which is shorter than its diff:
```python
import math

import jax
import jax.numpy as jnp
from jax import lax
from jax.sharding import PartitionSpec as P

NLON = 1440
M = 160
L = 160


smooth_width = 0.5


def padded_2(block, axis, dim, width):
    count = lax.axis_size(axis)
    forward = [(i, i + 1) for i in range(count - 1)]
    backward = [(target, source) for source, target in forward]
    low = lax.ppermute(
        lax.slice_in_dim(block, block.shape[dim] - width, None, axis=dim), axis, forward
    )
    high = lax.ppermute(lax.slice_in_dim(block, 0, width, axis=dim), axis, backward)
    return jnp.concatenate([low, block, high], axis=dim)


def wave_table():
    columns = jnp.arange(NLON, dtype=jnp.int32)
    orders = jnp.arange(M, dtype=jnp.int32)
    angles = (columns[:, None] * orders[None, :] % NLON).astype(jnp.float32) * (
        2.0 * math.pi / NLON
    )
    return (jnp.concatenate([jnp.cos(angles), -jnp.sin(angles)], axis=1) / math.sqrt(NLON)).astype(
        jnp.bfloat16
    )


def depthwise(padded, kernel):
    height = padded.shape[-2] - 6
    breadth = padded.shape[-1]
    widened = jnp.concatenate([padded[..., -3:], padded, padded[..., :3]], axis=-1)
    running = jnp.zeros(padded.shape[:-2] + (height, breadth), jnp.float32)
    for row_off in range(7):
        for col_off in range(7):
            running = (
                running
                + kernel[:, row_off, col_off][:, None, None]
                * widened[..., row_off : row_off + height, col_off : col_off + breadth]
            )
    return running


def soft_sign(gaps):
    return gaps / jnp.sqrt(gaps * gaps + smooth_width * smooth_width)


def local(fields, depth_kernel, mix_weight, legendre, truth, degree_order):
    table = wave_table()
    bands = lax.axis_size("lat")
    orders = M // bands
    mine = lax.all_to_all(legendre, "lat", split_axis=1, concat_axis=0, tiled=True)
    padded = padded_2(fields, "lat", 2, 3).astype(jnp.float32)
    hidden = padded[:, :, 3:-3] + depthwise(padded, depth_kernel)
    activation = jax.nn.gelu(hidden).astype(jnp.bfloat16)
    mixed_out = jnp.einsum(
        "oc,bcij->boij", mix_weight, activation, preferred_element_type=jnp.float32
    ).astype(jnp.bfloat16)
    spectral = jnp.dot(mixed_out, table, preferred_element_type=jnp.float32).astype(jnp.bfloat16)
    spectral = spectral.reshape(spectral.shape[:3] + (2, M))
    spectral = lax.all_to_all(spectral, "lat", split_axis=4, concat_axis=2, tiled=True)
    coeff = jnp.einsum("bcirm,iml->bcrml", spectral, mine, preferred_element_type=jnp.float32)
    share = coeff.shape[1] // lax.axis_size("ens")
    pooled = lax.all_to_all(
        coeff.astype(jnp.bfloat16), "ens", split_axis=1, concat_axis=0, tiled=True
    ).astype(jnp.float32)
    target = lax.dynamic_slice(
        truth,
        (lax.axis_index("ens") * share, 0, lax.axis_index("lat") * orders, 0),
        (share, 2, orders, L),
    ).astype(jnp.float32)
    count = pooled.shape[0]
    pair_sum = jnp.sum(soft_sign(pooled[:, None] - pooled[None]), axis=1)
    pooled_grad = soft_sign(pooled - target[None]) / count - pair_sum / (count * (count - 1))
    sent = lax.all_to_all(
        pooled_grad.astype(jnp.bfloat16), "ens", split_axis=0, concat_axis=1, tiled=True
    )
    spec_grad = jnp.einsum(
        "bcrml,iml->bcirm", sent, mine, preferred_element_type=jnp.float32
    ).astype(jnp.bfloat16)
    spec_grad = lax.all_to_all(spec_grad, "lat", split_axis=2, concat_axis=4, tiled=True)
    chosen = (jnp.arange(L, dtype=jnp.int32)[:, None] == degree_order[None, :]).astype(jnp.bfloat16)
    owned = jnp.einsum("bcrml,lj->bcrmj", sent, chosen, preferred_element_type=jnp.float32).astype(
        jnp.bfloat16
    )
    gradient = lax.all_to_all(owned, "lat", split_axis=4, concat_axis=3, tiled=True).astype(
        jnp.float32
    )
    spec_grad = spec_grad.reshape(spec_grad.shape[:3] + (2 * M,))
    mix_grad = jnp.dot(spec_grad, table.T, preferred_element_type=jnp.float32).astype(jnp.bfloat16)
    act_grad = jnp.einsum("oc,boij->bcij", mix_weight, mix_grad, preferred_element_type=jnp.float32)
    hid_grad = jax.vjp(jax.nn.gelu, hidden)[1](act_grad)[0]
    padded_grad = padded_2(hid_grad.astype(jnp.bfloat16), "lat", 2, 3).astype(hid_grad.dtype)
    grad_fields = (hid_grad + depthwise(padded_grad, depth_kernel[:, ::-1, ::-1])).astype(
        jnp.bfloat16
    )
    return (grad_fields, gradient)


def solution(mesh):
    placed = (P("ens", None, "lat", None), P(), P(), P("lat", None, None), P(), P())
    return jax.shard_map(
        local,
        mesh=mesh,
        in_specs=placed,
        out_specs=(P("ens", None, "lat", None), P("ens", None, None, None, "lat")),
        check_vma=False,
    )
```

time: 525 us -> 206 us (0.39)
  waiting for transfers between devices: 329 us -> 13.2 us
  local copies, waits for them, and re-layouts: 62.1 us -> 29.9 us
  blocking collectives: 9.77 us -> 37.9 us
  starting transfers between devices: 18.2 us -> 42.4 us
  matrix products: 21.8 us -> 9.07 us
  between operations: 14.8 us -> 2.17 us
    reduce_scatter x1 -> x0, waiting for transfers between devices: 219 us -> none  [local(): lax.psum_scatter(partial_sum.astype(jnp.bfloat16), 'lat', scatter_dimensi...]
    all_gather x1 -> x0, waiting for transfers between devices: 92.4 us -> none  [local(): all_degrees = lax.all_gather(sent, 'lat', axis=4, tiled=True)]
    all_to_all x0 -> x2, blocking collectives: none -> 28.1 us  [the longest x1 15.1 us: local(): lax.all_to_all(owned, 'lat', split_axis=4, concat_axis=3, tiled=True)]
    all_gather x1 -> x0, local copies, waits for them, and re-layouts: 25.4 us -> none  [local(): all_degrees = lax.all_gather(sent, 'lat', axis=4, tiled=True)]
    all_to_all x0 -> x2, starting transfers between devices: none -> 22 us  [the longest x1 12.7 us: local(): lax.all_to_all(legendre, 'lat', split_axis=1, concat_axis=0, tiled=True)]
    dot_general x2 -> x3, matrix products: 14.6 us -> 0.93 us  [the longest x1 0.41 us: local(): jnp.einsum('bcirm,iml->bcrml', spectral, mine, preferred_element_type=jnp...]
    convert_element_type x2 -> x5, local copies, waits for them, and re-layouts: 16.1 us -> 5.75 us  [the longest x2 1.93 us: local(): lax.all_to_all(owned, 'lat', split_axis=4, concat_axis=3, tiled=True)]
    all_to_all x0 -> x2, waiting for transfers between devices: none -> 7.63 us  [the longest x1 7.63 us: local(): lax.all_to_all(spectral, 'lat', split_axis=4, concat_axis=2, tiled=True)]
  transfers between devices with their start and end apart: 7 -> 7, of which waited for: 6 -> 2; matrix products, arithmetic and copies ran while one was open for 4% -> 27% of each run, Pallas kernels for 0% -> 0%
where the time goes in v1:
time: 206 us; the launch traced here: 203 us
  other arithmetic  67.9 us (33%)
  starting transfers between devices  42.4 us (21%)
  blocking collectives  37.9 us (18%)
  local copies, waits for them, and re-layouts  29.9 us (15%)
  waiting for transfers between devices  13.2 us (6%)
  matrix products  9.07 us (4%)
  between operations  2.17 us (1%)
    add x1, other arithmetic, local(): hidden = padded[:, :, 3:-3] + depthwise(padded, depth_kernel)  27.5 us
    convert_element_type x1, other arithmetic, local(): (hid_grad + depthwise(padded_grad, depth_kernel[:, ::-1, ::-1])).astype(j...  27.5 us
    all_to_all x1, blocking collectives, local(): lax.all_to_all(owned, 'lat', split_axis=4, concat_axis=3, tiled=True)  15.1 us
    unnamed x178, local copies, waits for them, and re-layouts  14.8 us
    all_to_all x1, blocking collectives, local(): lax.all_to_all(spec_grad, 'lat', split_axis=2, concat_axis=4, tiled=True)  13 us
    all_to_all x1, starting transfers between devices, local(): lax.all_to_all(legendre, 'lat', split_axis=1, concat_axis=0, tiled=True)  12.7 us
    ppermute x2, starting transfers between devices, padded_2(): lax.ppermute(lax.slice_in_dim(block, block.shape[dim] - width, None, axis...  10.2 us
    all_to_all x1, blocking collectives, local(): lax.all_to_all(pooled_grad.astype(jnp.bfloat16), 'ens', split_axis=0, con...  9.77 us
  transfers between devices with their start and end apart: 7, of which 2 were waited for; matrix products, arithmetic and copies ran while one was open for 27% of the time, Pallas kernels for 0%

profile of v1, /device:TPU:1, one launch (start us, length us, event | category | flops | bytes accessed | tf_op | source)
XLA Modules:
  0.0 202.6 jit_solution(17925919961467768960)
XLA Ops:
  0.7 1.3 fusion.328
  1.9 1.3 collective-permute-start.1
  3.2 5.4 %collective-permute-start = (bf16[2,24,3,1440]{3,1,2,0:T(8,128)(2,1)S(1)}, bf16[2,24,3,1440]{3,1,2,0:T(8,128)(2,1)}, u32[]{:S(2)}, u32[]{:S(2)}) collective-permute-start(bf16[2,24,3,1440]{3,1,2,0:T(8,128)(2,1)S(1)} %get-tuple-element.20), channel_id=1, source_target_pairs={{0,1},{1,2},{2,3},{3,4},{4,5},{5,6},{6,7},{7,8},{8,9},{9,10},{10,1... | collective-permute-start | bytes 1244168 | tf_op jit(solution)/shard_map/ppermute | solution.py:20
  8.7 0.3 copy.202
  9.0 1.4 reshape.143
  10.4 12.7 %all-to-all-start.1 = ((bf16[32,2,2400]{2,1,0:T(2,128)(2,1)}), bf16[32,2,2400]{2,1,0:T(2,128)(2,1)}, u32[]{:S(2)}, u32[]{:S(2)}) async-start(bf16[32,2,2400]{2,1,0:T(2,128)(2,1)} %reshape.143), calls=%async_computation.1 | async-start | bytes 622592 | tf_op jit(solution)/shard_map/all_to_all | solution.py:61
  23.5 0.6 slice_bitcast_fusion.46
  24.1 5.6 %sine_negate_fusion = (f32[1440,160]{0,1:T(8,128)}, f32[1440,160]{0,1:T(8,128)}) fusion(), kind=kLoop, calls=%fused_computation.465 | loop fusion | flops 2304000 | bytes 1843200 | tf_op jit(solution)/shard_map/neg | solution.py:33
  29.7 0.8 copy-done.5
  30.4 1.7 maximum_convert_fusion
  32.7 27.5 %fusion.145 = f32[2,24,6,1440]{3,1,2,0:T(8,128)} fusion(f32[2,24,12,3]{3,1,2,0:T(8,128)S(1)} %get-tuple-element.17, f32[2,24,12,1440]{3,1,2,0:T(8,128)S(1)} %maximum_convert_fusion, f32[2,24,12,3]{3,1,2,0:T(8,128)S(1)} %get-tuple-element.16, f32[24]{0:T(128)} %get-tuple-element.69, f32[24]{0:T(128)} %get-tuple-element.70, f32[24]{0:T(128)S(1)} %get-tuple-element.23, ...), kind=kLoop, calls=%fused_computation.233 | loop fusion | flops 58060800 | bytes 18195296 | tf_op jit(solution)/shard_map/add | solution.py:63
  60.1 3.2 %fusion.275 = bf16[2,24,6,320]{3,1,2,0:T(8,128)(2,1)S(1)} fusion(f32[2,24,6,1440]{3,1,2,0:T(8,128)} %fusion.145, f32[1440,160]{0,1:T(8,128)} %get-tuple-element.73, f32[1440,160]{0,1:T(8,128)} %get-tuple-element.74, bf16[24,24]{1,0:T(8,128)(2,1)S(1)} %copy-done), kind=kOutput, calls=%fused_computation.457 | convolution fusion | flops 290949120 | bytes 3687552 | tf_op jit(solution)/shard_map/dot_general | solution.py:68
  63.5 0.9 copy.140
  64.4 2.0 %reshape.141 = bf16[32,2,1440]{2,1,0:T(2,128)(2,1)} reshape(bf16[160,2,6,2,24]{4,3,2,1,0:T(2,128)(2,1)S(1)} %bitcast.189) | data formatting | bytes 368640
  66.5 9.3 %all-to-all-start = ((bf16[32,2,1440]{2,1,0:T(2,128)(2,1)}), bf16[32,2,1440]{2,1,0:T(2,128)(2,1)S(1)}, u32[]{:S(2)}, u32[]{:S(2)}) async-start(bf16[32,2,1440]{2,1,0:T(2,128)(2,1)} %reshape.141), calls=%async_computation | async-start | bytes 393216 | tf_op jit(solution)/shard_map/all_to_all | solution.py:70
  75.8 1.7 reshape.144
  77.6 0.3 all_to_all.71
  77.9 7.6 %all-to-all-done = bf16[32,2,1440]{2,1,0:T(2,128)(2,1)S(1)} async-done(((bf16[32,2,1440]{2,1,0:T(2,128)(2,1)}), bf16[32,2,1440]{2,1,0:T(2,128)(2,1)S(1)}, u32[]{:S(2)}, u32[]{:S(2)}) %all-to-all-start) | async-done | bytes 184352 | tf_op jit(solution)/shard_map/all_to_all | solution.py:70
  85.5 1.1 reshape.142
  86.6 0.7 copy.142
  87.3 0.4 fusion.277
  87.7 0.9 copy.147
  88.6 7.7 %all-to-all-start.2 = ((bf16[2,24,2,5,160]{4,2,0,3,1:T(2,128)(2,1)}), bf16[2,24,2,5,160]{4,2,0,3,1:T(2,128)(2,1)S(1)}, u32[]{:S(2)}, u32[]{:S(2)}) async-start(bf16[2,24,2,5,160]{4,2,0,3,1:T(2,128)(2,1)} %copy.147), calls=%async_computation.2 | async-start | bytes 491520 | tf_op jit(solution)/shard_map/all_to_all | solution.py:73
  96.3 0.8 dynamic-slice_convert_fusion
  97.1 5.5 %all-to-all-done.2 = bf16[2,24,2,5,160]{4,2,0,3,1:T(2,128)(2,1)S(1)} async-done(((bf16[2,24,2,5,160]{4,2,0,3,1:T(2,128)(2,1)}), bf16[2,24,2,5,160]{4,2,0,3,1:T(2,128)(2,1)S(1)}, u32[]{:S(2)}, u32[]{:S(2)}) %all-to-all-start.2) | async-done | bytes 153632 | tf_op jit(solution)/shard_map/all_to_all | solution.py:73
  103.3 2.7 %fusion.2 = f32[16,3,2,5,160]{4,3,2,1,0:T(8,128)S(1)} fusion(f32[16,3,2,5,160]{4,0,3,2,1:T(8,128)S(1)} %copy.151, f32[16,3,2,5,160]{4,3,2,1,0:T(8,128)S(1)} %copy.152), kind=kLoop, calls=%fused_computation.84 | loop fusion | flops 6067200 | bytes 921600 | tf_op jit(solution)/shard_map/reduce_sum | solution.py:82
  106.0 0.4 fusion.299
  106.6 9.8 %all_to_all.87 = bf16[16,3,2,5,160]{4,2,3,1,0:T(2,128)(2,1)S(1)} all-to-all(bf16[16,3,2,5,160]{4,2,3,1,0:T(2,128)(2,1)S(1)} %copy.155), channel_id=1, replica_groups=mesh['ens'=8,'lat'=32] {'ens'}, dimensions={0} | all-to-all | bytes 307200 | tf_op jit(solution)/shard_map/all_to_all | solution.py:84
  116.5 0.3 fusion.276
  116.8 1.6 copy.159
  118.5 1.4 reshape.147
  119.8 13.0 %all_to_all.88 = bf16[32,2,1440]{2,1,0:T(2,128)(2,1)S(1)} all-to-all(bf16[32,2,1440]{2,1,0:T(2,128)(2,1)S(1)} %reshape.147), channel_id=1, replica_groups=mesh['ens'=8,'lat'=32] {'lat'}, dimensions={0} | all-to-all | bytes 368640 | tf_op jit(solution)/shard_map/all_to_all | solution.py:90
  132.8 1.1 reshape.148
  133.9 1.6 copy.161
  135.5 5.0 %fusion.329 = (bf16[2,24,6,1440]{3,1,2,0:T(8,128)(2,1)S(1)}, f32[2,24,6,1440]{3,1,2,0:T(8,128)}) fusion(f32[2,24,6,1440]{3,1,2,0:T(8,128)S(1)} %copy-done.2, bf16[24,24]{1,0:T(8,128)(2,1)S(1)} %copy-done, bf16[2,24,6,320]{1,0,3,2:T(2,128)(2,1)} %bitcast.199, f32[1440,160]{0,1:T(8,128)} %get-tuple-element.73, f32[1440,160]{0,1:T(8,128)} %get-tuple-element.74), kind=kOutput, calls=%fused_computation.550 | convolution fusion | flops 295418880 | bytes 6175872 | tf_op jit(solution)/shard_map/oc,boij->bcij/dot_general | solution.py:100
  140.5 1.1 fusion.327
  141.6 1.3 collective-permute-start.3
  142.9 4.8 %collective-permute-start.2 = (bf16[2,24,3,1440]{3,1,2,0:T(8,128)(2,1)}, bf16[2,24,3,1440]{3,1,2,0:T(8,128)(2,1)}, u32[]{:S(2)}, u32[]{:S(2)}) collective-permute-start(bf16[2,24,3,1440]{3,1,2,0:T(8,128)(2,1)} %get-tuple-element.18), channel_id=1, source_target_pairs={{0,1},{1,2},{2,3},{3,4},{4,5},{5,6},{6,7},{7,8},{8,9},{9,10},{10,1... | collective-permute-start | bytes 1244168 | tf_op jit(solution)/shard_map/ppermute | solution.py:20
  147.9 1.3 copy.165
  149.2 0.9 reshape.145
  150.2 15.1 %all_to_all.89 = bf16[32,2,1200]{2,1,0:T(2,128)(2,1)S(1)} all-to-all(bf16[32,2,1200]{2,1,0:T(2,128)(2,1)S(1)} %reshape.145), channel_id=1, replica_groups=mesh['ens'=8,'lat'=32] {'lat'}, dimensions={0} | all-to-all | bytes 307200 | tf_op jit(solution)/shard_map/all_to_all | solution.py:95
  165.3 1.1 reshape.146
  166.4 1.3 copy.166
  167.7 1.4 copy.167
  169.0 0.6 copy.168
  169.6 2.7 %copy.169 = f32[2,24,2,160,5]{3,2,4,1,0:T(2,128)} copy(f32[2,24,2,160,5]{1,2,4,3,0:T(2,128)S(1)} %bitcast.188) | data formatting | bytes 614400
  172.7 1.8 maximum_convert_fusion.1
  175.1 27.5 %fusion.16 = bf16[2,24,6,1440]{3,1,2,0:T(8,128)(2,1)} fusion(f32[2,24,6,1440]{3,1,2,0:T(8,128)S(1)} %copy-done.3, f32[2,24,12,3]{3,1,2,0:T(8,128)S(1)} %get-tuple-element.15, f32[2,24,12,1440]{3,1,2,0:T(8,128)S(1)} %maximum_convert_fusion.1, f32[2,24,12,3]{3,1,2,0:T(8,128)S(1)} %get-tuple-element.14, f32[24]{0:T(128)} %get-tuple-element.69, ...), kind=kLoop, calls=%fused_computation.104 | loop fusion | flops 58475520 | bytes 19135328 | tf_op jit(solution)/shard_map/convert_element_type | solution.py:103
  (186 shorter events, 2.1 us)
Async XLA Ops:
  0.6 59.5 %copy-start = (bf16[24,24]{1,0:T(8,128)(2,1)S(1)}, bf16[24,24]{1,0:T(8,128)(2,1)}, u32[]{:S(2)}) copy-start(bf16[24,24]{1,0:T(8,128)(2,1)} %param.8) | copy-start | bytes 3460
  1.9 21.1 %copy-start.6 = (f32[24,7,7]{0,2,1:T(8,128)S(1)}, f32[24,7,7]{0,2,1:T(8,128)}, u32[]{:S(2)}) copy-start(f32[24,7,7]{0,2,1:T(8,128)} %param.7) | copy-start | bytes 14116
  1.9 27.7 %collective-permute-start.1 = (bf16[2,24,3,1440]{3,1,2,0:T(8,128)(2,1)S(1)}, bf16[2,24,3,1440]{3,1,2,0:T(8,128)(2,1)S(1)}, u32[]{:S(2)}, u32[]{:S(2)}) collective-permute-start(bf16[2,24,3,1440]{3,1,2,0:T(8,128)(2,1)S(1)} %get-tuple-element.21), channel_id=1, source_target_pairs={{1,0},{2,1},{3,2},{4,3},{5,4},{6,5},{7,6},{8,7},{9,8},{10,9},{11,1... | collective-permute-start | bytes 1244168 | tf_op jit(solution)/shard_map/ppermute | solution.py:23
  3.2 27.2 %collective-permute-start = (bf16[2,24,3,1440]{3,1,2,0:T(8,128)(2,1)S(1)}, bf16[2,24,3,1440]{3,1,2,0:T(8,128)(2,1)}, u32[]{:S(2)}, u32[]{:S(2)}) collective-permute-start(bf16[2,24,3,1440]{3,1,2,0:T(8,128)(2,1)S(1)} %get-tuple-element.20), channel_id=1, source_target_pairs={{0,1},{1,2},{2,3},{3,4},{4,5},{5,6},{6,7},{7,8},{8,9},{9,10},{10,1... | collective-permute-start | bytes 1244168 | tf_op jit(solution)/shard_map/ppermute | solution.py:20
  10.4 56.1 %all-to-all-start.1 = ((bf16[32,2,2400]{2,1,0:T(2,128)(2,1)}), bf16[32,2,2400]{2,1,0:T(2,128)(2,1)}, u32[]{:S(2)}, u32[]{:S(2)}) async-start(bf16[32,2,2400]{2,1,0:T(2,128)(2,1)} %reshape.143), calls=%async_computation.1 | async-start | bytes 622592 | tf_op jit(solution)/shard_map/all_to_all | solution.py:61
  23.1 9.2 %copy-start.7 = (f32[24]{0:T(128)}, f32[24]{0:T(128)S(1)}, u32[]{:S(2)}) copy-start(f32[24]{0:T(128)S(1)} %get-tuple-element.24) | copy-start | bytes 292
  23.1 9.2 %copy-start.9 = (f32[24]{0:T(128)}, f32[24]{0:T(128)S(1)}, u32[]{:S(2)}) copy-start(f32[24]{0:T(128)S(1)} %get-tuple-element.25) | copy-start | bytes 292
  23.1 9.2 %copy-start.11 = (f32[24]{0:T(128)}, f32[24]{0:T(128)S(1)}, u32[]{:S(2)}) copy-start(f32[24]{0:T(128)S(1)} %get-tuple-element.26) | copy-start | bytes 292
  23.1 9.2 %copy-start.13 = (f32[24]{0:T(128)}, f32[24]{0:T(128)S(1)}, u32[]{:S(2)}) copy-start(f32[24]{0:T(128)S(1)} %get-tuple-element.27) | copy-start | bytes 292
  23.1 9.2 %copy-start.15 = (f32[24]{0:T(128)}, f32[24]{0:T(128)S(1)}, u32[]{:S(2)}) copy-start(f32[24]{0:T(128)S(1)} %get-tuple-element.28) | copy-start | bytes 292
  23.1 9.2 %copy-start.17 = (f32[24]{0:T(128)}, f32[24]{0:T(128)S(1)}, u32[]{:S(2)}) copy-start(f32[24]{0:T(128)S(1)} %get-tuple-element.29) | copy-start | bytes 292
  23.1 9.2 %copy-start.19 = (f32[24]{0:T(128)}, f32[24]{0:T(128)S(1)}, u32[]{:S(2)}) copy-start(f32[24]{0:T(128)S(1)} %get-tuple-element.30) | copy-start | bytes 292
  23.1 9.2 %copy-start.21 = (f32[24]{0:T(128)}, f32[24]{0:T(128)S(1)}, u32[]{:S(2)}) copy-start(f32[24]{0:T(128)S(1)} %get-tuple-element.31) | copy-start | bytes 292
  23.2 9.2 %copy-start.23 = (f32[24]{0:T(128)}, f32[24]{0:T(128)S(1)}, u32[]{:S(2)}) copy-start(f32[24]{0:T(128)S(1)} %get-tuple-element.32) | copy-start | bytes 292
  23.2 9.2 %copy-start.25 = (f32[24]{0:T(128)}, f32[24]{0:T(128)S(1)}, u32[]{:S(2)}) copy-start(f32[24]{0:T(128)S(1)} %get-tuple-element.33) | copy-start | bytes 292
  23.2 9.2 %copy-start.27 = (f32[24]{0:T(128)}, f32[24]{0:T(128)S(1)}, u32[]{:S(2)}) copy-start(f32[24]{0:T(128)S(1)} %get-tuple-element.34) | copy-start | bytes 292
  23.2 9.2 %copy-start.29 = (f32[24]{0:T(128)}, f32[24]{0:T(128)S(1)}, u32[]{:S(2)}) copy-start(f32[24]{0:T(128)S(1)} %get-tuple-element.35) | copy-start | bytes 292
  23.2 9.2 %copy-start.31 = (f32[24]{0:T(128)}, f32[24]{0:T(128)S(1)}, u32[]{:S(2)}) copy-start(f32[24]{0:T(128)S(1)} %get-tuple-element.36) | copy-start | bytes 292
  23.2 9.2 %copy-start.33 = (f32[24]{0:T(128)}, f32[24]{0:T(128)S(1)}, u32[]{:S(2)}) copy-start(f32[24]{0:T(128)S(1)} %get-tuple-element.37) | copy-start | bytes 292
  23.2 9.2 %copy-start.35 = (f32[24]{0:T(128)}, f32[24]{0:T(128)S(1)}, u32[]{:S(2)}) copy-start(f32[24]{0:T(128)S(1)} %get-tuple-element.38) | copy-start | bytes 292
  23.2 9.2 %copy-start.37 = (f32[24]{0:T(128)}, f32[24]{0:T(128)S(1)}, u32[]{:S(2)}) copy-start(f32[24]{0:T(128)S(1)} %get-tuple-element.39) | copy-start | bytes 292
  23.2 9.2 %copy-start.39 = (f32[24]{0:T(128)}, f32[24]{0:T(128)S(1)}, u32[]{:S(2)}) copy-start(f32[24]{0:T(128)S(1)} %get-tuple-element.40) | copy-start | bytes 292
  23.3 9.2 %copy-start.41 = (f32[24]{0:T(128)}, f32[24]{0:T(128)S(1)}, u32[]{:S(2)}) copy-start(f32[24]{0:T(128)S(1)} %get-tuple-element.41) | copy-start | bytes 292
  23.3 9.2 %copy-start.43 = (f32[24]{0:T(128)}, f32[24]{0:T(128)S(1)}, u32[]{:S(2)}) copy-start(f32[24]{0:T(128)S(1)} %get-tuple-element.42) | copy-start | bytes 292
  23.3 9.2 %copy-start.45 = (f32[24]{0:T(128)}, f32[24]{0:T(128)S(1)}, u32[]{:S(2)}) copy-start(f32[24]{0:T(128)S(1)} %get-tuple-element.43) | copy-start | bytes 292
  23.3 9.2 %copy-start.47 = (f32[24]{0:T(128)}, f32[24]{0:T(128)S(1)}, u32[]{:S(2)}) copy-start(f32[24]{0:T(128)S(1)} %get-tuple-element.44) | copy-start | bytes 292
  23.3 9.2 %copy-start.49 = (f32[24]{0:T(128)}, f32[24]{0:T(128)S(1)}, u32[]{:S(2)}) copy-start(f32[24]{0:T(128)S(1)} %get-tuple-element.45) | copy-start | bytes 292
  23.3 9.2 %copy-start.51 = (f32[24]{0:T(128)}, f32[24]{0:T(128)S(1)}, u32[]{:S(2)}) copy-start(f32[24]{0:T(128)S(1)} %get-tuple-element.46) | copy-start | bytes 292
  23.3 9.2 %copy-start.53 = (f32[24]{0:T(128)}, f32[24]{0:T(128)S(1)}, u32[]{:S(2)}) copy-start(f32[24]{0:T(128)S(1)} %get-tuple-element.47) | copy-start | bytes 292
  23.3 9.2 %copy-start.55 = (f32[24]{0:T(128)}, f32[24]{0:T(128)S(1)}, u32[]{:S(2)}) copy-start(f32[24]{0:T(128)S(1)} %get-tuple-element.48) | copy-start | bytes 292
  23.3 9.2 %copy-start.57 = (f32[24]{0:T(128)}, f32[24]{0:T(128)S(1)}, u32[]{:S(2)}) copy-start(f32[24]{0:T(128)S(1)} %get-tuple-element.49) | copy-start | bytes 292
  23.4 9.2 %copy-start.59 = (f32[24]{0:T(128)}, f32[24]{0:T(128)S(1)}, u32[]{:S(2)}) copy-start(f32[24]{0:T(128)S(1)} %get-tuple-element.50) | copy-start | bytes 292
  23.4 9.2 %copy-start.61 = (f32[24]{0:T(128)}, f32[24]{0:T(128)S(1)}, u32[]{:S(2)}) copy-start(f32[24]{0:T(128)S(1)} %get-tuple-element.51) | copy-start | bytes 292
  23.4 9.2 %copy-start.63 = (f32[24]{0:T(128)}, f32[24]{0:T(128)S(1)}, u32[]{:S(2)}) copy-start(f32[24]{0:T(128)S(1)} %get-tuple-element.52) | copy-start | bytes 292
  23.4 9.2 %copy-start.65 = (f32[24]{0:T(128)}, f32[24]{0:T(128)S(1)}, u32[]{:S(2)}) copy-start(f32[24]{0:T(128)S(1)} %get-tuple-element.53) | copy-start | bytes 292
  23.4 9.2 %copy-start.67 = (f32[24]{0:T(128)}, f32[24]{0:T(128)S(1)}, u32[]{:S(2)}) copy-start(f32[24]{0:T(128)S(1)} %get-tuple-element.54) | copy-start | bytes 292
  23.4 9.2 %copy-start.69 = (f32[24]{0:T(128)}, f32[24]{0:T(128)S(1)}, u32[]{:S(2)}) copy-start(f32[24]{0:T(128)S(1)} %get-tuple-element.55) | copy-start | bytes 292
  23.4 9.2 %copy-start.71 = (f32[24]{0:T(128)}, f32[24]{0:T(128)S(1)}, u32[]{:S(2)}) copy-start(f32[24]{0:T(128)S(1)} %get-tuple-element.56) | copy-start | bytes 292
  23.4 9.2 %copy-start.73 = (f32[24]{0:T(128)}, f32[24]{0:T(128)S(1)}, u32[]{:S(2)}) copy-start(f32[24]{0:T(128)S(1)} %get-tuple-element.57) | copy-start | bytes 292
  23.4 9.2 %copy-start.75 = (f32[24]{0:T(128)}, f32[24]{0:T(128)S(1)}, u32[]{:S(2)}) copy-start(f32[24]{0:T(128)S(1)} %get-tuple-element.58) | copy-start | bytes 292
  23.4 9.2 %copy-start.77 = (f32[24]{0:T(128)}, f32[24]{0:T(128)S(1)}, u32[]{:S(2)}) copy-start(f32[24]{0:T(128)S(1)} %get-tuple-element.59) | copy-start | bytes 292
  24.1 8.6 %copy-start.81 = (f32[24]{0:T(128)}, f32[24]{0:T(128)S(1)}, u32[]{:S(2)}) copy-start(f32[24]{0:T(128)S(1)} %get-tuple-element.61) | copy-start | bytes 292
  66.5 19.0 %all-to-all-start = ((bf16[32,2,1440]{2,1,0:T(2,128)(2,1)}), bf16[32,2,1440]{2,1,0:T(2,128)(2,1)S(1)}, u32[]{:S(2)}, u32[]{:S(2)}) async-start(bf16[32,2,1440]{2,1,0:T(2,128)(2,1)} %reshape.141), calls=%async_computation | async-start | bytes 393216 | tf_op jit(solution)/shard_map/all_to_all | solution.py:70
  88.6 14.0 %all-to-all-start.2 = ((bf16[2,24,2,5,160]{4,2,0,3,1:T(2,128)(2,1)}), bf16[2,24,2,5,160]{4,2,0,3,1:T(2,128)(2,1)S(1)}, u32[]{:S(2)}, u32[]{:S(2)}) async-start(bf16[2,24,2,5,160]{4,2,0,3,1:T(2,128)(2,1)} %copy.147), calls=%async_computation.2 | async-start | bytes 491520 | tf_op jit(solution)/shard_map/all_to_all | solution.py:73
  119.8 15.7 %copy-start.2 = (f32[2,24,6,1440]{3,1,2,0:T(8,128)S(1)}, f32[2,24,6,1440]{3,1,2,0:T(8,128)}, u32[]{:S(2)}) copy-start(f32[2,24,6,1440]{3,1,2,0:T(8,128)} %fusion.145) | copy-start | bytes 4976644
  140.5 9.7 %copy-start.1 = (bf16[2,24,6,1440]{3,1,2,0:T(8,128)(2,1)}, bf16[2,24,6,1440]{3,1,2,0:T(8,128)(2,1)S(1)}, u32[]{:S(2)}) copy-start(bf16[2,24,6,1440]{3,1,2,0:T(8,128)(2,1)S(1)} %get-tuple-element.71) | copy-start | bytes 2488324
  141.6 31.1 %collective-permute-start.3 = (bf16[2,24,3,1440]{3,1,2,0:T(8,128)(2,1)}, bf16[2,24,3,1440]{3,1,2,0:T(8,128)(2,1)}, u32[]{:S(2)}, u32[]{:S(2)}) collective-permute-start(bf16[2,24,3,1440]{3,1,2,0:T(8,128)(2,1)} %get-tuple-element.19), channel_id=1, source_target_pairs={{1,0},{2,1},{3,2},{4,3},{5,4},{6,5},{7,6},{8,7},{9,8},{10,9},{11,1... | collective-permute-start | bytes 1244168 | tf_op jit(solution)/shard_map/ppermute | solution.py:23
  142.9 29.8 %collective-permute-start.2 = (bf16[2,24,3,1440]{3,1,2,0:T(8,128)(2,1)}, bf16[2,24,3,1440]{3,1,2,0:T(8,128)(2,1)}, u32[]{:S(2)}, u32[]{:S(2)}) collective-permute-start(bf16[2,24,3,1440]{3,1,2,0:T(8,128)(2,1)} %get-tuple-element.18), channel_id=1, source_target_pairs={{0,1},{1,2},{2,3},{3,4},{4,5},{5,6},{6,7},{7,8},{8,9},{9,10},{10,1... | collective-permute-start | bytes 1244168 | tf_op jit(solution)/shard_map/ppermute | solution.py:20
  (43 other events, 118.0 us)

commit v2 on v1

v2 whole, which is shorter than its diff:
```python
import math

import jax
import jax.numpy as jnp
import ml_dtypes
import numpy as np
from jax import lax
from jax.experimental import pallas as pl
from jax.experimental.pallas import tpu as pltpu
from jax.sharding import PartitionSpec as P

C = 24
NLON = 1440
M = 160
L = 160
BANDS = 32
ROWS = 6
ORDERS = M // BANDS
ENS = 8
PART = 112
BF = jnp.bfloat16
F32 = jnp.float32


def wave_table():
    m = (np.arange(BANDS)[None, :] * ORDERS + np.arange(ORDERS)[:, None]).reshape(-1)
    angles = (m[:, None] * np.arange(NLON)[None, :] % NLON) * (2.0 * math.pi / NLON)
    both = np.concatenate([np.cos(angles), -np.sin(angles)], axis=0) / math.sqrt(NLON)
    return both.astype(np.float32).astype(ml_dtypes.bfloat16)


def banded(kernel):
    cols = jnp.broadcast_to(
        jnp.transpose(kernel, (2, 0, 1))[:, None], (7, 3, C, 7)
    ).reshape(504, 7).astype(BF)
    out_row = lax.broadcasted_iota(jnp.int32, (504, 216), 0)
    in_row = lax.broadcasted_iota(jnp.int32, (504, 216), 1)
    same = (out_row % C) == (in_row % C)
    gap = in_row // C - (out_row // C) % 3
    total = jnp.zeros((504, 216), BF)
    for p in range(7):
        total = jnp.where(same & (gap == p), cols[:, p : p + 1], total)
    return total


def wrapped(x):
    return jnp.concatenate([x[:, NLON - 3 :], x, x[:, :93]], axis=1)


def conv_half(low, own, high, weights, ext, prod, k, h):
    if h == 0:
        ext[0:72, :] = wrapped(low[k])
        ext[72:216, :] = wrapped(own[k])
    else:
        ext[0:144, :] = wrapped(own[k])
        ext[144:216, :] = wrapped(high[k])
    prod[...] = jnp.dot(weights[...], ext[...], preferred_element_type=F32)
    total = prod[0:72, 0:NLON]
    for q in range(1, 7):
        total = total + prod[q * 72 : (q + 1) * 72, q : q + NLON]
    return total


def forward_kernel(low, own, high, weights, table, placing, slope, send, ext, prod, act, rows):
    c0 = math.sqrt(2.0 / math.pi)
    for k in range(2):
        for h in range(2):
            part = slice(h * 72, (h + 1) * 72)
            x = own[k, part, :].astype(F32) + conv_half(low, own, high, weights, ext, prod, k, h)
            sq = x * x
            t = jnp.tanh(c0 * x * (1.0 + 0.044715 * sq))
            half = 0.5 * (1.0 + t)
            act[k, part, :] = (x * half).astype(BF)
            slope[k, part, :] = (
                half + 0.5 * x * (1.0 - t * t) * (c0 * (1.0 + 0.134145 * sq))
            ).astype(BF)
    spec = jnp.zeros((2 * M, 384), F32)
    for k in range(2):
        waves = lax.dot_general(
            table[...], act[k], (((1,), (1,)), ((), ())), preferred_element_type=F32
        ).astype(BF)
        spec = spec + jnp.dot(waves, placing[k], preferred_element_type=F32)
    rows[:, 30:32, :] = jnp.zeros((BANDS, 2, 128), F32)
    for a in range(10):
        for t in range(3):
            rows[:, t * 10 + a, :] = spec[a * 32 : (a + 1) * 32, t * 128 : (t + 1) * 128]
    send[...] = rows[...].astype(BF)


def legendre_kernel(recv, leg, coeff, rows):
    rows[...] = recv[...].astype(F32)
    lane = lax.broadcasted_iota(jnp.int32, (L, 128), 1)
    for ml in range(ORDERS):
        acc = []
        for r in range(2):
            a = jnp.concatenate(
                [rows[:, t * 10 + r * 5 + ml, :] for t in range(3)], axis=0
            ).astype(BF)
            for par in range(2):
                acc.append(
                    lax.dot_general(
                        leg[ml, par * 96 : (par + 1) * 96, :],
                        a,
                        (((0,), (0,)), ((), ())),
                        preferred_element_type=F32,
                    )
                )
        first = acc[0] + pltpu.roll(acc[1], 64, 1)
        second = pltpu.roll(acc[2], 64, 1) + acc[3]
        coeff[ml * L : (ml + 1) * L, :] = jnp.where(lane < 64, first, second).astype(BF)
    coeff[800:896, :] = jnp.zeros((96, 128), BF)


def soft_sign(gaps):
    return gaps * lax.rsqrt(gaps * gaps + 0.25)


def score_kernel(pooled, target, grad):
    lane = lax.broadcasted_iota(jnp.int32, (16, 128), 1) % 64

    def step(s, carry):
        at = pl.ds(pl.multiple_of(s * 16, 16), 16)
        x = [pooled[a, at, :].astype(F32) for a in range(ENS)]
        y = [
            jnp.where(lane < 24, pltpu.roll(v, 104, 1), pltpu.roll(v, 24, 1)) for v in x
        ]
        y = [jnp.where(lane < 48, v, 0.0) for v in y]
        goal = target[at, :].astype(F32)
        for a in range(ENS):
            pair = jnp.zeros((16, 128), F32)
            for b in range(ENS):
                if b != a:
                    pair = pair + soft_sign(x[a] - x[b])
                pair = pair + soft_sign(x[a] - y[b])
            grad[a, at, :] = (soft_sign(x[a] - goal) / 16.0 - pair / 240.0).astype(BF)
        return carry

    lax.fori_loop(0, PART // 16, step, 0)


def spread_kernel(grad, leg, chosen, send, owned, rows, more):
    rows[:, 30:32, :] = jnp.zeros((BANDS, 2, 128), F32)
    more[:, 25:32, :] = jnp.zeros((BANDS, 7, 128), F32)
    for ml in range(ORDERS):
        g = grad[ml * L : (ml + 1) * L, :]
        s = jnp.dot(leg[ml], g, preferred_element_type=F32)
        for j in range(ROWS):
            rows[:, ml * 6 + j, :] = s[j * 32 : (j + 1) * 32, :]
        o = jnp.dot(chosen[...], g, preferred_element_type=F32)
        for j in range(5):
            more[:, ml * 5 + j, :] = o[j * 32 : (j + 1) * 32, :]
    send[...] = rows[...].astype(BF)
    owned[...] = more[...].astype(BF)


def backward_kernel(recv, mixing, table, slope, hid, rows, left):
    rows[...] = jnp.dot(
        recv[...].reshape(BANDS * 32, 128), mixing[...], preferred_element_type=F32
    ).reshape(BANDS, 32, 128)
    for i in range(ROWS):
        j = (i % 2) * 3 + i // 2
        q = jnp.concatenate([rows[:, ml * 6 + j, :] for ml in range(ORDERS)], axis=0)
        qt = q.T
        for r in range(2):
            for k in range(2):
                left[r, k, i * 24 : (i + 1) * 24, :] = qt[r * 64 + k * 24 : r * 64 + k * 24 + 24, :]
    for k in range(2):
        grad = jnp.dot(left[0, k].astype(BF), table[0:M, :], preferred_element_type=F32)
        grad = grad + jnp.dot(left[1, k].astype(BF), table[M:, :], preferred_element_type=F32)
        hid[k] = (grad * slope[k].astype(F32)).astype(BF)


def final_kernel(low, own, high, weights, out, ext, prod):
    for k in range(2):
        for h in range(2):
            part = slice(h * 72, (h + 1) * 72)
            out[k, part, :] = (
                own[k, part, :].astype(F32)
                + conv_half(low, own, high, weights, ext, prod, k, h)
            ).astype(BF)


def call(kernel, outs, scratch, *args):
    spec = pl.BlockSpec(memory_space=pltpu.VMEM)
    return pl.pallas_call(
        kernel,
        out_shape=[jax.ShapeDtypeStruct(s, BF) for s in outs],
        in_specs=[spec] * len(args),
        out_specs=[spec] * len(outs),
        scratch_shapes=[pltpu.VMEM(s, d) for s, d in scratch],
        compiler_params=pltpu.CompilerParams(vmem_limit_bytes=48 << 20),
    )(*args)


def edges(x):
    count = lax.axis_size("lat")
    up = [(i, i + 1) for i in range(count - 1)]
    low = lax.ppermute(x[:, 72:], "lat", up)
    high = lax.ppermute(x[:, :72], "lat", [(b, a) for a, b in up])
    return low, high


def swap(x, axis):
    return lax.all_to_all(x, axis, split_axis=0, concat_axis=0, tiled=True)


CONV = [((216, 1536), BF), ((504, 1536), F32)]
CHUNK = (BANDS, 32, 128)


def local(fields, depth_kernel, mix_weight, legendre, truth, degree_order):
    table = jnp.asarray(wave_table())
    x = jnp.transpose(fields, (0, 2, 1, 3)).reshape(2, 144, NLON)
    low, high = edges(x)
    leg = legendre.reshape(3, 2, BANDS, ORDERS, L).transpose(2, 3, 1, 0, 4)
    leg = swap(leg, "lat").transpose(1, 2, 3, 0, 4).reshape(ORDERS, 192, L)
    block = jnp.transpose(mix_weight)
    placing = jnp.stack(
        [
            jnp.kron(jnp.eye(ROWS, dtype=BF), jnp.pad(block, ((0, 0), (24 * k, 40 - 24 * k))))
            for k in range(2)
        ]
    )
    mixing = jnp.kron(
        jnp.eye(2, dtype=BF),
        jnp.pad(jnp.kron(jnp.eye(2, dtype=BF), mix_weight), ((0, 16), (0, 16))),
    )
    weights = banded(depth_kernel)
    flipped = banded(depth_kernel[:, ::-1, ::-1])
    lanes = np.arange(128)
    spot = (
        (lanes[None, None, :] // 64 == np.arange(2)[None, :, None])
        & (lanes[None, None, :] % 64 < 48)
        & (lanes[None, None, :] % 64 % 24 == np.arange(C)[:, None, None])
    )
    mine = lax.dynamic_slice_in_dim(truth, lax.axis_index("lat") * ORDERS, ORDERS, 2)
    target = jnp.einsum(
        "crml,crn->mln", mine, jnp.asarray(spot, BF), preferred_element_type=F32
    ).astype(BF)
    target = jnp.pad(target.reshape(800, 128), ((0, 96), (0, 0)))
    target = lax.dynamic_slice_in_dim(target, lax.axis_index("ens") * PART, PART, 0)
    place = degree_order.reshape(BANDS, 5).T.reshape(L)
    chosen = (place[:, None] == jnp.arange(L, dtype=jnp.int32)[None, :]).astype(BF)

    slope, send = call(
        forward_kernel,
        [(2, 144, NLON), CHUNK],
        CONV + [((2, 144, NLON), BF), (CHUNK, F32)],
        low, x, high, weights, table, placing,
    )
    (coeff,) = call(legendre_kernel, [(896, 128)], [(CHUNK, F32)], swap(send, "lat"), leg)
    pooled = swap(coeff.reshape(ENS, PART, 128), "ens")
    (grad,) = call(score_kernel, [(ENS, PART, 128)], [], pooled, target)
    grad = swap(grad, "ens").reshape(896, 128)
    send, owned = call(
        spread_kernel, [CHUNK, CHUNK], [(CHUNK, F32), (CHUNK, F32)], grad, leg, chosen
    )
    recv = swap(send, "lat")
    owned = swap(owned, "lat")
    (hid,) = call(
        backward_kernel,
        [(2, 144, NLON)],
        [(CHUNK, F32), ((2, 2, 144, M), F32)],
        recv, mixing, table, slope,
    )
    low, high = edges(hid)
    (out,) = call(final_kernel, [(2, 144, NLON)], CONV, low, hid, high, flipped)
    grad_fields = jnp.transpose(out.reshape(2, ROWS, C, NLON), (0, 2, 1, 3))
    score = owned[:, :25].reshape(BANDS, ORDERS, 5, 2, 64)[..., :48]
    score = score.reshape(BANDS, ORDERS, 5, 2, 2, C).transpose(4, 5, 3, 0, 1, 2)
    return grad_fields, score.reshape(2, C, 2, M, 5).astype(F32)


def solution(mesh):
    placed = (P("ens", None, "lat", None), P(), P(), P("lat", None, None), P(), P())
    return jax.shard_map(
        local,
        mesh=mesh,
        in_specs=placed,
        out_specs=(P("ens", None, "lat", None), P("ens", None, None, None, "lat")),
        check_vma=False,
    )
```

time: 206 us -> 140 us (0.68)
  other arithmetic: 67.9 us -> 6.01 us
  blocking collectives: 37.9 us -> 0 us
  waiting for transfers between devices: 13.2 us -> 33.5 us
  Pallas kernels: 0 us -> 19.9 us
  starting transfers between devices: 42.4 us -> 51.7 us
  matrix products: 9.07 us -> 0.26 us
  local copies, waits for them, and re-layouts: 29.9 us -> 24.8 us
    all_to_all x3 -> x0, blocking collectives: 37.9 us -> none  [the longest x1 15.1 us: local(): lax.all_to_all(owned, 'lat', split_axis=4, concat_axis=3, tiled=True)]
    convert_element_type x6 -> x5, other arithmetic: 32.2 us -> 1.1 us  [the longest x1 1 us: local(): return (grad_fields, score.reshape(2, C, 2, M, 5).astype(F32))]
    add x1 -> x2, other arithmetic: 27.5 us -> 0.02 us  [banded(): same = out_row % C == in_row % C]
    all_to_all x3 -> x6, waiting for transfers between devices: 13.2 us -> 33.5 us  [swap(): return lax.all_to_all(x, axis, split_axis=0, concat_axis=0, tiled=True)]
    pallas_call x0 -> x6, Pallas kernels: none -> 19.9 us  [call(): pl.pallas_call(kernel, out_shape=[jax.ShapeDtypeStruct(s, BF) for s in ou...]
    all_to_all x3 -> x6, starting transfers between devices: 29.7 us -> 41.9 us  [swap(): return lax.all_to_all(x, axis, split_axis=0, concat_axis=0, tiled=True)]
    dot_general x5 -> x1, matrix products: 9.07 us -> 0.26 us  [local(): jnp.einsum('crml,crn->mln', mine, jnp.asarray(spot, BF), preferred_elemen...]
    unnamed x178 -> x43, local copies, waits for them, and re-layouts: 14.8 us -> 7.9 us
  transfers between devices with their start and end apart: 7 -> 10, of which waited for: 2 -> 6; matrix products, arithmetic and copies ran while one was open for 27% -> 20% of each run, Pallas kernels for 0% -> 6%
where the time goes in v2:
time: 140 us; the launch traced here: 137 us
  starting transfers between devices  51.7 us (37%)
  waiting for transfers between devices  33.5 us (24%)
  local copies, waits for them, and re-layouts  24.8 us (18%)
  Pallas kernels  19.9 us (14%)
  other arithmetic  6.01 us (4%)
    all_to_all x6, starting transfers between devices, swap(): return lax.all_to_all(x, axis, split_axis=0, concat_axis=0, tiled=True)  41.9 us
    all_to_all x6, waiting for transfers between devices, swap(): return lax.all_to_all(x, axis, split_axis=0, concat_axis=0, tiled=True)  33.5 us
    pallas_call x6, Pallas kernels, call(): pl.pallas_call(kernel, out_shape=[jax.ShapeDtypeStruct(s, BF) for s in ou...  19.9 us
    unnamed x43, local copies, waits for them, and re-layouts  7.9 us
    ppermute x2, starting transfers between devices, edges(): low = lax.ppermute(x[:, 72:], 'lat', up)  7.19 us
    convert_element_type x2, local copies, waits for them, and re-layouts, local(): return (grad_fields, score.reshape(2, C, 2, M, 5).astype(F32))  6.1 us
    select_n x2, other arithmetic, banded(): total = jnp.where(same & (gap == p), cols[:, p:p + 1], total)  3.34 us
    slice x2, local copies, waits for them, and re-layouts, edges(): high = lax.ppermute(x[:, :72], 'lat', [(b, a) for a, b in up])  3.27 us
  transfers between devices with their start and end apart: 10, of which 6 were waited for; matrix products, arithmetic and copies ran while one was open for 20% of the time, Pallas kernels for 6%

profile of v2, /device:TPU:1, one launch (start us, length us, event | category | flops | bytes accessed | tf_op | source)
XLA Modules:
  0.0 137.2 jit_solution(2376414242788704809)
XLA Ops:
  0.7 2.3 %fusion.31 = (bf16[2,72,1440]{2,1,0:T(8,128)(2,1)}, bf16[2,72,1440]{2,1,0:T(8,128)(2,1)}) fusion(bf16[2,144,1440]{2,1,0:T(8,128)(2,1)} %bitcast.40), kind=kLoop, calls=%fused_computation.74 | loop fusion | bytes 1658880 | tf_op jit(solution)/shard_map/slice | solution.py:199
  2.9 4.0 %collective-permute-start = (bf16[2,72,1440]{2,1,0:T(8,128)(2,1)}, bf16[2,72,1440]{2,1,0:T(8,128)(2,1)S(1)}, u32[]{:S(2)}, u32[]{:S(2)}) collective-permute-start(bf16[2,72,1440]{2,1,0:T(8,128)(2,1)} %get-tuple-element.33), channel_id=1, source_target_pairs={{0,1},{1,2},{2,3},{3,4},{4,5},{5,6},{6,7},{7,8},{8,9},{9,10},{10,1... | collective-permute-start | bytes 1244168 | tf_op jit(solution)/shard_map/ppermute | solution.py:198
  7.0 1.3 collective-permute-start.1
  8.3 2.1 %copy.39 = bf16[6,160,160]{2,0,1:T(8,128)(2,1)} copy(bf16[6,160,160]{2,1,0:T(8,128)(2,1)} %param.11) | data formatting | bytes 614400 | tf_op args[3]
  10.4 2.5 %reshape.124 = bf16[3,2,32,5,160]{4,1,0,3,2:T(2,128)(2,1)} reshape(bf16[6,160,160]{2,0,1:T(8,128)(2,1)} %copy.39) | data formatting | bytes 614400 | tf_op jit(solution)/shard_map/reshape | solution.py:215
  12.9 12.9 %all-to-all-start.1 = ((bf16[32,5,2,3,160]{4,2,3,1,0:T(2,128)(2,1)}), bf16[32,5,2,3,160]{4,2,3,1,0:T(2,128)(2,1)}, u32[]{:S(2)}, u32[]{:S(2)}) async-start(bf16[32,5,2,3,160]{4,2,3,1,0:T(2,128)(2,1)} %bitcast.45), calls=%async_computation.1 | async-start | bytes 983040 | tf_op jit(solution)/shard_map/all_to_all | solution.py:204
  26.0 0.1 convert_element_type.68
  26.1 0.6 slice_reduce_fusion.13
  26.9 0.1 broadcast_multiply_fusion.1
  27.0 0.6 fusion.26
  27.6 0.6 compare_and_fusion
  28.2 0.2 mul.110
  28.4 0.2 mul.113
  28.7 2.1 %select_select_fusion.1.weights = bf16[504,216]{1,0:T(8,128)(2,1)S(1)} fusion(bf16[504]{0:T(512)(128)(2,1)S(1)} %get-tuple-element.24, bf16[504]{0:T(512)(128)(2,1)S(1)} %get-tuple-element.25, bf16[504]{0:T(512)(128)(2,1)S(1)} %get-tuple-element.26, bf16[504]{0:T(512)(128)(2,1)} %get-tuple-element.27, bf16[504]{0:T(512)(128)(2,1)} %get-tuple-element.28, ...), kind=kLoop, calls=%fused_computation.25 | loop fusion | flops 3592512 | bytes 237744 | tf_op jit(solution)/shard_map/jit(_where)/select_n | solution.py:42
  30.9 0.8 copy-done.2
  31.6 1.0 copy-done.3
  32.7 6.9 %shard_map.95 = (bf16[2,144,1440]{2,1,0:T(8,128)(2,1)S(1)}, bf16[32,32,128]{2,1,0:T(8,128)(2,1)}) custom-call(bf16[2,72,1440]{2,1,0:T(8,128)(2,1)S(1)} %collective-permute-done.low, bf16[2,144,1440]{2,1,0:T(8,128)(2,1)S(1)} %bitcast.41, bf16[2,72,1440]{2,1,0:T(8,128)(2,1)S(1)} %copy-done.3, bf16[504,216]{1,0:T(8,128)(2,1)S(1)} %select_select_fusion.1.weights, ...), custom_call_target="tpu_custom_call" | custom-call | tf_op jit(solution)/shard_map/pallas_call | solution.py:185
  39.5 1.2 all-to-all-done.1
  40.7 7.9 %all-to-all-start = ((bf16[32,32,128]{2,1,0:T(8,128)(2,1)}), bf16[32,32,128]{2,1,0:T(8,128)(2,1)S(1)}, u32[]{:S(2)}, u32[]{:S(2)}) async-start(bf16[32,32,128]{2,1,0:T(8,128)(2,1)} %get-tuple-element.6), calls=%async_computation | async-start | bytes 524288 | tf_op jit(solution)/shard_map/all_to_all | solution.py:204
  48.7 0.8 reshape.129
  49.7 1.1 constant_dynamic-slice_fusion
  50.7 0.3 fusion
  51.0 1.1 copy.40
  52.1 7.0 %all-to-all-done.recv = bf16[32,32,128]{2,1,0:T(8,128)(2,1)S(1)} async-done(((bf16[32,32,128]{2,1,0:T(8,128)(2,1)}), bf16[32,32,128]{2,1,0:T(8,128)(2,1)S(1)}, u32[]{:S(2)}, u32[]{:S(2)}) %all-to-all-start) | async-done | bytes 262176 | tf_op jit(solution)/shard_map/all_to_all | solution.py:204
  59.1 1.3 shard_map.96
  60.4 8.1 %all-to-all-start.2 = ((bf16[8,112,128]{2,1,0:T(8,128)(2,1)}), bf16[8,112,128]{2,1,0:T(8,128)(2,1)S(1)}, u32[]{:S(2)}, u32[]{:S(2)}) async-start(bf16[8,112,128]{2,1,0:T(8,128)(2,1)} %bitcast.8), calls=%async_computation.2 | async-start | bytes 458752 | tf_op jit(solution)/shard_map/all_to_all | solution.py:204
  68.5 6.1 %all-to-all-done.2.pooled = bf16[8,112,128]{2,1,0:T(8,128)(2,1)S(1)} async-done(((bf16[8,112,128]{2,1,0:T(8,128)(2,1)}), bf16[8,112,128]{2,1,0:T(8,128)(2,1)S(1)}, u32[]{:S(2)}, u32[]{:S(2)}) %all-to-all-start.2) | async-done | bytes 229408 | tf_op jit(solution)/shard_map/all_to_all | solution.py:204
  74.7 2.4 %shard_map.97 = bf16[8,112,128]{2,1,0:T(8,128)(2,1)} custom-call(bf16[8,112,128]{2,1,0:T(8,128)(2,1)S(1)} %all-to-all-done.2.pooled, bf16[112,128]{1,0:T(8,128)(2,1)S(1)} %pad_dynamic-slice_fusion.target), custom_call_target="tpu_custom_call" | custom-call | tf_op jit(solution)/shard_map/pallas_call | solution.py:185
  77.2 4.3 %all-to-all-start.3 = ((bf16[8,112,128]{2,1,0:T(8,128)(2,1)}), bf16[8,112,128]{2,1,0:T(8,128)(2,1)S(1)}, u32[]{:S(2)}, u32[]{:S(2)}) async-start(bf16[8,112,128]{2,1,0:T(8,128)(2,1)} %shard_map.97), calls=%async_computation.3 | async-start | bytes 458752 | tf_op jit(solution)/shard_map/all_to_all | solution.py:204
  81.6 6.1 %all-to-all-done.3 = bf16[8,112,128]{2,1,0:T(8,128)(2,1)S(1)} async-done(((bf16[8,112,128]{2,1,0:T(8,128)(2,1)}), bf16[8,112,128]{2,1,0:T(8,128)(2,1)S(1)}, u32[]{:S(2)}, u32[]{:S(2)}) %all-to-all-start.3) | async-done | bytes 229408 | tf_op jit(solution)/shard_map/all_to_all | solution.py:204
  87.7 1.7 %shard_map.98 = (bf16[32,32,128]{2,1,0:T(8,128)(2,1)}, bf16[32,32,128]{2,1,0:T(8,128)(2,1)}) custom-call(bf16[896,128]{1,0:T(8,128)(2,1)S(1)} %bitcast.42, bf16[5,192,160]{2,1,0:T(8,128)(2,1)S(1)} %bitcast.39, bf16[160,160]{1,0:T(8,128)(2,1)S(1)} %fusion.19.chosen), custom_call_target="tpu_custom_call" | custom-call | tf_op jit(solution)/shard_map/pallas_call | solution.py:185
  89.4 4.1 %all-to-all-start.4 = ((bf16[32,32,128]{2,1,0:T(8,128)(2,1)}), bf16[32,32,128]{2,1,0:T(8,128)(2,1)S(1)}, u32[]{:S(2)}, u32[]{:S(2)}) async-start(bf16[32,32,128]{2,1,0:T(8,128)(2,1)} %get-tuple-element.7), calls=%async_computation.4 | async-start | bytes 524288 | tf_op jit(solution)/shard_map/all_to_all | solution.py:204
  93.6 0.1 broadcast_multiply_fusion.2
  93.9 0.1 convert_element_type.75
  94.1 10.6 %all-to-all-done.4.recv = bf16[32,32,128]{2,1,0:T(8,128)(2,1)S(1)} async-done(((bf16[32,32,128]{2,1,0:T(8,128)(2,1)}), bf16[32,32,128]{2,1,0:T(8,128)(2,1)S(1)}, u32[]{:S(2)}, u32[]{:S(2)}) %all-to-all-start.4) | async-done | bytes 262176 | tf_op jit(solution)/shard_map/all_to_all | solution.py:204
  104.7 4.6 %all-to-all-start.5 = ((bf16[32,32,128]{2,1,0:T(8,128)(2,1)}), bf16[32,32,128]{2,1,0:T(8,128)(2,1)S(1)}, u32[]{:S(2)}, u32[]{:S(2)}) async-start(bf16[32,32,128]{2,1,0:T(8,128)(2,1)} %get-tuple-element.9), calls=%async_computation.5 | async-start | bytes 524288 | tf_op jit(solution)/shard_map/all_to_all | solution.py:204
  109.3 1.2 shard_map.99.own
  110.5 1.0 fusion.30
  111.5 3.1 %collective-permute-start.2 = (bf16[2,72,1440]{2,1,0:T(8,128)(2,1)}, bf16[2,72,1440]{2,1,0:T(8,128)(2,1)S(1)}, u32[]{:S(2)}, u32[]{:S(2)}) collective-permute-start(bf16[2,72,1440]{2,1,0:T(8,128)(2,1)} %get-tuple-element.31), channel_id=1, source_target_pairs={{0,1},{1,2},{2,3},{3,4},{4,5},{5,6},{6,7},{7,8},{8,9},{9,10},{10,1... | collective-permute-start | bytes 1244168 | tf_op jit(solution)/shard_map/ppermute | solution.py:198
  114.6 1.3 collective-permute-start.3
  116.0 1.2 select_select_fusion.weights
  117.2 2.5 %all-to-all-done.5 = bf16[32,32,128]{2,1,0:T(8,128)(2,1)S(1)} async-done(((bf16[32,32,128]{2,1,0:T(8,128)(2,1)}), bf16[32,32,128]{2,1,0:T(8,128)(2,1)S(1)}, u32[]{:S(2)}, u32[]{:S(2)}) %all-to-all-start.5) | async-done | bytes 262176 | tf_op jit(solution)/shard_map/all_to_all | solution.py:204
  119.7 0.2 reshape.136
  119.9 1.0 copy_convert_fusion
  120.9 2.6 %copy.45 = f32[32,5,5,2,48]{0,4,3,2,1:T(8,128)} copy(f32[32,5,5,2,48]{4,0,3,2,1:T(8,128)} %copy_convert_fusion) | data formatting | bytes 614400 | tf_op jit(solution)/shard_map/convert_element_type | solution.py:271
  123.5 3.5 %copy.46 = f32[2,24,2,32,5,5]{1,2,5,4,3,0:T(2,128)} copy(f32[2,24,2,32,5,5]{3,1,0,2,5,4:T(8,128)} %bitcast.44) | data formatting | bytes 614400 | tf_op jit(solution)/shard_map/convert_element_type | solution.py:271
  127.0 3.8 %copy.47 = f32[2,24,2,160,5]{3,2,4,1,0:T(2,128)} copy(f32[2,24,2,160,5]{1,2,4,3,0:T(2,128)} %bitcast.43) | data formatting | bytes 614400
  130.8 6.4 %shard_map.100 = bf16[2,144,1440]{2,1,0:T(8,128)(2,1)} custom-call(bf16[2,72,1440]{2,1,0:T(8,128)(2,1)S(1)} %collective-permute-done.2.low, bf16[2,144,1440]{2,1,0:T(8,128)(2,1)S(1)} %shard_map.99.own, bf16[2,72,1440]{2,1,0:T(8,128)(2,1)S(1)} %collective-permute-done.3.high, bf16[504,216]{1,0:T(8,128)(2,1)S(1)} %select_select_fusion.weights), custom_call_target="tpu_custom_call" | custom-call | tf_op jit(solution)/shard_map/pallas_call | solution.py:185
  (64 shorter events, 1.0 us)
Async XLA Ops:
  0.6 31.0 %copy-start = (bf16[320,1440]{1,0:T(8,128)(2,1)S(1)}, bf16[320,1440]{1,0:T(8,128)(2,1)}, u32[]{:S(2)}) copy-start(bf16[320,1440]{1,0:T(8,128)(2,1)} %constant.82.clone.table) | copy-start | bytes 2764804
  0.6 31.0 %copy-start.1 = (bf16[2,24,6,1440]{3,1,2,0:T(8,128)(2,1)S(1)}, bf16[2,24,6,1440]{3,1,2,0:T(8,128)(2,1)}, u32[]{:S(2)}) copy-start(bf16[2,24,6,1440]{3,1,2,0:T(8,128)(2,1)} %param.8) | copy-start | bytes 2488324
  0.7 25.3 %copy-start.4 = (f32[24,7,7]{0,2,1:T(8,128)S(1)}, f32[24,7,7]{0,2,1:T(8,128)}, u32[]{:S(2)}) copy-start(f32[24,7,7]{0,2,1:T(8,128)} %param.9) | copy-start | bytes 14116
  0.7 26.1 %copy-start.5 = (bf16[24,24]{1,0:T(8,128)(2,1)S(1)}, bf16[24,24]{1,0:T(8,128)(2,1)}, u32[]{:S(2)}) copy-start(bf16[24,24]{1,0:T(8,128)(2,1)} %param.10) | copy-start | bytes 3460
  2.9 27.9 %collective-permute-start = (bf16[2,72,1440]{2,1,0:T(8,128)(2,1)}, bf16[2,72,1440]{2,1,0:T(8,128)(2,1)S(1)}, u32[]{:S(2)}, u32[]{:S(2)}) collective-permute-start(bf16[2,72,1440]{2,1,0:T(8,128)(2,1)} %get-tuple-element.33), channel_id=1, source_target_pairs={{0,1},{1,2},{2,3},{3,4},{4,5},{5,6},{6,7},{7,8},{8,9},{9,10},{10,1... | collective-permute-start | bytes 1244168 | tf_op jit(solution)/shard_map/ppermute | solution.py:198
  7.0 23.9 %collective-permute-start.1 = (bf16[2,72,1440]{2,1,0:T(8,128)(2,1)}, bf16[2,72,1440]{2,1,0:T(8,128)(2,1)S(1)}, u32[]{:S(2)}, u32[]{:S(2)}) collective-permute-start(bf16[2,72,1440]{2,1,0:T(8,128)(2,1)} %get-tuple-element.32), channel_id=1, source_target_pairs={{1,0},{2,1},{3,2},{4,3},{5,4},{6,5},{7,6},{8,7},{9,8},{10,9},{11,1... | collective-permute-start | bytes 1244168 | tf_op jit(solution)/shard_map/ppermute | solution.py:199
  12.9 37.8 %copy-start.6 = (bf16[24,2,128,1]{2,0,1,3:T(8,128)(2,1)S(1)}, bf16[24,2,128,1]{2,0,1,3:T(8,128)(2,1)}, u32[]{:S(2)}) copy-start(bf16[24,2,128,1]{2,0,1,3:T(8,128)(2,1)} %constant.94) | copy-start | bytes 36868
  12.9 27.8 %all-to-all-start.1 = ((bf16[32,5,2,3,160]{4,2,3,1,0:T(2,128)(2,1)}), bf16[32,5,2,3,160]{4,2,3,1,0:T(2,128)(2,1)}, u32[]{:S(2)}, u32[]{:S(2)}) async-start(bf16[32,5,2,3,160]{4,2,3,1,0:T(2,128)(2,1)} %bitcast.45), calls=%async_computation.1 | async-start | bytes 983040 | tf_op jit(solution)/shard_map/all_to_all | solution.py:204
  25.9 4.9 %copy-start.7 = (s32[216]{0:T(256)}, s32[216]{0:T(256)S(1)}, u32[]{:S(2)}) copy-start(s32[216]{0:T(256)S(1)} %get-tuple-element.42) | copy-start | bytes 2596
  25.9 4.9 %copy-start.9 = (s32[216]{0:T(256)}, s32[216]{0:T(256)S(1)}, u32[]{:S(2)}) copy-start(s32[216]{0:T(256)S(1)} %get-tuple-element.43) | copy-start | bytes 2596
  25.9 4.9 %copy-start.11 = (s32[216]{0:T(256)}, s32[216]{0:T(256)S(1)}, u32[]{:S(2)}) copy-start(s32[216]{0:T(256)S(1)} %get-tuple-element.48) | copy-start | bytes 2596
  25.9 4.9 %copy-start.13 = (s32[216]{0:T(256)}, s32[216]{0:T(256)S(1)}, u32[]{:S(2)}) copy-start(s32[216]{0:T(256)S(1)} %get-tuple-element.49) | copy-start | bytes 2596
  27.6 3.3 %copy-start.15 = (pred[504]{0:T(512)(128)(4,1)}, pred[504]{0:T(512)(128)(4,1)S(1)}, u32[]{:S(2)}) copy-start(pred[504]{0:T(512)(128)(4,1)S(1)} %get-tuple-element.44) | copy-start | bytes 1516
  30.9 0.8 copy-start.2
  31.6 1.0 copy-start.3
  40.7 18.4 %all-to-all-start = ((bf16[32,32,128]{2,1,0:T(8,128)(2,1)}), bf16[32,32,128]{2,1,0:T(8,128)(2,1)S(1)}, u32[]{:S(2)}, u32[]{:S(2)}) async-start(bf16[32,32,128]{2,1,0:T(8,128)(2,1)} %get-tuple-element.6), calls=%async_computation | async-start | bytes 524288 | tf_op jit(solution)/shard_map/all_to_all | solution.py:204
  60.4 14.3 %all-to-all-start.2 = ((bf16[8,112,128]{2,1,0:T(8,128)(2,1)}), bf16[8,112,128]{2,1,0:T(8,128)(2,1)S(1)}, u32[]{:S(2)}, u32[]{:S(2)}) async-start(bf16[8,112,128]{2,1,0:T(8,128)(2,1)} %bitcast.8), calls=%async_computation.2 | async-start | bytes 458752 | tf_op jit(solution)/shard_map/all_to_all | solution.py:204
  77.1 38.8 %copy-start.8 = (s32[216]{0:T(256)S(1)}, s32[216]{0:T(256)}, u32[]{:S(2)}) copy-start(s32[216]{0:T(256)} %copy-done.7) | copy-start | bytes 2596
  77.1 38.8 %copy-start.10 = (s32[216]{0:T(256)S(1)}, s32[216]{0:T(256)}, u32[]{:S(2)}) copy-start(s32[216]{0:T(256)} %copy-done.9) | copy-start | bytes 2596
  77.1 38.8 %copy-start.12 = (s32[216]{0:T(256)S(1)}, s32[216]{0:T(256)}, u32[]{:S(2)}) copy-start(s32[216]{0:T(256)} %copy-done.11) | copy-start | bytes 2596
  77.1 38.8 %copy-start.14 = (s32[216]{0:T(256)S(1)}, s32[216]{0:T(256)}, u32[]{:S(2)}) copy-start(s32[216]{0:T(256)} %copy-done.13) | copy-start | bytes 2596
  77.1 38.8 %copy-start.16 = (pred[504]{0:T(512)(128)(4,1)S(1)}, pred[504]{0:T(512)(128)(4,1)}, u32[]{:S(2)}) copy-start(pred[504]{0:T(512)(128)(4,1)} %copy-done.15) | copy-start | bytes 1516
  77.2 38.8 %copy-start.17 = (pred[504]{0:T(512)(128)(4,1)S(1)}, pred[504]{0:T(512)(128)(4,1)}, u32[]{:S(2)}) copy-start(pred[504]{0:T(512)(128)(4,1)} %get-tuple-element.45) | copy-start | bytes 1516
  77.2 38.8 %copy-start.18 = (pred[216]{0:T(512)(128)(4,1)S(1)}, pred[216]{0:T(512)(128)(4,1)}, u32[]{:S(2)}) copy-start(pred[216]{0:T(512)(128)(4,1)} %get-tuple-element.46) | copy-start | bytes 652
  77.2 38.8 %copy-start.19 = (pred[216]{0:T(512)(128)(4,1)S(1)}, pred[216]{0:T(512)(128)(4,1)}, u32[]{:S(2)}) copy-start(pred[216]{0:T(512)(128)(4,1)} %get-tuple-element.47) | copy-start | bytes 652
  77.2 10.5 %all-to-all-start.3 = ((bf16[8,112,128]{2,1,0:T(8,128)(2,1)}), bf16[8,112,128]{2,1,0:T(8,128)(2,1)S(1)}, u32[]{:S(2)}, u32[]{:S(2)}) async-start(bf16[8,112,128]{2,1,0:T(8,128)(2,1)} %shard_map.97), calls=%async_computation.3 | async-start | bytes 458752 | tf_op jit(solution)/shard_map/all_to_all | solution.py:204
  89.4 15.3 %all-to-all-start.4 = ((bf16[32,32,128]{2,1,0:T(8,128)(2,1)}), bf16[32,32,128]{2,1,0:T(8,128)(2,1)S(1)}, u32[]{:S(2)}, u32[]{:S(2)}) async-start(bf16[32,32,128]{2,1,0:T(8,128)(2,1)} %get-tuple-element.7), calls=%async_computation.4 | async-start | bytes 524288 | tf_op jit(solution)/shard_map/all_to_all | solution.py:204
  104.7 15.0 %all-to-all-start.5 = ((bf16[32,32,128]{2,1,0:T(8,128)(2,1)}), bf16[32,32,128]{2,1,0:T(8,128)(2,1)S(1)}, u32[]{:S(2)}, u32[]{:S(2)}) async-start(bf16[32,32,128]{2,1,0:T(8,128)(2,1)} %get-tuple-element.9), calls=%async_computation.5 | async-start | bytes 524288 | tf_op jit(solution)/shard_map/all_to_all | solution.py:204
  111.5 19.4 %collective-permute-start.2 = (bf16[2,72,1440]{2,1,0:T(8,128)(2,1)}, bf16[2,72,1440]{2,1,0:T(8,128)(2,1)S(1)}, u32[]{:S(2)}, u32[]{:S(2)}) collective-permute-start(bf16[2,72,1440]{2,1,0:T(8,128)(2,1)} %get-tuple-element.31), channel_id=1, source_target_pairs={{0,1},{1,2},{2,3},{3,4},{4,5},{5,6},{6,7},{7,8},{8,9},{9,10},{10,1... | collective-permute-start | bytes 1244168 | tf_op jit(solution)/shard_map/ppermute | solution.py:198
  114.6 16.2 %collective-permute-start.3 = (bf16[2,72,1440]{2,1,0:T(8,128)(2,1)}, bf16[2,72,1440]{2,1,0:T(8,128)(2,1)S(1)}, u32[]{:S(2)}, u32[]{:S(2)}) collective-permute-start(bf16[2,72,1440]{2,1,0:T(8,128)(2,1)} %get-tuple-element.30), channel_id=1, source_target_pairs={{1,0},{2,1},{3,2},{4,3},{5,4},{6,5},{7,6},{8,7},{9,8},{10,9},{11,1... | collective-permute-start | bytes 1244168 | tf_op jit(solution)/shard_map/ppermute | solution.py:199

commit v3 on v2

v3 whole, which is shorter than its diff:
```python
import math

import jax
import jax.numpy as jnp
import ml_dtypes
import numpy as np
from jax import lax
from jax.experimental import pallas as pl
from jax.experimental.pallas import tpu as pltpu
from jax.sharding import PartitionSpec as P

C = 24
NLON = 1440
M = 160
L = 160
BANDS = 32
ROWS = 6
ORDERS = M // BANDS
ENS = 8
PART = 112
BF = jnp.bfloat16
F32 = jnp.float32
MESH = pl.DeviceIdType.MESH


def wave_table():
    m = (np.arange(BANDS)[None, :] * ORDERS + np.arange(ORDERS)[:, None]).reshape(-1)
    angles = (m[:, None] * np.arange(NLON)[None, :] % NLON) * (2.0 * math.pi / NLON)
    both = np.concatenate([np.cos(angles), -np.sin(angles)], axis=0) / math.sqrt(NLON)
    return both.astype(np.float32).astype(ml_dtypes.bfloat16)


def wrapped(x):
    return jnp.concatenate([x[:, NLON - 3 :], x, x[:, :93]], axis=1)


def spread_weights(cols, dst, tmp, flip):
    lane = lax.broadcasted_iota(jnp.int32, (C, 216), 1)
    same = lane % C == lax.broadcasted_iota(jnp.int32, (C, 216), 0)
    for h in range(2):
        row = lane // C
        window = lax.rem(row + 3, 9) if h == 0 else row
        masks = [same & (window == g) for g in range(9)]
        for q in range(7):
            taps = []
            for p in range(7):
                a, b = (6 - q, 6 - p) if flip else (q, p)
                taps.append(jnp.broadcast_to(cols[a, :, b : b + 1], (C, 216)))
            for i in range(3):
                total = jnp.zeros((C, 216), F32)
                for p in range(7):
                    total = jnp.where(masks[i + p], taps[p], total)
                tmp[q * 72 + i * 24 : q * 72 + i * 24 + 24, :] = total
        dst[h] = tmp[...].astype(BF)


def conv_half(weights, ext, prod, h):
    prod[...] = jnp.dot(weights[h], ext[...], preferred_element_type=F32)
    total = prod[0:72, 0:NLON]
    for q in range(1, 7):
        total = total + prod[q * 72 : (q + 1) * 72, q : q + NLON]
    return total


def soft_sign(gaps):
    return gaps * lax.rsqrt(gaps * gaps + 0.25)


class Exchange:
    def __init__(self, axis, count, me, block, slot, sent, landed, sems):
        self.axis, self.count, self.me = axis, count, me
        self.block, self.slot = block, slot
        self.sent, self.landed, self.sems = sent, landed, sems

    def copy(self, source, target, peer):
        return pltpu.make_async_remote_copy(
            src_ref=source,
            dst_ref=target,
            send_sem=self.sems.at[0],
            recv_sem=self.sems.at[1],
            device_id={self.axis: peer},
            device_id_type=MESH,
        )

    def start(self):
        def step(s, carry):
            peer = lax.rem(self.me + s, self.count)
            self.copy(self.block(peer), self.slot(self.me), peer).start()
            return carry

        lax.fori_loop(1, self.count, step, 0)

    def whole(self):
        return self.copy(self.sent, self.landed, lax.rem(self.me + 1, self.count))

    def arrived(self):
        self.whole().wait_recv()

    def done(self):
        self.whole().wait_send()


def kernel(
    x, legl, cols, table, placing, mixing, target, chosen,
    out, score,
    low, high, low2, high2, weights, flipped, wtmp, ext, prod, act, slope, hid,
    legf, legsend, legrecv, leg,
    rows, more, send1, recv1, coeff, pooled, grads, gback, send4, recv4, send5, recv5,
    left, turn,
    halo_sems, halo2_sems, leg_sems, sems1, sems2, sems3, sems4, sems5,
):
    me = lax.axis_index("lat")
    em = lax.axis_index("ens")
    after = lax.rem(me + 1, BANDS)
    before = lax.rem(me + BANDS - 1, BANDS)

    barrier = pltpu.get_barrier_semaphore()

    def greet(axis, count, mine):
        def step(s, carry):
            pl.semaphore_signal(
                barrier, 1, device_id={axis: lax.rem(mine + s, count)}, device_id_type=MESH
            )
            return carry

        lax.fori_loop(1, count, step, 0)

    greet("lat", BANDS, me)
    greet("ens", ENS, em)
    pl.semaphore_wait(barrier, BANDS - 1 + ENS - 1)

    def halo(source, lo, hi, sems, k):
        return (
            pltpu.make_async_remote_copy(
                src_ref=source.at[k, 1], dst_ref=lo.at[k],
                send_sem=sems.at[0, k], recv_sem=sems.at[1, k],
                device_id={"lat": after}, device_id_type=MESH,
            ),
            pltpu.make_async_remote_copy(
                src_ref=source.at[k, 0], dst_ref=hi.at[k],
                send_sem=sems.at[2, k], recv_sem=sems.at[3, k],
                device_id={"lat": before}, device_id_type=MESH,
            ),
        )

    halos = [halo(x, low, high, halo_sems, k) for k in range(2)]
    for pair in halos:
        for copy in pair:
            copy.start()

    for i in range(ROWS):
        j = (i % 2) * 3 + i // 2
        legf[0] = legl[i, :, 0:128].astype(F32)
        legf[1] = jnp.concatenate(
            [legl[i, :, 128:L].astype(F32), jnp.zeros((M, 256 - L), F32)], axis=1
        )
        for ml in range(ORDERS):
            for b in range(2):
                more[b, :, ml * 6 + j, :] = legf[b, pl.ds(ml, BANDS, stride=ORDERS), :]
    for b in range(2):
        more[b, :, 30:32, :] = jnp.zeros((BANDS, 2, 128), F32)
        legsend[:, b] = more[b].astype(BF)
    legx = Exchange(
        "lat", BANDS, me, lambda p: legsend.at[p], lambda m: legrecv.at[m],
        legsend.at[pl.ds(0, BANDS - 1)], legrecv.at[pl.ds(0, BANDS - 1)], leg_sems,
    )
    legx.start()
    legrecv[me] = legsend[me]
    spread_weights(cols, weights, wtmp, False)

    def fill_halo(lo, hi, k, h):
        if h == 0:
            edge = wrapped(lo[k].astype(F32))
            ext[144:216, :] = jnp.where(me > 0, edge, 0.0).astype(BF)
        else:
            edge = wrapped(hi[k].astype(F32))
            ext[144:216, :] = jnp.where(me < BANDS - 1, edge, 0.0).astype(BF)

    c0 = math.sqrt(2.0 / math.pi)
    spec = jnp.zeros((2 * M, 384), F32)
    for k in range(2):
        ext[0:72, :] = wrapped(x[k, 0])
        ext[72:144, :] = wrapped(x[k, 1])
        for h in range(2):
            halos[k][h].wait_recv()
            fill_halo(low, high, k, h)
            v = x[k, h].astype(F32) + conv_half(weights, ext, prod, h)
            sq = v * v
            t = jnp.tanh(c0 * v * (1.0 + 0.044715 * sq))
            half = 0.5 * (1.0 + t)
            act[h * 72 : (h + 1) * 72, :] = (v * half).astype(BF)
            slope[k, h] = (half + 0.5 * v * (1.0 - t * t) * (c0 * (1.0 + 0.134145 * sq))).astype(BF)
        waves = lax.dot_general(
            table[...], act[...], (((1,), (1,)), ((), ())), preferred_element_type=F32
        ).astype(BF)
        spec = spec + jnp.dot(waves, placing[k], preferred_element_type=F32)
    rows[:, 30:32, :] = jnp.zeros((BANDS, 2, 128), F32)
    for a in range(10):
        for t in range(3):
            rows[:, t * 10 + a, :] = spec[a * 32 : (a + 1) * 32, t * 128 : (t + 1) * 128]
    send1[...] = rows[...].astype(BF)
    x1 = Exchange(
        "lat", BANDS, me, lambda p: send1.at[p], lambda m: recv1.at[m],
        send1.at[pl.ds(0, BANDS - 1)], recv1.at[pl.ds(0, BANDS - 1)], sems1,
    )
    x1.start()
    recv1[me] = send1[me]

    legx.arrived()
    for b in range(2):
        more[b] = legrecv[:, b].astype(F32)
    for ml in range(ORDERS):
        for j in range(ROWS):
            at = slice(j * 32, (j + 1) * 32)
            leg[ml, at, 0:128] = more[0, :, ml * 6 + j, :].astype(BF)
            leg[ml, at, 128:L] = more[1, :, ml * 6 + j, 0 : L - 128].astype(BF)

    x1.arrived()
    rows[...] = recv1[...].astype(F32)
    lane = lax.broadcasted_iota(jnp.int32, (L, 128), 1)
    for ml in range(ORDERS):
        acc = []
        for r in range(2):
            a = jnp.concatenate(
                [rows[:, t * 10 + r * 5 + ml, :] for t in range(3)], axis=0
            ).astype(BF)
            for par in range(2):
                acc.append(
                    lax.dot_general(
                        leg[ml, par * 96 : (par + 1) * 96, :],
                        a,
                        (((0,), (0,)), ((), ())),
                        preferred_element_type=F32,
                    )
                )
        first = acc[0] + pltpu.roll(acc[1], 64, 1)
        second = pltpu.roll(acc[2], 64, 1) + acc[3]
        coeff[ml * L : (ml + 1) * L, :] = jnp.where(lane < 64, first, second).astype(BF)
    coeff[800:896, :] = jnp.zeros((96, 128), BF)

    def piece(ref, e):
        return ref.at[pl.ds(pl.multiple_of(e * PART, 16), PART)]

    x2 = Exchange(
        "ens", ENS, em, lambda p: piece(coeff, p), lambda m: pooled.at[m],
        coeff.at[pl.ds(0, (ENS - 1) * PART)], pooled.at[pl.ds(0, ENS - 1)], sems2,
    )
    x2.start()
    pooled[em] = piece(coeff, em)[...]
    spread_weights(cols, flipped, wtmp, True)
    x2.arrived()

    small = lax.broadcasted_iota(jnp.int32, (16, 128), 1) % 64

    def step(s, carry):
        at = pl.ds(pl.multiple_of(s * 16, 16), 16)
        u = [pooled[a, at, :].astype(F32) for a in range(ENS)]
        w = [jnp.where(small < 24, pltpu.roll(v, 104, 1), pltpu.roll(v, 24, 1)) for v in u]
        w = [jnp.where(small < 48, v, 0.0) for v in w]
        goal = target[at, :].astype(F32)
        for a in range(ENS):
            pair = jnp.zeros((16, 128), F32)
            for b in range(ENS):
                if b != a:
                    pair = pair + soft_sign(u[a] - u[b])
                pair = pair + soft_sign(u[a] - w[b])
            grads[a, at, :] = (soft_sign(u[a] - goal) / 16.0 - pair / 240.0).astype(BF)
        return carry

    lax.fori_loop(0, PART // 16, step, 0)
    x3 = Exchange(
        "ens", ENS, em, lambda p: grads.at[p], lambda m: piece(gback, m),
        grads.at[pl.ds(0, ENS - 1)], gback.at[pl.ds(0, (ENS - 1) * PART)], sems3,
    )
    x3.start()
    piece(gback, em)[...] = grads[em]
    x3.arrived()

    for ml in range(ORDERS):
        s = jnp.dot(leg[ml], gback[ml * L : (ml + 1) * L, :], preferred_element_type=F32)
        for j in range(ROWS):
            rows[:, ml * 6 + j, :] = s[j * 32 : (j + 1) * 32, :]
    send4[...] = rows[...].astype(BF)
    x4 = Exchange(
        "lat", BANDS, me, lambda p: send4.at[p], lambda m: recv4.at[m],
        send4.at[pl.ds(0, BANDS - 1)], recv4.at[pl.ds(0, BANDS - 1)], sems4,
    )
    x4.start()
    recv4[me] = send4[me]
    for ml in range(ORDERS):
        o = jnp.dot(chosen[...], gback[ml * L : (ml + 1) * L, :], preferred_element_type=F32)
        for j in range(5):
            rows[:, ml * 5 + j, :] = o[j * 32 : (j + 1) * 32, :]
    send5[...] = rows[...].astype(BF)
    x5 = Exchange(
        "lat", BANDS, me, lambda p: send5.at[p], lambda m: recv5.at[m],
        send5.at[pl.ds(0, BANDS - 1)], recv5.at[pl.ds(0, BANDS - 1)], sems5,
    )
    x5.start()
    recv5[me] = send5[me]

    x4.arrived()
    rows[...] = jnp.dot(
        recv4[...].reshape(BANDS * 32, 128), mixing[...], preferred_element_type=F32
    ).reshape(BANDS, 32, 128)
    for i in range(ROWS):
        j = (i % 2) * 3 + i // 2
        q = jnp.concatenate([rows[:, ml * 6 + j, :] for ml in range(ORDERS)], axis=0)
        qt = q.T
        for r in range(2):
            for k in range(2):
                left[r, k, i * 24 : (i + 1) * 24, :] = qt[r * 64 + k * 24 : r * 64 + k * 24 + 24, :]
    halos2 = []
    for k in range(2):
        grad = jnp.dot(left[0, k].astype(BF), table[0:M, :], preferred_element_type=F32)
        grad = grad + jnp.dot(left[1, k].astype(BF), table[M:, :], preferred_element_type=F32)
        for h in range(2):
            hid[k, h] = (grad[h * 72 : (h + 1) * 72] * slope[k, h].astype(F32)).astype(BF)
        pair = halo(hid, low2, high2, halo2_sems, k)
        for copy in pair:
            copy.start()
        halos2.append(pair)

    x5.arrived()
    rows[...] = recv5[...].astype(F32)
    for j in range(5):
        for ml in range(ORDERS):
            turn[pl.ds(ml, BANDS, stride=ORDERS), :] = rows[:, ml * 5 + j, :]
        qt = turn[...].T
        for r in range(2):
            for k in range(2):
                score[k, :, j, r, :] = qt[r * 64 + k * 24 : r * 64 + k * 24 + 24, :]

    for k in range(2):
        ext[0:72, :] = wrapped(hid[k, 0])
        ext[72:144, :] = wrapped(hid[k, 1])
        for h in range(2):
            halos2[k][h].wait_recv()
            fill_halo(low2, high2, k, h)
            out[k, h] = (hid[k, h].astype(F32) + conv_half(flipped, ext, prod, h)).astype(BF)

    for pairs in (halos, halos2):
        for pair in pairs:
            for copy in pair:
                copy.wait_send()
    for exchange in (legx, x1, x2, x3, x4, x5):
        exchange.done()


HALF = (2, 2, 72, NLON)
CHUNK = (BANDS, 32, 128)


def whole(*args):
    spec = pl.BlockSpec(memory_space=pltpu.VMEM)
    pair = pltpu.SemaphoreType.DMA((2,))
    scratch = [
        ((2, 72, NLON), BF), ((2, 72, NLON), BF), ((2, 72, NLON), BF), ((2, 72, NLON), BF),
        ((2, 504, 216), BF), ((2, 504, 216), BF), ((504, 216), F32),
        ((216, 1536), BF), ((504, 1536), F32), ((144, NLON), BF), (HALF, BF), (HALF, BF),
        ((2, M, 128), F32), ((BANDS, 2, 32, 128), BF), ((BANDS, 2, 32, 128), BF), ((ORDERS, 192, L), BF),
        (CHUNK, F32), ((2,) + CHUNK, F32), (CHUNK, BF), (CHUNK, BF),
        ((896, 128), BF), ((ENS, PART, 128), BF), ((ENS, PART, 128), BF), ((896, 128), BF),
        (CHUNK, BF), (CHUNK, BF), (CHUNK, BF), (CHUNK, BF),
        ((2, 2, 144, M), F32), ((M, 128), F32),
    ]
    return pl.pallas_call(
        kernel,
        out_shape=[
            jax.ShapeDtypeStruct(HALF, BF),
            jax.ShapeDtypeStruct((2, C, 5, 2, M), F32),
        ],
        in_specs=[spec] * len(args),
        out_specs=[spec, spec],
        scratch_shapes=[pltpu.VMEM(s, d) for s, d in scratch]
        + [pltpu.SemaphoreType.DMA((4, 2))] * 2
        + [pair] * 6,
        compiler_params=pltpu.CompilerParams(
            vmem_limit_bytes=52 << 20, collective_id=0, has_side_effects=True
        ),
    )(*args)


def local(fields, depth_kernel, mix_weight, legendre, truth, degree_order):
    table = jnp.asarray(wave_table())
    x = jnp.transpose(fields, (0, 2, 1, 3)).reshape(HALF)
    block = jnp.transpose(mix_weight)
    placing = jnp.stack(
        [
            jnp.kron(jnp.eye(ROWS, dtype=BF), jnp.pad(block, ((0, 0), (24 * k, 40 - 24 * k))))
            for k in range(2)
        ]
    )
    mixing = jnp.kron(
        jnp.eye(2, dtype=BF),
        jnp.pad(jnp.kron(jnp.eye(2, dtype=BF), mix_weight), ((0, 16), (0, 16))),
    )
    lanes = np.arange(128)
    spot = (
        (lanes[None, None, :] // 64 == np.arange(2)[None, :, None])
        & (lanes[None, None, :] % 64 < 48)
        & (lanes[None, None, :] % 64 % 24 == np.arange(C)[:, None, None])
    )
    mine = lax.dynamic_slice_in_dim(truth, lax.axis_index("lat") * ORDERS, ORDERS, 2)
    target = jnp.einsum(
        "crml,crn->mln", mine, jnp.asarray(spot, BF), preferred_element_type=F32
    ).astype(BF)
    target = jnp.pad(target.reshape(800, 128), ((0, 96), (0, 0)))
    target = lax.dynamic_slice_in_dim(target, lax.axis_index("ens") * PART, PART, 0)
    place = degree_order.reshape(BANDS, 5).T.reshape(L)
    chosen = (place[:, None] == jnp.arange(L, dtype=jnp.int32)[None, :]).astype(BF)
    cols = jnp.transpose(depth_kernel, (2, 0, 1))
    out, score = whole(x, legendre, cols, table, placing, mixing, target, chosen)
    grad_fields = jnp.transpose(out.reshape(2, ROWS, C, NLON), (0, 2, 1, 3))
    return grad_fields, jnp.transpose(score, (0, 1, 3, 4, 2))


def solution(mesh):
    placed = (P("ens", None, "lat", None), P(), P(), P("lat", None, None), P(), P())
    return jax.shard_map(
        local,
        mesh=mesh,
        in_specs=placed,
        out_specs=(P("ens", None, "lat", None), P("ens", None, None, None, "lat")),
        check_vma=False,
    )
```

time: 140 us -> 97.5 us (0.70); the launches traced: 137 us -> 97 us
  Pallas kernels: 19.9 us -> 85.8 us
  starting transfers between devices: 51.7 us -> 0 us
  waiting for transfers between devices: 33.5 us -> 0 us
  local copies, waits for them, and re-layouts: 24.8 us -> 8.35 us
  other arithmetic: 6.01 us -> 1.16 us
    pallas_call x6 -> x1, Pallas kernels: 19.9 us -> 85.8 us  [whole(): pl.pallas_call(kernel, out_shape=[jax.ShapeDtypeStruct(HALF, BF), jax.Sha...]
    all_to_all x6 -> x0, starting transfers between devices: 41.9 us -> none  [swap(): return lax.all_to_all(x, axis, split_axis=0, concat_axis=0, tiled=True)]
    all_to_all x6 -> x0, waiting for transfers between devices: 33.5 us -> none  [swap(): return lax.all_to_all(x, axis, split_axis=0, concat_axis=0, tiled=True)]
    ppermute x4 -> x0, starting transfers between devices: 9.77 us -> none  [the longest x2 7.19 us: edges(): low = lax.ppermute(x[:, 72:], 'lat', up)]
    convert_element_type x4 -> x0, local copies, waits for them, and re-layouts: 6.31 us -> none  [the longest x2 6.1 us: local(): return (grad_fields, score.reshape(2, C, 2, M, 5).astype(F32))]
    slice x4 -> x0, local copies, waits for them, and re-layouts: 3.96 us -> none  [the longest x2 3.27 us: edges(): high = lax.ppermute(x[:, :72], 'lat', [(b, a) for a, b in up])]
    select_n x2 -> x0, other arithmetic: 3.34 us -> none  [banded(): total = jnp.where(same & (gap == p), cols[:, p:p + 1], total)]
    reshape x2 -> x0, local copies, waits for them, and re-layouts: 2.68 us -> none  [the longest x1 2.48 us: local(): leg = legendre.reshape(3, 2, BANDS, ORDERS, L).transpose(2, 3, 1, 0, 4)]
  transfers between devices with their start and end apart: 10 -> 0, of which waited for: 6 -> 0; matrix products, arithmetic and copies ran while one was open for 20% -> 0% of each run, Pallas kernels for 6% -> 0%
where the time goes in v3:
time: 97.5 us; the launch traced here: 97 us
  Pallas kernels  85.8 us (88%)
  local copies, waits for them, and re-layouts  8.35 us (9%)
  other arithmetic  1.16 us (1%)
    pallas_call x1, Pallas kernels, whole(): pl.pallas_call(kernel, out_shape=[jax.ShapeDtypeStruct(HALF, BF), jax.Sha...  85.8 us
    unnamed x6, local copies, waits for them, and re-layouts  5.57 us

profile of v3, /device:TPU:1, one launch (start us, length us, event | category | flops | bytes accessed | tf_op | source)
XLA Modules:
  0.0 97.0 jit_solution(14250268956466530182)
XLA Ops:
  0.7 0.8 copy.21
  1.4 0.1 fusion.4
  1.5 0.8 reshape.98
  2.3 0.1 copy.18
  2.4 0.1 eq.37
  2.5 0.8 broadcast_multiply_fusion.3
  3.2 0.1 mul.118
  3.3 0.1 broadcast_multiply_fusion.2
  3.5 0.1 mul.121.mixing
  3.6 0.1 fusion.1.chosen
  3.7 0.9 copy.14
  4.5 1.1 %constant_dynamic-slice_fusion = bf16[24,2,5,160]{3,2,1,0:T(8,128)(2,1)S(1)} fusion(bf16[24,2,160,160]{3,2,1,0:T(8,128)(2,1)} %param.12, s32[]{:T(128)S(6)} %select_n.6), kind=kLoop, calls=%fused_computation.14 | loop fusion | bytes 153604 | tf_op jit(solution)/shard_map/dynamic_slice | solution.py:404
  5.6 1.0 fusion
  6.6 0.1 pad_dynamic-slice_fusion.target
  6.6 0.1 broadcast_multiply_fusion.1
  6.8 0.2 mul.110
  7.0 0.2 mul.113
  7.2 0.0 copy-start
  7.3 1.0 %copy-done = bf16[6,160,160]{2,1,0:T(8,128)(2,1)S(1)} copy-done((bf16[6,160,160]{2,1,0:T(8,128)(2,1)S(1)}, bf16[6,160,160]{2,1,0:T(8,128)(2,1)}, u32[]{:S(2)}) %copy-start) | copy-done | bytes 307224
  8.3 85.8 %shard_map.95 = (bf16[2,2,72,1440]{3,2,1,0:T(8,128)(2,1)}, f32[2,24,5,2,160]{4,3,2,1,0:T(2,128)S(1)}) custom-call(bf16[2,2,72,1440]{3,2,1,0:T(8,128)(2,1)} %bitcast.20, bf16[6,160,160]{2,1,0:T(8,128)(2,1)S(1)} %copy-done, f32[7,24,7]{2,1,0:T(8,128)S(1)} %bitcast.19, bf16[320,1440]{1,0:T(8,128)(2,1)} %constant.25.clone.table, ...), custom_call_target="tpu_custom_call" | custom-call | tf_op jit(solution)/shard_map/pallas_call | solution.py:367
  94.1 2.1 %copy.27 = bf16[2,24,6,1440]{3,1,2,0:T(8,128)(2,1)} copy(bf16[2,24,6,1440]{3,1,2,0:T(8,128)(2,1)} %bitcast.21) | data formatting | bytes 1658880
  96.3 0.8 copy.28
  (4 shorter events, 0.1 us)
Async XLA Ops:
  7.2 1.0 %copy-start = (bf16[6,160,160]{2,1,0:T(8,128)(2,1)S(1)}, bf16[6,160,160]{2,1,0:T(8,128)(2,1)}, u32[]{:S(2)}) copy-start(bf16[6,160,160]{2,1,0:T(8,128)(2,1)} %legl.1) | copy-start | bytes 921604

commit v4 on v3

--- a/solution.py
+++ b/solution.py
@@ -34,24 +34,65 @@
     return jnp.concatenate([x[:, NLON - 3 :], x, x[:, :93]], axis=1)
 
 
-def spread_weights(cols, dst, tmp, flip):
-    lane = lax.broadcasted_iota(jnp.int32, (C, 216), 1)
-    same = lane % C == lax.broadcasted_iota(jnp.int32, (C, 216), 0)
+def iota(shape, axis):
+    return lax.broadcasted_iota(jnp.int32, shape, axis)
+
+
+def onehot(hit):
+    return jnp.where(hit, 1.0, 0.0).astype(BF)
+
+
+def tile_taps(kern, taps):
+    again = onehot(iota((C, 216), 1) % C == iota((C, 216), 0))
+    for p in range(7):
+        taps[p] = jnp.dot(kern[p].astype(BF), again, preferred_element_type=F32)
+
+
+def spread_weights(taps, dst, tmp, flip):
+    lane = iota((C, 216), 1)
+    same = lane % C == iota((C, 216), 0)
     for h in range(2):
         row = lane // C
         window = lax.rem(row + 3, 9) if h == 0 else row
         masks = [same & (window == g) for g in range(9)]
         for q in range(7):
-            taps = []
+            tap = []
             for p in range(7):
-                a, b = (6 - q, 6 - p) if flip else (q, p)
-                taps.append(jnp.broadcast_to(cols[a, :, b : b + 1], (C, 216)))
+                a, b = (6 - p, 6 - q) if flip else (p, q)
+                tap.append(jnp.broadcast_to(taps[a, b : b + 1, :], (C, 216)))
             for i in range(3):
                 total = jnp.zeros((C, 216), F32)
                 for p in range(7):
-                    total = jnp.where(masks[i + p], taps[p], total)
+                    total = jnp.where(masks[i + p], tap[p], total)
                 tmp[q * 72 + i * 24 : q * 72 + i * 24 + 24, :] = total
         dst[h] = tmp[...].astype(BF)
+
+
+def place_mix(mix, placing):
+    row = iota((144, C), 0)
+    tall = lax.dot_general(
+        onehot(row % C == iota((144, C), 1)), mix[...], (((1,), (1,)), ((), ())),
+        preferred_element_type=F32,
+    ).astype(BF)
+    for k in range(2):
+        wide = onehot(iota((C, 384), 1) % 64 == iota((C, 384), 0) + C * k)
+        full = jnp.dot(tall, wide, preferred_element_type=F32)
+        same = iota((144, 384), 0) // C == iota((144, 384), 1) // 64
+        placing[k] = jnp.where(same, full, 0.0).astype(BF)
+
+
+def group(v):
+    return v // 64 * 2 + v % 64 // C, v % 64 % C
+
+
+def mix_lanes(mix):
+    rk, o = group(iota((128, C), 0))
+    tall = jnp.dot(onehot(o == iota((128, C), 1)), mix[...], preferred_element_type=F32).astype(BF)
+    rk, c = group(iota((C, 128), 1))
+    full = jnp.dot(tall, onehot(c == iota((C, 128), 0)), preferred_element_type=F32)
+    a, b = iota((128, 128), 0), iota((128, 128), 1)
+    same = (group(a)[0] == group(b)[0]) & (a % 64 < 48) & (b % 64 < 48)
+    return jnp.where(same, full, 0.0).astype(BF)
 
 
 def conv_half(weights, ext, prod, h):
@@ -101,19 +142,35 @@
 
 
 def kernel(
-    x, legl, cols, table, placing, mixing, target, chosen,
+    x_hbm, leg_hbm, kern, table_hbm, mix, truth, order,
     out, score,
+    x, legl, table, window, wide, taps, placing, target, chosen,
     low, high, low2, high2, weights, flipped, wtmp, ext, prod, act, slope, hid,
-    legf, legsend, legrecv, leg,
-    rows, more, send1, recv1, coeff, pooled, grads, gback, send4, recv4, send5, recv5,
+    legf, legsend, legrecv, legall, leg,
+    rows, stage, more, send1, recv1, coeff, pooled, grads, gback, send4, recv4, send5, recv5,
     left, turn,
-    halo_sems, halo2_sems, leg_sems, sems1, sems2, sems3, sems4, sems5,
+    load_sems, halo_sems, halo2_sems, leg_sems, leg2_sems, sems1, sems2, sems3, sems4, sems5,
 ):
     me = lax.axis_index("lat")
     em = lax.axis_index("ens")
     after = lax.rem(me + 1, BANDS)
     before = lax.rem(me + BANDS - 1, BANDS)
 
+    m0 = me * ORDERS
+    base = jnp.minimum(m0 // 8 * 8, M - 16)
+    loads = [
+        pltpu.make_async_copy(source, target_, load_sems.at[n])
+        for n, (source, target_) in enumerate(
+            [
+                (leg_hbm, legl),
+                (x_hbm, x),
+                (truth.at[:, :, pl.ds(pl.multiple_of(base, 8), 16), :], window),
+                (table_hbm, table),
+            ]
+        )
+    ]
+    for load in loads:
+        load.start()
     barrier = pltpu.get_barrier_semaphore()
 
     def greet(axis, count, mine):
@@ -143,30 +200,33 @@
             ),
         )
 
-    halos = [halo(x, low, high, halo_sems, k) for k in range(2)]
+    halos = [halo(x_hbm, low, high, halo_sems, k) for k in range(2)]
     for pair in halos:
         for copy in pair:
             copy.start()
 
+    loads[0].wait()
     for i in range(ROWS):
-        j = (i % 2) * 3 + i // 2
-        legf[0] = legl[i, :, 0:128].astype(F32)
-        legf[1] = jnp.concatenate(
+        legf[0, i] = legl[i, :, 0:128].astype(F32)
+        legf[1, i] = jnp.concatenate(
             [legl[i, :, 128:L].astype(F32), jnp.zeros((M, 256 - L), F32)], axis=1
         )
-        for ml in range(ORDERS):
-            for b in range(2):
-                more[b, :, ml * 6 + j, :] = legf[b, pl.ds(ml, BANDS, stride=ORDERS), :]
-    for b in range(2):
-        more[b, :, 30:32, :] = jnp.zeros((BANDS, 2, 128), F32)
-        legsend[:, b] = more[b].astype(BF)
+    for q in range(4):
+        n = jnp.minimum(em * 4 + q, 29)
+        for b in range(2):
+            stage[:, q * 2 + b, :] = legf[
+                b, n // ORDERS, pl.ds(lax.rem(n, ORDERS), BANDS, stride=ORDERS), :
+            ]
+    legsend[...] = stage[...].astype(BF)
     legx = Exchange(
         "lat", BANDS, me, lambda p: legsend.at[p], lambda m: legrecv.at[m],
         legsend.at[pl.ds(0, BANDS - 1)], legrecv.at[pl.ds(0, BANDS - 1)], leg_sems,
     )
     legx.start()
     legrecv[me] = legsend[me]
-    spread_weights(cols, weights, wtmp, False)
+    tile_taps(kern, taps)
+    spread_weights(taps, weights, wtmp, False)
+    place_mix(mix, placing)
 
     def fill_halo(lo, hi, k, h):
         if h == 0:
@@ -176,6 +236,8 @@
             edge = wrapped(hi[k].astype(F32))
             ext[144:216, :] = jnp.where(me < BANDS - 1, edge, 0.0).astype(BF)
 
+    loads[1].wait()
+    loads[3].wait()
     c0 = math.sqrt(2.0 / math.pi)
     spec = jnp.zeros((2 * M, 384), F32)
     for k in range(2):
@@ -194,6 +256,14 @@
             table[...], act[...], (((1,), (1,)), ((), ())), preferred_element_type=F32
         ).astype(BF)
         spec = spec + jnp.dot(waves, placing[k], preferred_element_type=F32)
+        if k == 0:
+            legx.arrived()
+            legx2 = Exchange(
+                "ens", ENS, em, lambda p: legrecv, lambda m: legall.at[m],
+                legall.at[pl.ds(0, ENS - 1)], legall.at[pl.ds(0, ENS - 1)], leg2_sems,
+            )
+            legx2.start()
+            legall[em] = legrecv[...]
     rows[:, 30:32, :] = jnp.zeros((BANDS, 2, 128), F32)
     for a in range(10):
         for t in range(3):
@@ -206,14 +276,41 @@
     x1.start()
     recv1[me] = send1[me]
 
-    legx.arrived()
-    for b in range(2):
-        more[b] = legrecv[:, b].astype(F32)
+    loads[2].wait()
+    wide[0] = window[:, :, :, 0:128].astype(F32).reshape(2 * C, 16, 128)
+    wide[1] = jnp.concatenate(
+        [
+            window[:, :, :, 128:L].astype(F32).reshape(2 * C, 16, L - 128),
+            jnp.zeros((2 * C, 16, 256 - L), F32),
+        ],
+        axis=2,
+    )
+    cr, at = iota((2 * C, 128), 0), iota((2 * C, 128), 1)
+    spot = onehot((at // 64 == cr % 2) & (at % 64 < 48) & (at % 64 % C == cr // 2))
     for ml in range(ORDERS):
-        for j in range(ROWS):
+        for b in range(2):
+            part = wide[b, :, m0 - base + ml, :].astype(BF)
+            t = lax.dot_general(part, spot, (((0,), (0,)), ((), ())), preferred_element_type=F32)
+            if b == 0:
+                target[ml * L : ml * L + 128, :] = t.astype(BF)
+            else:
+                target[ml * L + 128 : ml * L + L, :] = t[0 : L - 128].astype(BF)
+    target[800:896, :] = jnp.zeros((96, 128), BF)
+    place = iota((L, L), 0)
+    spots = onehot(iota((L, L), 1) == place % BANDS * 5 + place // BANDS)
+    kept = onehot(place == jnp.broadcast_to(order[...], (L, L)))
+    chosen[...] = lax.dot_general(
+        spots, kept, (((1,), (1,)), ((), ())), preferred_element_type=F32
+    ).astype(BF)
+
+    legx2.arrived()
+    more[...] = legall[...].astype(F32)
+    for ml in range(ORDERS):
+        for i in range(ROWS):
+            n, j = i * ORDERS + ml, (i % 2) * 3 + i // 2
             at = slice(j * 32, (j + 1) * 32)
-            leg[ml, at, 0:128] = more[0, :, ml * 6 + j, :].astype(BF)
-            leg[ml, at, 128:L] = more[1, :, ml * 6 + j, 0 : L - 128].astype(BF)
+            leg[ml, at, 0:128] = more[n // 4, :, n % 4 * 2, :].astype(BF)
+            leg[ml, at, 128:L] = more[n // 4, :, n % 4 * 2 + 1, 0 : L - 128].astype(BF)
 
     x1.arrived()
     rows[...] = recv1[...].astype(F32)
@@ -247,24 +344,32 @@
     )
     x2.start()
     pooled[em] = piece(coeff, em)[...]
-    spread_weights(cols, flipped, wtmp, True)
+    spread_weights(taps, flipped, wtmp, True)
     x2.arrived()
 
     small = lax.broadcasted_iota(jnp.int32, (16, 128), 1) % 64
+
+    def other(v):
+        return jnp.where(small < 24, pltpu.roll(v, 104, 1), pltpu.roll(v, 24, 1))
 
     def step(s, carry):
         at = pl.ds(pl.multiple_of(s * 16, 16), 16)
         u = [pooled[a, at, :].astype(F32) for a in range(ENS)]
-        w = [jnp.where(small < 24, pltpu.roll(v, 104, 1), pltpu.roll(v, 24, 1)) for v in u]
-        w = [jnp.where(small < 48, v, 0.0) for v in w]
-        goal = target[at, :].astype(F32)
+        w = [jnp.where(small < 48, other(v), 0.0) for v in u]
+        goal = target[pl.ds(pl.multiple_of(em * PART + s * 16, 16), 16), :].astype(F32)
+        plus = [jnp.zeros((16, 128), F32)] * ENS
+        for b in range(ENS):
+            turned = jnp.zeros((16, 128), F32)
+            for a in range(b):
+                one = soft_sign(u[a] - u[b])
+                two = soft_sign(u[a] - w[b])
+                plus[a] = plus[a] + (one + two)
+                plus[b] = plus[b] - one
+                turned = turned + two
+            plus[b] = plus[b] + soft_sign(u[b] - w[b])
+            plus[b] = plus[b] - jnp.where(small < 48, other(turned), 0.0)
         for a in range(ENS):
-            pair = jnp.zeros((16, 128), F32)
-            for b in range(ENS):
-                if b != a:
-                    pair = pair + soft_sign(u[a] - u[b])
-                pair = pair + soft_sign(u[a] - w[b])
-            grads[a, at, :] = (soft_sign(u[a] - goal) / 16.0 - pair / 240.0).astype(BF)
+            grads[a, at, :] = (soft_sign(u[a] - goal) / 16.0 - plus[a] / 240.0).astype(BF)
         return carry
 
     lax.fori_loop(0, PART // 16, step, 0)
@@ -274,6 +379,7 @@
     )
     x3.start()
     piece(gback, em)[...] = grads[em]
+    mixing = mix_lanes(mix)
     x3.arrived()
 
     for ml in range(ORDERS):
@@ -296,12 +402,12 @@
         "lat", BANDS, me, lambda p: send5.at[p], lambda m: recv5.at[m],
         send5.at[pl.ds(0, BANDS - 1)], recv5.at[pl.ds(0, BANDS - 1)], sems5,
     )
+    recv5[me] = send5[me]
+
+    x4.arrived()
     x5.start()
-    recv5[me] = send5[me]
-
-    x4.arrived()
     rows[...] = jnp.dot(
-        recv4[...].reshape(BANDS * 32, 128), mixing[...], preferred_element_type=F32
+        recv4[...].reshape(BANDS * 32, 128), mixing, preferred_element_type=F32
     ).reshape(BANDS, 32, 128)
     for i in range(ROWS):
         j = (i % 2) * 3 + i // 2
@@ -343,7 +449,7 @@
         for pair in pairs:
             for copy in pair:
                 copy.wait_send()
-    for exchange in (legx, x1, x2, x3, x4, x5):
+    for exchange in (legx, legx2, x1, x2, x3, x4, x5):
         exchange.done()
 
 
@@ -352,14 +458,21 @@
 
 
 def whole(*args):
-    spec = pl.BlockSpec(memory_space=pltpu.VMEM)
+    vmem = pl.BlockSpec(memory_space=pltpu.VMEM)
+    far = pl.BlockSpec(memory_space=pl.ANY)
     pair = pltpu.SemaphoreType.DMA((2,))
+    halo = (2, 72, NLON)
+    eighth = (BANDS, 8, 128)
     scratch = [
-        ((2, 72, NLON), BF), ((2, 72, NLON), BF), ((2, 72, NLON), BF), ((2, 72, NLON), BF),
+        (HALF, BF), ((ROWS, M, L), BF), ((2 * M, NLON), BF), ((C, 2, 16, L), BF),
+        ((2, 2 * C, 16, 128), F32), ((7, 7, 216), F32), ((2, 144, 384), BF), ((896, 128), BF),
+        ((L, L), BF),
+        (halo, BF), (halo, BF), (halo, BF), (halo, BF),
         ((2, 504, 216), BF), ((2, 504, 216), BF), ((504, 216), F32),
         ((216, 1536), BF), ((504, 1536), F32), ((144, NLON), BF), (HALF, BF), (HALF, BF),
-        ((2, M, 128), F32), ((BANDS, 2, 32, 128), BF), ((BANDS, 2, 32, 128), BF), ((ORDERS, 192, L), BF),
-        (CHUNK, F32), ((2,) + CHUNK, F32), (CHUNK, BF), (CHUNK, BF),
+        ((2, ROWS, M, 128), F32), (eighth, BF), (eighth, BF), ((ENS,) + eighth, BF),
+        ((ORDERS, 192, L), BF),
+        (CHUNK, F32), (eighth, F32), ((ENS,) + eighth, F32), (CHUNK, BF), (CHUNK, BF),
         ((896, 128), BF), ((ENS, PART, 128), BF), ((ENS, PART, 128), BF), ((896, 128), BF),
         (CHUNK, BF), (CHUNK, BF), (CHUNK, BF), (CHUNK, BF),
         ((2, 2, 144, M), F32), ((M, 128), F32),
@@ -370,11 +483,12 @@
             jax.ShapeDtypeStruct(HALF, BF),
             jax.ShapeDtypeStruct((2, C, 5, 2, M), F32),
         ],
-        in_specs=[spec] * len(args),
-        out_specs=[spec, spec],
+        in_specs=[far, far, vmem, far, vmem, far, vmem],
+        out_specs=[vmem, vmem],
         scratch_shapes=[pltpu.VMEM(s, d) for s, d in scratch]
+        + [pltpu.SemaphoreType.DMA((4,))]
         + [pltpu.SemaphoreType.DMA((4, 2))] * 2
-        + [pair] * 6,
+        + [pair] * 7,
         compiler_params=pltpu.CompilerParams(
             vmem_limit_bytes=52 << 20, collective_id=0, has_side_effects=True
         ),
@@ -384,33 +498,8 @@
 def local(fields, depth_kernel, mix_weight, legendre, truth, degree_order):
     table = jnp.asarray(wave_table())
     x = jnp.transpose(fields, (0, 2, 1, 3)).reshape(HALF)
-    block = jnp.transpose(mix_weight)
-    placing = jnp.stack(
-        [
-            jnp.kron(jnp.eye(ROWS, dtype=BF), jnp.pad(block, ((0, 0), (24 * k, 40 - 24 * k))))
-            for k in range(2)
-        ]
-    )
-    mixing = jnp.kron(
-        jnp.eye(2, dtype=BF),
-        jnp.pad(jnp.kron(jnp.eye(2, dtype=BF), mix_weight), ((0, 16), (0, 16))),
-    )
-    lanes = np.arange(128)
-    spot = (
-        (lanes[None, None, :] // 64 == np.arange(2)[None, :, None])
-        & (lanes[None, None, :] % 64 < 48)
-        & (lanes[None, None, :] % 64 % 24 == np.arange(C)[:, None, None])
-    )
-    mine = lax.dynamic_slice_in_dim(truth, lax.axis_index("lat") * ORDERS, ORDERS, 2)
-    target = jnp.einsum(
-        "crml,crn->mln", mine, jnp.asarray(spot, BF), preferred_element_type=F32
-    ).astype(BF)
-    target = jnp.pad(target.reshape(800, 128), ((0, 96), (0, 0)))
-    target = lax.dynamic_slice_in_dim(target, lax.axis_index("ens") * PART, PART, 0)
-    place = degree_order.reshape(BANDS, 5).T.reshape(L)
-    chosen = (place[:, None] == jnp.arange(L, dtype=jnp.int32)[None, :]).astype(BF)
-    cols = jnp.transpose(depth_kernel, (2, 0, 1))
-    out, score = whole(x, legendre, cols, table, placing, mixing, target, chosen)
+    kern = jnp.transpose(depth_kernel, (1, 2, 0))
+    out, score = whole(x, legendre, kern, table, mix_weight, truth, degree_order.reshape(1, L))
     grad_fields = jnp.transpose(out.reshape(2, ROWS, C, NLON), (0, 2, 1, 3))
     return grad_fields, jnp.transpose(score, (0, 1, 3, 4, 2))
 

time: 97.5 us -> 86.1 us (0.88)
  Pallas kernels: 85.8 us -> 80.4 us
  local copies, waits for them, and re-layouts: 8.35 us -> 4.83 us
  other arithmetic: 1.16 us -> 0 us
    pallas_call x1, Pallas kernels: 85.8 us -> 80.4 us  [whole(): pl.pallas_call(kernel, out_shape=[jax.ShapeDtypeStruct(HALF, BF), jax.Sha...]
    dynamic_slice x2 -> x0, local copies, waits for them, and re-layouts: 1.12 us -> none  [the longest x1 1.07 us: local(): lax.dynamic_slice_in_dim(truth, lax.axis_index('lat') * ORDERS, ORDERS, 2)]
    mul x3 -> x0, other arithmetic: 1.03 us -> none  [the longest x1 0.79 us: local(): jnp.kron(jnp.eye(2, dtype=BF), mix_weight)]
    unnamed x6 -> x10, local copies, waits for them, and re-layouts: 5.57 us -> 4.83 us
where the time goes in v4:
time: 86.1 us; the launch traced here: 85.8 us
  Pallas kernels  80.4 us (93%)
  local copies, waits for them, and re-layouts  4.83 us (6%)
    pallas_call x1, Pallas kernels, whole(): pl.pallas_call(kernel, out_shape=[jax.ShapeDtypeStruct(HALF, BF), jax.Sha...  80.4 us
    unnamed x10, local copies, waits for them, and re-layouts  4.83 us

profile of v4, /device:TPU:1, one launch (start us, length us, event | category | flops | bytes accessed | tf_op | source)
XLA Modules:
  0.0 85.8 jit_solution(2809524350458454498)
XLA Ops:
  0.6 0.0 copy-start
  0.6 1.0 %copy-done = bf16[6,160,160]{2,1,0:T(8,128)(2,1)S(1)} copy-done((bf16[6,160,160]{2,1,0:T(8,128)(2,1)S(1)}, bf16[6,160,160]{2,1,0:T(8,128)(2,1)}, u32[]{:S(2)}) %copy-start) | copy-done | bytes 307224
  1.7 0.0 copy-start.1
  1.7 0.7 copy-done.1
  2.4 0.0 copy-start.2
  2.4 0.7 copy-done.2
  3.1 0.0 copy-start.3
  3.1 0.7 copy-done.3
  3.8 80.4 %shard_map.86 = (bf16[2,2,72,1440]{3,2,1,0:T(8,128)(2,1)S(1)}, f32[2,24,5,2,160]{4,3,2,1,0:T(2,128)S(1)}) custom-call(bf16[2,2,72,1440]{3,2,1,0:T(8,128)(2,1)} %bitcast.13, bf16[6,160,160]{2,1,0:T(8,128)(2,1)S(1)} %copy-done, f32[7,7,24]{2,1,0:T(8,128)S(1)} %bitcast.11, bf16[320,1440]{1,0:T(8,128)(2,1)} %constant.2.clone.table_hbm, ...), custom_call_target="tpu_custom_call" | custom-call | tf_op jit(solution)/shard_map/pallas_call | solution.py:480
  84.1 0.9 %copy.11 = bf16[2,24,6,1440]{3,1,2,0:T(8,128)(2,1)} copy(bf16[2,24,6,1440]{3,1,2,0:T(8,128)(2,1)S(1)} %bitcast.9) | data formatting | bytes 1658880
  85.1 0.8 copy.12
Async XLA Ops:
  0.6 1.0 %copy-start = (bf16[6,160,160]{2,1,0:T(8,128)(2,1)S(1)}, bf16[6,160,160]{2,1,0:T(8,128)(2,1)}, u32[]{:S(2)}) copy-start(bf16[6,160,160]{2,1,0:T(8,128)(2,1)} %leg_hbm.1) | copy-start | bytes 921604
  1.7 0.7 copy-start.1
  2.4 0.7 copy-start.2
  3.1 0.7 copy-start.3

commit v5 on v4

--- a/solution.py
+++ b/solution.py
@@ -142,9 +142,9 @@
 
 
 def kernel(
-    x_hbm, leg_hbm, kern, table_hbm, mix, truth, order,
+    x_hbm, leg_hbm, kern_hbm, table_hbm, mix_hbm, truth, order_hbm,
     out, score,
-    x, legl, table, window, wide, taps, placing, target, chosen,
+    x, legl, table, kern, mix, order, window, wide, taps, placing, target, chosen,
     low, high, low2, high2, weights, flipped, wtmp, ext, prod, act, slope, hid,
     legf, legsend, legrecv, legall, leg,
     rows, stage, more, send1, recv1, coeff, pooled, grads, gback, send4, recv4, send5, recv5,
@@ -166,6 +166,9 @@
                 (x_hbm, x),
                 (truth.at[:, :, pl.ds(pl.multiple_of(base, 8), 16), :], window),
                 (table_hbm, table),
+                (kern_hbm, kern),
+                (mix_hbm, mix),
+                (order_hbm, order),
             ]
         )
     ]
@@ -224,8 +227,10 @@
     )
     legx.start()
     legrecv[me] = legsend[me]
+    loads[4].wait()
     tile_taps(kern, taps)
     spread_weights(taps, weights, wtmp, False)
+    loads[5].wait()
     place_mix(mix, placing)
 
     def fill_halo(lo, hi, k, h):
@@ -298,6 +303,7 @@
     target[800:896, :] = jnp.zeros((96, 128), BF)
     place = iota((L, L), 0)
     spots = onehot(iota((L, L), 1) == place % BANDS * 5 + place // BANDS)
+    loads[6].wait()
     kept = onehot(place == jnp.broadcast_to(order[...], (L, L)))
     chosen[...] = lax.dot_general(
         spots, kept, (((1,), (1,)), ((), ())), preferred_element_type=F32
@@ -427,16 +433,6 @@
             copy.start()
         halos2.append(pair)
 
-    x5.arrived()
-    rows[...] = recv5[...].astype(F32)
-    for j in range(5):
-        for ml in range(ORDERS):
-            turn[pl.ds(ml, BANDS, stride=ORDERS), :] = rows[:, ml * 5 + j, :]
-        qt = turn[...].T
-        for r in range(2):
-            for k in range(2):
-                score[k, :, j, r, :] = qt[r * 64 + k * 24 : r * 64 + k * 24 + 24, :]
-
     for k in range(2):
         ext[0:72, :] = wrapped(hid[k, 0])
         ext[72:144, :] = wrapped(hid[k, 1])
@@ -444,6 +440,16 @@
             halos2[k][h].wait_recv()
             fill_halo(low2, high2, k, h)
             out[k, h] = (hid[k, h].astype(F32) + conv_half(flipped, ext, prod, h)).astype(BF)
+        if k == 0:
+            x5.arrived()
+            rows[...] = recv5[...].astype(F32)
+            for j in range(5):
+                for ml in range(ORDERS):
+                    turn[pl.ds(ml, BANDS, stride=ORDERS), :] = rows[:, ml * 5 + j, :]
+                qt = turn[...].T
+                for r in range(2):
+                    for k in range(2):
+                        score[k, :, j, r, :] = qt[r * 64 + k * 24 : r * 64 + k * 24 + 24, :]
 
     for pairs in (halos, halos2):
         for pair in pairs:
@@ -459,12 +465,13 @@
 
 def whole(*args):
     vmem = pl.BlockSpec(memory_space=pltpu.VMEM)
-    far = pl.BlockSpec(memory_space=pl.ANY)
+    far = pl.BlockSpec(memory_space=pltpu.HBM)
     pair = pltpu.SemaphoreType.DMA((2,))
     halo = (2, 72, NLON)
     eighth = (BANDS, 8, 128)
     scratch = [
-        (HALF, BF), ((ROWS, M, L), BF), ((2 * M, NLON), BF), ((C, 2, 16, L), BF),
+        (HALF, BF), ((ROWS, M, L), BF), ((2 * M, NLON), BF), ((7, 7, C), F32), ((C, C), BF),
+        ((1, L), jnp.int32), ((C, 2, 16, L), BF),
         ((2, 2 * C, 16, 128), F32), ((7, 7, 216), F32), ((2, 144, 384), BF), ((896, 128), BF),
         ((L, L), BF),
         (halo, BF), (halo, BF), (halo, BF), (halo, BF),
@@ -483,10 +490,10 @@
             jax.ShapeDtypeStruct(HALF, BF),
             jax.ShapeDtypeStruct((2, C, 5, 2, M), F32),
         ],
-        in_specs=[far, far, vmem, far, vmem, far, vmem],
+        in_specs=[far] * len(args),
         out_specs=[vmem, vmem],
         scratch_shapes=[pltpu.VMEM(s, d) for s, d in scratch]
-        + [pltpu.SemaphoreType.DMA((4,))]
+        + [pltpu.SemaphoreType.DMA((7,))]
         + [pltpu.SemaphoreType.DMA((4, 2))] * 2
         + [pair] * 7,
         compiler_params=pltpu.CompilerParams(

time: 86.1 us -> 86.1 us (level)
  no operation moved by 1% of the time
where the time goes in v5:
time: 86.1 us; the launch traced here: 85.8 us
  Pallas kernels  80.3 us (93%)
  local copies, waits for them, and re-layouts  4.83 us (6%)
    pallas_call x1, Pallas kernels, whole(): pl.pallas_call(kernel, out_shape=[jax.ShapeDtypeStruct(HALF, BF), jax.Sha...  80.3 us
    unnamed x10, local copies, waits for them, and re-layouts  4.83 us

profile of v5, /device:TPU:1, one launch (start us, length us, event | category | flops | bytes accessed | tf_op | source)
XLA Modules:
  0.0 85.8 jit_solution(5525016231582544358)
XLA Ops:
  0.6 0.0 copy-start
  0.6 1.0 %copy-done = bf16[6,160,160]{2,1,0:T(8,128)(2,1)S(1)} copy-done((bf16[6,160,160]{2,1,0:T(8,128)(2,1)S(1)}, bf16[6,160,160]{2,1,0:T(8,128)(2,1)}, u32[]{:S(2)}) %copy-start) | copy-done | bytes 307224
  1.7 0.0 copy-start.1
  1.7 0.7 copy-done.1
  2.4 0.0 copy-start.2
  2.4 0.7 copy-done.2
  3.1 0.0 copy-start.3
  3.1 0.7 copy-done.3
  3.8 80.3 %shard_map.86 = (bf16[2,2,72,1440]{3,2,1,0:T(8,128)(2,1)S(1)}, f32[2,24,5,2,160]{4,3,2,1,0:T(2,128)S(1)}) custom-call(bf16[2,2,72,1440]{3,2,1,0:T(8,128)(2,1)} %bitcast.13, bf16[6,160,160]{2,1,0:T(8,128)(2,1)S(1)} %copy-done, f32[7,7,24]{2,1,0:T(8,128)S(1)} %bitcast.11, bf16[320,1440]{1,0:T(8,128)(2,1)} %constant.2.clone.table_hbm, ...), custom_call_target="tpu_custom_call" | custom-call | tf_op jit(solution)/shard_map/pallas_call | solution.py:487
  84.1 0.9 %copy.11 = bf16[2,24,6,1440]{3,1,2,0:T(8,128)(2,1)} copy(bf16[2,24,6,1440]{3,1,2,0:T(8,128)(2,1)S(1)} %bitcast.9) | data formatting | bytes 1658880
  85.0 0.8 copy.12
Async XLA Ops:
  0.6 1.0 %copy-start = (bf16[6,160,160]{2,1,0:T(8,128)(2,1)S(1)}, bf16[6,160,160]{2,1,0:T(8,128)(2,1)}, u32[]{:S(2)}) copy-start(bf16[6,160,160]{2,1,0:T(8,128)(2,1)} %leg_hbm.1) | copy-start | bytes 921604
  1.7 0.7 copy-start.1
  2.4 0.7 copy-start.2
  3.1 0.7 copy-start.3

commit v6 on v5

--- a/solution.py
+++ b/solution.py
@@ -17,7 +17,8 @@
 ROWS = 6
 ORDERS = M // BANDS
 ENS = 8
-PART = 112
+WORLD = ENS * BANDS
+SHARE = C // ENS
 BF = jnp.bfloat16
 F32 = jnp.float32
 MESH = pl.DeviceIdType.MESH
@@ -74,25 +75,50 @@
         onehot(row % C == iota((144, C), 1)), mix[...], (((1,), (1,)), ((), ())),
         preferred_element_type=F32,
     ).astype(BF)
+    lane = iota((C, 384), 1)
+    q = lane % 16
+    channel = lane % 128 // 16 * SHARE + q % 3
+    full_lane = iota((144, 384), 1)
+    line = full_lane // 128 * 2 + full_lane % 16 // 6
+    same = (iota((144, 384), 0) // C == line) & (full_lane % 16 < 12)
     for k in range(2):
-        wide = onehot(iota((C, 384), 1) % 64 == iota((C, 384), 0) + C * k)
+        wide = onehot((channel == iota((C, 384), 0)) & (q % 6 // 3 == k))
         full = jnp.dot(tall, wide, preferred_element_type=F32)
-        same = iota((144, 384), 0) // C == iota((144, 384), 1) // 64
         placing[k] = jnp.where(same, full, 0.0).astype(BF)
 
 
-def group(v):
-    return v // 64 * 2 + v % 64 // C, v % 64 % C
-
-
-def mix_lanes(mix):
-    rk, o = group(iota((128, C), 0))
-    tall = jnp.dot(onehot(o == iota((128, C), 1)), mix[...], preferred_element_type=F32).astype(BF)
-    rk, c = group(iota((C, 128), 1))
-    full = jnp.dot(tall, onehot(c == iota((C, 128), 0)), preferred_element_type=F32)
-    a, b = iota((128, 128), 0), iota((128, 128), 1)
-    same = (group(a)[0] == group(b)[0]) & (a % 64 < 48) & (b % 64 < 48)
-    return jnp.where(same, full, 0.0).astype(BF)
+def gather_lanes(dst):
+    for a in range(10):
+        r, ml = a // ORDERS, a % ORDERS
+        row = iota((128, 1), 0)
+        q = row % 16
+        spot = row // 16 * 128 + q // 6 * 60 + ml * 12 + r * 6 + q % 6
+        spot = jnp.where(q < 12, spot, -1)
+        dst[a * 128 : (a + 1) * 128, :] = onehot(iota((128, 1024), 1) == spot)
+
+
+def mix_lanes(mix, dst):
+    row, lane = iota((128, 1), 0), iota((1, 1280), 1)
+    par, ml, r, k = row // 60, row % 60 // 12, row % 12 // 6, row % 6 // 3
+    code = jnp.where(row < 120, ((r * 5 + ml) * 2 + par) * 2 + k, -1)
+    kc = lane % 64
+    seen = jnp.where(kc < 48, lane // 64 * 2 + kc // C, -2)
+    same = code == seen
+    wide = onehot(iota((C, 1280), 1) % 64 % C == iota((C, 1280), 0))
+    for e in range(ENS):
+        pick = onehot(iota((128, C), 1) == e * SHARE + iota((128, C), 0) % 3)
+        tall = jnp.dot(pick, mix[...], preferred_element_type=F32).astype(BF)
+        full = jnp.dot(tall, wide, preferred_element_type=F32)
+        dst[e * 128 : (e + 1) * 128, :] = jnp.where(same, full, 0.0).astype(BF)
+
+
+def scatter_lanes(dst):
+    row = iota((128, 1), 0)
+    for e in range(ENS):
+        ml, r, k = row // 12, row % 12 // 6, row % 6 // 3
+        spot = ml * 128 + r * 64 + k * C + e * SHARE + row % 3
+        spot = jnp.where(row < 60, spot, -1)
+        dst[e * 128 : (e + 1) * 128, :] = onehot(iota((128, 640), 1) == spot)
 
 
 def conv_half(weights, ext, prod, h):
@@ -113,13 +139,18 @@
         self.block, self.slot = block, slot
         self.sent, self.landed, self.sems = sent, landed, sems
 
+    def device(self, peer):
+        if self.axis is None:
+            return {"ens": peer // BANDS, "lat": lax.rem(peer, BANDS)}
+        return {self.axis: peer}
+
     def copy(self, source, target, peer):
         return pltpu.make_async_remote_copy(
             src_ref=source,
             dst_ref=target,
             send_sem=self.sems.at[0],
             recv_sem=self.sems.at[1],
-            device_id={self.axis: peer},
+            device_id=self.device(peer),
             device_id_type=MESH,
         )
 
@@ -147,9 +178,9 @@
     x, legl, table, kern, mix, order, window, wide, taps, placing, target, chosen,
     low, high, low2, high2, weights, flipped, wtmp, ext, prod, act, slope, hid,
     legf, legsend, legrecv, legall, leg,
-    rows, stage, more, send1, recv1, coeff, pooled, grads, gback, send4, recv4, send5, recv5,
-    left, turn,
-    load_sems, halo_sems, halo2_sems, leg_sems, leg2_sems, sems1, sems2, sems3, sems4, sems5,
+    flat, stage, more, send1, recv1, coeff, grads, send4, recv4, send5, recv5,
+    left, turn, regroup, mixing, regroup5,
+    load_sems, halo_sems, halo2_sems, leg_sems, leg2_sems, sems1, sems4, sems5, entered,
 ):
     me = lax.axis_index("lat")
     em = lax.axis_index("ens")
@@ -188,6 +219,14 @@
     greet("lat", BANDS, me)
     greet("ens", ENS, em)
     pl.semaphore_wait(barrier, BANDS - 1 + ENS - 1)
+
+    def tell(s, carry):
+        pl.semaphore_signal(
+            entered, 1, device_id={"ens": lax.rem(em + s, ENS)}, device_id_type=MESH
+        )
+        return carry
+
+    lax.fori_loop(1, ENS, tell, 0)
 
     def halo(source, lo, hi, sems, k):
         return (
@@ -232,6 +271,7 @@
     spread_weights(taps, weights, wtmp, False)
     loads[5].wait()
     place_mix(mix, placing)
+    gather_lanes(regroup)
 
     def fill_halo(lo, hi, k, h):
         if h == 0:
@@ -269,17 +309,39 @@
             )
             legx2.start()
             legall[em] = legrecv[...]
-    rows[:, 30:32, :] = jnp.zeros((BANDS, 2, 128), F32)
-    for a in range(10):
+    spec = spec.astype(BF)
+    lined = jnp.concatenate(
+        [
+            jnp.concatenate(
+                [spec[a * 32 : (a + 1) * 32, t * 128 : (t + 1) * 128] for a in range(10)], axis=1
+            )
+            for t in range(3)
+        ],
+        axis=0,
+    )
+    lined = jnp.dot(lined, regroup[...], preferred_element_type=F32)
+
+    def tile(e, t):
+        return pl.ds(e * 128 + t, BANDS, stride=4)
+
+    for e in range(ENS):
         for t in range(3):
-            rows[:, t * 10 + a, :] = spec[a * 32 : (a + 1) * 32, t * 128 : (t + 1) * 128]
-    send1[...] = rows[...].astype(BF)
-    x1 = Exchange(
-        "lat", BANDS, me, lambda p: send1.at[p], lambda m: recv1.at[m],
-        send1.at[pl.ds(0, BANDS - 1)], recv1.at[pl.ds(0, BANDS - 1)], sems1,
-    )
+            flat[tile(e, t), :] = lined[t * 32 : (t + 1) * 32, e * 128 : (e + 1) * 128]
+        flat[tile(e, 3), :] = jnp.zeros((BANDS, 128), F32)
+    send1[...] = flat[...].reshape(WORLD, 4, 128).astype(BF)
+    self_at = em * BANDS + me
+
+    def swap_all(send, recv, sems):
+        exchange = Exchange(
+            None, WORLD, self_at, lambda p: send.at[p], lambda m: recv.at[m],
+            send.at[pl.ds(0, WORLD - 1)], recv.at[pl.ds(0, WORLD - 1)], sems,
+        )
+        return exchange
+
+    pl.semaphore_wait(entered, ENS - 1)
+    x1 = swap_all(send1, recv1, sems1)
     x1.start()
-    recv1[me] = send1[me]
+    recv1[self_at] = send1[self_at]
 
     loads[2].wait()
     wide[0] = window[:, :, :, 0:128].astype(F32).reshape(2 * C, 16, 128)
@@ -290,17 +352,26 @@
         ],
         axis=2,
     )
+    lane = iota((80, 128), 1)
+
+    def folded(v):
+        return jnp.where(
+            lane % 64 < 60, jnp.where(lane < 64, v[0:80], pltpu.roll(v[80:160], 64, 1)), 0.0
+        )
+
     cr, at = iota((2 * C, 128), 0), iota((2 * C, 128), 1)
-    spot = onehot((at // 64 == cr % 2) & (at % 64 < 48) & (at % 64 % C == cr // 2))
+    mine = (cr // 2 == em * SHARE + at % 3) & (cr % 2 == at % 12 // 6)
+    goal0, goal1 = jnp.zeros((128, 128), F32), jnp.zeros((128, 128), F32)
     for ml in range(ORDERS):
+        spot = onehot(mine & (at // 12 == ml))
         for b in range(2):
             part = wide[b, :, m0 - base + ml, :].astype(BF)
             t = lax.dot_general(part, spot, (((0,), (0,)), ((), ())), preferred_element_type=F32)
             if b == 0:
-                target[ml * L : ml * L + 128, :] = t.astype(BF)
+                goal0 = goal0 + t
             else:
-                target[ml * L + 128 : ml * L + L, :] = t[0 : L - 128].astype(BF)
-    target[800:896, :] = jnp.zeros((96, 128), BF)
+                goal1 = goal1 + t
+    target[...] = folded(jnp.concatenate([goal0, goal1[0 : L - 128]], axis=0))
     place = iota((L, L), 0)
     spots = onehot(iota((L, L), 1) == place % BANDS * 5 + place // BANDS)
     loads[6].wait()
@@ -317,52 +388,46 @@
             at = slice(j * 32, (j + 1) * 32)
             leg[ml, at, 0:128] = more[n // 4, :, n % 4 * 2, :].astype(BF)
             leg[ml, at, 128:L] = more[n // 4, :, n % 4 * 2 + 1, 0 : L - 128].astype(BF)
+    spread_weights(taps, flipped, wtmp, True)
+    mix_lanes(mix, mixing)
+    scatter_lanes(regroup5)
 
     x1.arrived()
-    rows[...] = recv1[...].astype(F32)
-    lane = lax.broadcasted_iota(jnp.int32, (L, 128), 1)
+
+    def arranged(recv):
+        flat[...] = recv[...].astype(F32).reshape(WORLD * 4, 128)
+        return jnp.concatenate(
+            [
+                jnp.concatenate([flat[tile(e, t), :] for e in range(ENS)], axis=1)
+                for t in range(3)
+            ],
+            axis=0,
+        )
+
+    waves = arranged(recv1)
+    kind = iota((96, 1024), 1) % 128 // 12
+    acc = jnp.zeros((L, 1024), F32)
     for ml in range(ORDERS):
-        acc = []
-        for r in range(2):
-            a = jnp.concatenate(
-                [rows[:, t * 10 + r * 5 + ml, :] for t in range(3)], axis=0
-            ).astype(BF)
-            for par in range(2):
-                acc.append(
-                    lax.dot_general(
-                        leg[ml, par * 96 : (par + 1) * 96, :],
-                        a,
-                        (((0,), (0,)), ((), ())),
-                        preferred_element_type=F32,
-                    )
-                )
-        first = acc[0] + pltpu.roll(acc[1], 64, 1)
-        second = pltpu.roll(acc[2], 64, 1) + acc[3]
-        coeff[ml * L : (ml + 1) * L, :] = jnp.where(lane < 64, first, second).astype(BF)
-    coeff[800:896, :] = jnp.zeros((96, 128), BF)
-
-    def piece(ref, e):
-        return ref.at[pl.ds(pl.multiple_of(e * PART, 16), PART)]
-
-    x2 = Exchange(
-        "ens", ENS, em, lambda p: piece(coeff, p), lambda m: pooled.at[m],
-        coeff.at[pl.ds(0, (ENS - 1) * PART)], pooled.at[pl.ds(0, ENS - 1)], sems2,
-    )
-    x2.start()
-    pooled[em] = piece(coeff, em)[...]
-    spread_weights(taps, flipped, wtmp, True)
-    x2.arrived()
-
-    small = lax.broadcasted_iota(jnp.int32, (16, 128), 1) % 64
+        both = jnp.concatenate(
+            [jnp.where(kind == ml, waves, 0.0), jnp.where(kind == ml + 5, waves, 0.0)], axis=0
+        ).astype(BF)
+        acc = acc + lax.dot_general(
+            leg[ml], both, (((0,), (0,)), ((), ())), preferred_element_type=F32
+        )
+    for e in range(ENS):
+        v = acc[:, e * 128 : (e + 1) * 128]
+        coeff[e] = folded(v + pltpu.roll(v, 68, 1))
+
+    small = iota((16, 128), 1) % 64
 
     def other(v):
-        return jnp.where(small < 24, pltpu.roll(v, 104, 1), pltpu.roll(v, 24, 1))
+        return jnp.where(small % 6 < 3, pltpu.roll(v, 125, 1), pltpu.roll(v, 3, 1))
 
     def step(s, carry):
         at = pl.ds(pl.multiple_of(s * 16, 16), 16)
-        u = [pooled[a, at, :].astype(F32) for a in range(ENS)]
-        w = [jnp.where(small < 48, other(v), 0.0) for v in u]
-        goal = target[pl.ds(pl.multiple_of(em * PART + s * 16, 16), 16), :].astype(F32)
+        u = [coeff[a, at, :] for a in range(ENS)]
+        w = [jnp.where(small < 60, other(v), 0.0) for v in u]
+        goal = target[at, :]
         plus = [jnp.zeros((16, 128), F32)] * ENS
         for b in range(ENS):
             turned = jnp.zeros((16, 128), F32)
@@ -373,55 +438,58 @@
                 plus[b] = plus[b] - one
                 turned = turned + two
             plus[b] = plus[b] + soft_sign(u[b] - w[b])
-            plus[b] = plus[b] - jnp.where(small < 48, other(turned), 0.0)
+            plus[b] = plus[b] - jnp.where(small < 60, other(turned), 0.0)
         for a in range(ENS):
-            grads[a, at, :] = (soft_sign(u[a] - goal) / 16.0 - plus[a] / 240.0).astype(BF)
+            coeff[a, at, :] = soft_sign(u[a] - goal) / 16.0 - plus[a] / 240.0
         return carry
 
-    lax.fori_loop(0, PART // 16, step, 0)
-    x3 = Exchange(
-        "ens", ENS, em, lambda p: grads.at[p], lambda m: piece(gback, m),
-        grads.at[pl.ds(0, ENS - 1)], gback.at[pl.ds(0, (ENS - 1) * PART)], sems3,
-    )
-    x3.start()
-    piece(gback, em)[...] = grads[em]
-    mixing = mix_lanes(mix)
-    x3.arrived()
-
+    lax.fori_loop(0, 5, step, 0)
+    for e in range(ENS):
+        g = coeff[e]
+        tall = jnp.concatenate([g, pltpu.roll(g, 64, 1)], axis=0)
+        grads[:, e * 128 : (e + 1) * 128] = jnp.where(iota((L, 128), 1) < 60, tall, 0.0).astype(BF)
+    kind = iota((L, 1024), 1) % 128 // 12
+    acc = jnp.zeros((192, 1024), F32)
     for ml in range(ORDERS):
-        s = jnp.dot(leg[ml], gback[ml * L : (ml + 1) * L, :], preferred_element_type=F32)
-        for j in range(ROWS):
-            rows[:, ml * 6 + j, :] = s[j * 32 : (j + 1) * 32, :]
-    send4[...] = rows[...].astype(BF)
-    x4 = Exchange(
-        "lat", BANDS, me, lambda p: send4.at[p], lambda m: recv4.at[m],
-        send4.at[pl.ds(0, BANDS - 1)], recv4.at[pl.ds(0, BANDS - 1)], sems4,
-    )
+        g = jnp.where(kind == ml, grads[...].astype(F32), 0.0).astype(BF)
+        acc = acc + jnp.dot(leg[ml], g, preferred_element_type=F32)
+    for e in range(ENS):
+        for t in range(3):
+            even = acc[t * 32 : (t + 1) * 32, e * 128 : (e + 1) * 128]
+            odd = acc[96 + t * 32 : 96 + (t + 1) * 32, e * 128 : (e + 1) * 128]
+            flat[tile(e, t), :] = even + pltpu.roll(odd, 60, 1)
+    send4[...] = flat[...].reshape(WORLD, 4, 128).astype(BF)
+    x4 = swap_all(send4, recv4, sems4)
     x4.start()
-    recv4[me] = send4[me]
-    for ml in range(ORDERS):
-        o = jnp.dot(chosen[...], gback[ml * L : (ml + 1) * L, :], preferred_element_type=F32)
-        for j in range(5):
-            rows[:, ml * 5 + j, :] = o[j * 32 : (j + 1) * 32, :]
-    send5[...] = rows[...].astype(BF)
-    x5 = Exchange(
-        "lat", BANDS, me, lambda p: send5.at[p], lambda m: recv5.at[m],
-        send5.at[pl.ds(0, BANDS - 1)], recv5.at[pl.ds(0, BANDS - 1)], sems5,
-    )
-    recv5[me] = send5[me]
+    recv4[self_at] = send4[self_at]
+    o = jnp.dot(chosen[...], grads[...], preferred_element_type=F32)
+    for e in range(ENS):
+        part = [o[j * 32 : (j + 1) * 32, e * 128 : (e + 1) * 128] for j in range(5)]
+        for t in range(2):
+            flat[tile(e, t), :] = part[2 * t] + pltpu.roll(part[2 * t + 1], 64, 1)
+        flat[tile(e, 2), :] = part[4]
+    send5[...] = flat[...].reshape(WORLD, 4, 128).astype(BF)
+    x5 = swap_all(send5, recv5, sems5)
+    recv5[self_at] = send5[self_at]
 
     x4.arrived()
     x5.start()
-    rows[...] = jnp.dot(
-        recv4[...].reshape(BANDS * 32, 128), mixing, preferred_element_type=F32
-    ).reshape(BANDS, 32, 128)
-    for i in range(ROWS):
-        j = (i % 2) * 3 + i // 2
-        q = jnp.concatenate([rows[:, ml * 6 + j, :] for ml in range(ORDERS)], axis=0)
-        qt = q.T
+    lined = jnp.dot(arranged(recv4).astype(BF), mixing[...], preferred_element_type=F32)
+    for t in range(3):
         for r in range(2):
-            for k in range(2):
-                left[r, k, i * 24 : (i + 1) * 24, :] = qt[r * 64 + k * 24 : r * 64 + k * 24 + 24, :]
+            q = jnp.concatenate(
+                [
+                    lined[t * 32 : (t + 1) * 32, (r * 5 + ml) * 128 : (r * 5 + ml + 1) * 128]
+                    for ml in range(ORDERS)
+                ],
+                axis=0,
+            )
+            qt = q.T
+            for par in range(2):
+                for k in range(2):
+                    at = par * 64 + k * C
+                    i = 2 * t + par
+                    left[r, k, i * C : (i + 1) * C, :] = qt[at : at + C, :]
     halos2 = []
     for k in range(2):
         grad = jnp.dot(left[0, k].astype(BF), table[0:M, :], preferred_element_type=F32)
@@ -442,10 +510,22 @@
             out[k, h] = (hid[k, h].astype(F32) + conv_half(flipped, ext, prod, h)).astype(BF)
         if k == 0:
             x5.arrived()
-            rows[...] = recv5[...].astype(F32)
+            got = arranged(recv5)
+            lined = []
+            for j in range(5):
+                v = got[j // 2 * 32 : j // 2 * 32 + 32]
+                if j % 2:
+                    v = jnp.concatenate(
+                        [pltpu.roll(v[:, e * 128 : (e + 1) * 128], 64, 1) for e in range(ENS)], axis=1
+                    )
+                lined.append(v)
+            lined = jnp.concatenate(lined, axis=0).astype(BF)
+            lined = jnp.dot(lined, regroup5[...], preferred_element_type=F32)
             for j in range(5):
                 for ml in range(ORDERS):
-                    turn[pl.ds(ml, BANDS, stride=ORDERS), :] = rows[:, ml * 5 + j, :]
+                    turn[pl.ds(ml, BANDS, stride=ORDERS), :] = lined[
+                        j * 32 : (j + 1) * 32, ml * 128 : (ml + 1) * 128
+                    ]
                 qt = turn[...].T
                 for r in range(2):
                     for k in range(2):
@@ -455,12 +535,12 @@
         for pair in pairs:
             for copy in pair:
                 copy.wait_send()
-    for exchange in (legx, legx2, x1, x2, x3, x4, x5):
+    for exchange in (legx, legx2, x1, x4, x5):
         exchange.done()
 
 
 HALF = (2, 2, 72, NLON)
-CHUNK = (BANDS, 32, 128)
+CHUNK = (WORLD, 4, 128)
 
 
 def whole(*args):
@@ -472,17 +552,17 @@
     scratch = [
         (HALF, BF), ((ROWS, M, L), BF), ((2 * M, NLON), BF), ((7, 7, C), F32), ((C, C), BF),
         ((1, L), jnp.int32), ((C, 2, 16, L), BF),
-        ((2, 2 * C, 16, 128), F32), ((7, 7, 216), F32), ((2, 144, 384), BF), ((896, 128), BF),
+        ((2, 2 * C, 16, 128), F32), ((7, 7, 216), F32), ((2, 144, 384), BF), ((80, 128), F32),
         ((L, L), BF),
         (halo, BF), (halo, BF), (halo, BF), (halo, BF),
         ((2, 504, 216), BF), ((2, 504, 216), BF), ((504, 216), F32),
         ((216, 1536), BF), ((504, 1536), F32), ((144, NLON), BF), (HALF, BF), (HALF, BF),
         ((2, ROWS, M, 128), F32), (eighth, BF), (eighth, BF), ((ENS,) + eighth, BF),
         ((ORDERS, 192, L), BF),
-        (CHUNK, F32), (eighth, F32), ((ENS,) + eighth, F32), (CHUNK, BF), (CHUNK, BF),
-        ((896, 128), BF), ((ENS, PART, 128), BF), ((ENS, PART, 128), BF), ((896, 128), BF),
-        (CHUNK, BF), (CHUNK, BF), (CHUNK, BF), (CHUNK, BF),
+        ((WORLD * 4, 128), F32), (eighth, F32), ((ENS,) + eighth, F32), (CHUNK, BF), (CHUNK, BF),
+        ((ENS, 80, 128), F32), ((L, 1024), BF), (CHUNK, BF), (CHUNK, BF), (CHUNK, BF), (CHUNK, BF),
         ((2, 2, 144, M), F32), ((M, 128), F32),
+        ((1280, 1024), BF), ((1024, 1280), BF), ((1024, 640), BF),
     ]
     return pl.pallas_call(
         kernel,
@@ -495,9 +575,10 @@
         scratch_shapes=[pltpu.VMEM(s, d) for s, d in scratch]
         + [pltpu.SemaphoreType.DMA((7,))]
         + [pltpu.SemaphoreType.DMA((4, 2))] * 2
-        + [pair] * 7,
+        + [pair] * 5
+        + [pltpu.SemaphoreType.REGULAR],
         compiler_params=pltpu.CompilerParams(
-            vmem_limit_bytes=52 << 20, collective_id=0, has_side_effects=True
+            vmem_limit_bytes=62 << 20, collective_id=0, has_side_effects=True
         ),
     )(*args)
 

time: 86.1 us -> 82.9 us (0.963)
  Pallas kernels: 80.3 us -> 78 us
    pallas_call x1, Pallas kernels: 80.3 us -> 78 us  [whole(): pl.pallas_call(kernel, out_shape=[jax.ShapeDtypeStruct(HALF, BF), jax.Sha...]
    unnamed x10 -> x2, local copies, waits for them, and re-layouts: 4.83 us -> 4.11 us
where the time goes in v6:
time: 82.9 us; the launch traced here: 82.8 us
  Pallas kernels  78 us (94%)
  local copies, waits for them, and re-layouts  4.11 us (5%)
    pallas_call x1, Pallas kernels, whole(): pl.pallas_call(kernel, out_shape=[jax.ShapeDtypeStruct(HALF, BF), jax.Sha...  78 us
    unnamed x2, local copies, waits for them, and re-layouts  4.11 us

profile of v6, /device:TPU:1, one launch (start us, length us, event | category | flops | bytes accessed | tf_op | source)
XLA Modules:
  0.0 82.8 jit_solution(160592329834681304)
XLA Ops:
  0.6 78.0 %shard_map.86 = (bf16[2,2,72,1440]{3,2,1,0:T(8,128)(2,1)}, f32[2,24,5,2,160]{4,3,2,1,0:T(2,128)}) custom-call(bf16[2,2,72,1440]{3,2,1,0:T(8,128)(2,1)} %bitcast.9, bf16[6,160,160]{2,1,0:T(8,128)(2,1)} %leg_hbm.1, f32[7,7,24]{2,1,0:T(8,128)} %bitcast.12, bf16[320,1440]{1,0:T(8,128)(2,1)} %constant.2.clone.table_hbm, bf16[24,24]{1,0:T(8,128)(2,1)} %mix_hbm.1, ...), custom_call_target="tpu_custom_call" | custom-call | tf_op jit(solution)/shard_map/pallas_call | solution.py:567
  78.6 2.1 %copy.11 = bf16[2,24,6,1440]{3,1,2,0:T(8,128)(2,1)} copy(bf16[2,24,6,1440]{3,1,2,0:T(8,128)(2,1)} %bitcast.10) | data formatting | bytes 1658880
  80.8 2.0 %copy.12 = f32[2,24,2,160,5]{3,2,4,1,0:T(2,128)} copy(f32[2,24,2,160,5]{3,2,4,1,0:T(2,128)} %bitcast.11) | data formatting | bytes 614400

commit v7 on v6

--- a/solution.py
+++ b/solution.py
@@ -87,14 +87,11 @@
         placing[k] = jnp.where(same, full, 0.0).astype(BF)
 
 
-def gather_lanes(dst):
-    for a in range(10):
-        r, ml = a // ORDERS, a % ORDERS
-        row = iota((128, 1), 0)
-        q = row % 16
-        spot = row // 16 * 128 + q // 6 * 60 + ml * 12 + r * 6 + q % 6
-        spot = jnp.where(q < 12, spot, -1)
-        dst[a * 128 : (a + 1) * 128, :] = onehot(iota((128, 1024), 1) == spot)
+def gather_lanes():
+    a, e, q = np.meshgrid(np.arange(10), np.arange(ENS), np.arange(16), indexing="ij")
+    spot = e * 128 + q // 6 * 60 + a % ORDERS * 12 + a // ORDERS * 6 + q % 6
+    spot = np.where(q < 12, spot, -1).reshape(-1, 1)
+    return (np.arange(1024) == spot).astype(ml_dtypes.bfloat16)
 
 
 def mix_lanes(mix, dst):
@@ -112,13 +109,11 @@
         dst[e * 128 : (e + 1) * 128, :] = jnp.where(same, full, 0.0).astype(BF)
 
 
-def scatter_lanes(dst):
-    row = iota((128, 1), 0)
-    for e in range(ENS):
-        ml, r, k = row // 12, row % 12 // 6, row % 6 // 3
-        spot = ml * 128 + r * 64 + k * C + e * SHARE + row % 3
-        spot = jnp.where(row < 60, spot, -1)
-        dst[e * 128 : (e + 1) * 128, :] = onehot(iota((128, 640), 1) == spot)
+def scatter_lanes():
+    e, row = np.meshgrid(np.arange(ENS), np.arange(128), indexing="ij")
+    spot = row // 12 * 128 + row % 12 // 6 * 64 + row % 6 // 3 * C + e * SHARE + row % 3
+    spot = np.where(row < 60, spot, -1).reshape(-1, 1)
+    return (np.arange(640) == spot).astype(ml_dtypes.bfloat16)
 
 
 def conv_half(weights, ext, prod, h):
@@ -173,7 +168,7 @@
 
 
 def kernel(
-    x_hbm, leg_hbm, kern_hbm, table_hbm, mix_hbm, truth, order_hbm,
+    x_hbm, leg_hbm, kern_hbm, table_hbm, mix_hbm, truth, order_hbm, gather_hbm, scatter_hbm,
     out, score,
     x, legl, table, kern, mix, order, window, wide, taps, placing, target, chosen,
     low, high, low2, high2, weights, flipped, wtmp, ext, prod, act, slope, hid,
@@ -200,6 +195,8 @@
                 (kern_hbm, kern),
                 (mix_hbm, mix),
                 (order_hbm, order),
+                (gather_hbm, regroup),
+                (scatter_hbm, regroup5),
             ]
         )
     ]
@@ -271,7 +268,6 @@
     spread_weights(taps, weights, wtmp, False)
     loads[5].wait()
     place_mix(mix, placing)
-    gather_lanes(regroup)
 
     def fill_halo(lo, hi, k, h):
         if h == 0:
@@ -319,6 +315,7 @@
         ],
         axis=0,
     )
+    loads[7].wait()
     lined = jnp.dot(lined, regroup[...], preferred_element_type=F32)
 
     def tile(e, t):
@@ -388,9 +385,7 @@
             at = slice(j * 32, (j + 1) * 32)
             leg[ml, at, 0:128] = more[n // 4, :, n % 4 * 2, :].astype(BF)
             leg[ml, at, 128:L] = more[n // 4, :, n % 4 * 2 + 1, 0 : L - 128].astype(BF)
-    spread_weights(taps, flipped, wtmp, True)
     mix_lanes(mix, mixing)
-    scatter_lanes(regroup5)
 
     x1.arrived()
 
@@ -472,6 +467,7 @@
     x5 = swap_all(send5, recv5, sems5)
     recv5[self_at] = send5[self_at]
 
+    spread_weights(taps, flipped, wtmp, True)
     x4.arrived()
     x5.start()
     lined = jnp.dot(arranged(recv4).astype(BF), mixing[...], preferred_element_type=F32)
@@ -520,6 +516,7 @@
                     )
                 lined.append(v)
             lined = jnp.concatenate(lined, axis=0).astype(BF)
+            loads[8].wait()
             lined = jnp.dot(lined, regroup5[...], preferred_element_type=F32)
             for j in range(5):
                 for ml in range(ORDERS):
@@ -573,7 +570,7 @@
         in_specs=[far] * len(args),
         out_specs=[vmem, vmem],
         scratch_shapes=[pltpu.VMEM(s, d) for s, d in scratch]
-        + [pltpu.SemaphoreType.DMA((7,))]
+        + [pltpu.SemaphoreType.DMA((9,))]
         + [pltpu.SemaphoreType.DMA((4, 2))] * 2
         + [pair] * 5
         + [pltpu.SemaphoreType.REGULAR],
@@ -587,7 +584,10 @@
     table = jnp.asarray(wave_table())
     x = jnp.transpose(fields, (0, 2, 1, 3)).reshape(HALF)
     kern = jnp.transpose(depth_kernel, (1, 2, 0))
-    out, score = whole(x, legendre, kern, table, mix_weight, truth, degree_order.reshape(1, L))
+    out, score = whole(
+        x, legendre, kern, table, mix_weight, truth, degree_order.reshape(1, L),
+        jnp.asarray(gather_lanes()), jnp.asarray(scatter_lanes()),
+    )
     grad_fields = jnp.transpose(out.reshape(2, ROWS, C, NLON), (0, 2, 1, 3))
     return grad_fields, jnp.transpose(score, (0, 1, 3, 4, 2))
 

time: 82.9 us -> 82.8 us (level)
  no operation moved by 1% of the time
where the time goes in v7:
time: 82.8 us; the launch traced here: 82.6 us
  Pallas kernels  77.9 us (94%)
  local copies, waits for them, and re-layouts  4.11 us (5%)
    pallas_call x1, Pallas kernels, whole(): pl.pallas_call(kernel, out_shape=[jax.ShapeDtypeStruct(HALF, BF), jax.Sha...  77.9 us
    unnamed x2, local copies, waits for them, and re-layouts  4.11 us

profile of v7, /device:TPU:1, one launch (start us, length us, event | category | flops | bytes accessed | tf_op | source)
XLA Modules:
  0.0 82.6 jit_solution(6065918601705574413)
XLA Ops:
  0.6 77.9 %shard_map.104 = (bf16[2,2,72,1440]{3,2,1,0:T(8,128)(2,1)}, f32[2,24,5,2,160]{4,3,2,1,0:T(2,128)}) custom-call(bf16[2,2,72,1440]{3,2,1,0:T(8,128)(2,1)} %bitcast.9, bf16[6,160,160]{2,1,0:T(8,128)(2,1)} %leg_hbm.1, f32[7,7,24]{2,1,0:T(8,128)} %bitcast.12, bf16[320,1440]{1,0:T(8,128)(2,1)} %constant.6.clone.table_hbm, bf16[24,24]{1,0:T(8,128)(2,1)} %mix_hbm.1, ...), custom_call_target="tpu_custom_call" | custom-call | tf_op jit(solution)/shard_map/pallas_call | solution.py:564
  78.5 2.1 %copy.13 = bf16[2,24,6,1440]{3,1,2,0:T(8,128)(2,1)} copy(bf16[2,24,6,1440]{3,1,2,0:T(8,128)(2,1)} %bitcast.10) | data formatting | bytes 1658880
  80.6 2.0 %copy.14 = f32[2,24,2,160,5]{3,2,4,1,0:T(2,128)} copy(f32[2,24,2,160,5]{3,2,4,1,0:T(2,128)} %bitcast.11) | data formatting | bytes 614400

commit v8 on v7

--- a/solution.py
+++ b/solution.py
@@ -134,37 +134,62 @@
         self.block, self.slot = block, slot
         self.sent, self.landed, self.sems = sent, landed, sems
 
-    def device(self, peer):
-        if self.axis is None:
-            return {"ens": peer // BANDS, "lat": lax.rem(peer, BANDS)}
-        return {self.axis: peer}
-
-    def copy(self, source, target, peer):
+    def copy(self, source, target, device):
         return pltpu.make_async_remote_copy(
             src_ref=source,
             dst_ref=target,
             send_sem=self.sems.at[0],
             recv_sem=self.sems.at[1],
-            device_id=self.device(peer),
+            device_id=device,
             device_id_type=MESH,
         )
 
     def start(self):
         def step(s, carry):
             peer = lax.rem(self.me + s, self.count)
-            self.copy(self.block(peer), self.slot(self.me), peer).start()
+            self.copy(self.block(peer), self.slot(self.me), {self.axis: peer}).start()
             return carry
 
         lax.fori_loop(1, self.count, step, 0)
 
     def whole(self):
-        return self.copy(self.sent, self.landed, lax.rem(self.me + 1, self.count))
+        return self.copy(self.sent, self.landed, {self.axis: lax.rem(self.me + 1, self.count)})
 
     def arrived(self):
         self.whole().wait_recv()
 
     def done(self):
         self.whole().wait_send()
+
+
+class Everyone(Exchange):
+    def __init__(self, send, recv, em, me, sems):
+        self.send, self.recv, self.em, self.lat, self.sems = send, recv, em, me, sems
+        self.at = em * BANDS + me
+
+    def start(self):
+        owners = [lax.rem(self.em + u, ENS) for u in range(ENS)]
+
+        def one(e, band):
+            self.copy(
+                self.send.at[e * BANDS + band], self.recv.at[self.at], {"ens": e, "lat": band}
+            ).start()
+
+        def step(s, carry):
+            band = lax.rem(self.lat + s, BANDS)
+            for e in owners:
+                one(e, band)
+            return carry
+
+        lax.fori_loop(1, BANDS, step, 0)
+        for e in owners[1:]:
+            one(e, self.lat)
+
+    def whole(self):
+        rest = pl.ds(0, WORLD - 1)
+        return self.copy(
+            self.send.at[rest], self.recv.at[rest], {"lat": lax.rem(self.lat + 1, BANDS)}
+        )
 
 
 def kernel(
@@ -328,15 +353,8 @@
     send1[...] = flat[...].reshape(WORLD, 4, 128).astype(BF)
     self_at = em * BANDS + me
 
-    def swap_all(send, recv, sems):
-        exchange = Exchange(
-            None, WORLD, self_at, lambda p: send.at[p], lambda m: recv.at[m],
-            send.at[pl.ds(0, WORLD - 1)], recv.at[pl.ds(0, WORLD - 1)], sems,
-        )
-        return exchange
-
     pl.semaphore_wait(entered, ENS - 1)
-    x1 = swap_all(send1, recv1, sems1)
+    x1 = Everyone(send1, recv1, em, me, sems1)
     x1.start()
     recv1[self_at] = send1[self_at]
 
@@ -454,7 +472,7 @@
             odd = acc[96 + t * 32 : 96 + (t + 1) * 32, e * 128 : (e + 1) * 128]
             flat[tile(e, t), :] = even + pltpu.roll(odd, 60, 1)
     send4[...] = flat[...].reshape(WORLD, 4, 128).astype(BF)
-    x4 = swap_all(send4, recv4, sems4)
+    x4 = Everyone(send4, recv4, em, me, sems4)
     x4.start()
     recv4[self_at] = send4[self_at]
     o = jnp.dot(chosen[...], grads[...], preferred_element_type=F32)
@@ -464,12 +482,11 @@
             flat[tile(e, t), :] = part[2 * t] + pltpu.roll(part[2 * t + 1], 64, 1)
         flat[tile(e, 2), :] = part[4]
     send5[...] = flat[...].reshape(WORLD, 4, 128).astype(BF)
-    x5 = swap_all(send5, recv5, sems5)
+    x5 = Everyone(send5, recv5, em, me, sems5)
     recv5[self_at] = send5[self_at]
 
     spread_weights(taps, flipped, wtmp, True)
     x4.arrived()
-    x5.start()
     lined = jnp.dot(arranged(recv4).astype(BF), mixing[...], preferred_element_type=F32)
     for t in range(3):
         for r in range(2):
@@ -496,6 +513,7 @@
         for copy in pair:
             copy.start()
         halos2.append(pair)
+    x5.start()
 
     for k in range(2):
         ext[0:72, :] = wrapped(hid[k, 0])
@@ -504,29 +522,28 @@
             halos2[k][h].wait_recv()
             fill_halo(low2, high2, k, h)
             out[k, h] = (hid[k, h].astype(F32) + conv_half(flipped, ext, prod, h)).astype(BF)
-        if k == 0:
-            x5.arrived()
-            got = arranged(recv5)
-            lined = []
-            for j in range(5):
-                v = got[j // 2 * 32 : j // 2 * 32 + 32]
-                if j % 2:
-                    v = jnp.concatenate(
-                        [pltpu.roll(v[:, e * 128 : (e + 1) * 128], 64, 1) for e in range(ENS)], axis=1
-                    )
-                lined.append(v)
-            lined = jnp.concatenate(lined, axis=0).astype(BF)
-            loads[8].wait()
-            lined = jnp.dot(lined, regroup5[...], preferred_element_type=F32)
-            for j in range(5):
-                for ml in range(ORDERS):
-                    turn[pl.ds(ml, BANDS, stride=ORDERS), :] = lined[
-                        j * 32 : (j + 1) * 32, ml * 128 : (ml + 1) * 128
-                    ]
-                qt = turn[...].T
-                for r in range(2):
-                    for k in range(2):
-                        score[k, :, j, r, :] = qt[r * 64 + k * 24 : r * 64 + k * 24 + 24, :]
+    x5.arrived()
+    got = arranged(recv5)
+    lined = []
+    for j in range(5):
+        v = got[j // 2 * 32 : j // 2 * 32 + 32]
+        if j % 2:
+            v = jnp.concatenate(
+                [pltpu.roll(v[:, e * 128 : (e + 1) * 128], 64, 1) for e in range(ENS)], axis=1
+            )
+        lined.append(v)
+    lined = jnp.concatenate(lined, axis=0).astype(BF)
+    loads[8].wait()
+    lined = jnp.dot(lined, regroup5[...], preferred_element_type=F32)
+    for j in range(5):
+        for ml in range(ORDERS):
+            turn[pl.ds(ml, BANDS, stride=ORDERS), :] = lined[
+                j * 32 : (j + 1) * 32, ml * 128 : (ml + 1) * 128
+            ]
+        qt = turn[...].T
+        for r in range(2):
+            for k in range(2):
+                score[k, :, j, r, :] = qt[r * 64 + k * 24 : r * 64 + k * 24 + 24, :]
 
     for pairs in (halos, halos2):
         for pair in pairs:

time: 82.8 us -> 85.3 us (1.030)
  Pallas kernels: 77.9 us -> 80.4 us
    pallas_call x1, Pallas kernels: 77.9 us -> 80.4 us  [whole(): pl.pallas_call(kernel, out_shape=[jax.ShapeDtypeStruct(HALF, BF), jax.Sha...]
where the time goes in v8:
time: 85.3 us; the launch traced here: 85.1 us
  Pallas kernels  80.4 us (94%)
  local copies, waits for them, and re-layouts  4.11 us (5%)
    pallas_call x1, Pallas kernels, whole(): pl.pallas_call(kernel, out_shape=[jax.ShapeDtypeStruct(HALF, BF), jax.Sha...  80.4 us
    unnamed x2, local copies, waits for them, and re-layouts  4.11 us

profile of v8, /device:TPU:1, one launch (start us, length us, event | category | flops | bytes accessed | tf_op | source)
XLA Modules:
  0.0 85.1 jit_solution(15563688919172894993)
XLA Ops:
  0.6 80.4 %shard_map.104 = (bf16[2,2,72,1440]{3,2,1,0:T(8,128)(2,1)}, f32[2,24,5,2,160]{4,3,2,1,0:T(2,128)}) custom-call(bf16[2,2,72,1440]{3,2,1,0:T(8,128)(2,1)} %bitcast.9, bf16[6,160,160]{2,1,0:T(8,128)(2,1)} %leg_hbm.1, f32[7,7,24]{2,1,0:T(8,128)} %bitcast.12, bf16[320,1440]{1,0:T(8,128)(2,1)} %constant.6.clone.table_hbm, bf16[24,24]{1,0:T(8,128)(2,1)} %mix_hbm.1, ...), custom_call_target="tpu_custom_call" | custom-call | tf_op jit(solution)/shard_map/pallas_call | solution.py:581
  81.0 2.1 %copy.13 = bf16[2,24,6,1440]{3,1,2,0:T(8,128)(2,1)} copy(bf16[2,24,6,1440]{3,1,2,0:T(8,128)(2,1)} %bitcast.10) | data formatting | bytes 1658880
  83.2 2.0 %copy.14 = f32[2,24,2,160,5]{3,2,4,1,0:T(2,128)} copy(f32[2,24,2,160,5]{3,2,4,1,0:T(2,128)} %bitcast.11) | data formatting | bytes 614400

commit v9 on v7

--- a/solution.py
+++ b/solution.py
@@ -134,37 +134,60 @@
         self.block, self.slot = block, slot
         self.sent, self.landed, self.sems = sent, landed, sems
 
-    def device(self, peer):
-        if self.axis is None:
-            return {"ens": peer // BANDS, "lat": lax.rem(peer, BANDS)}
-        return {self.axis: peer}
-
-    def copy(self, source, target, peer):
+    def copy(self, source, target, device):
         return pltpu.make_async_remote_copy(
             src_ref=source,
             dst_ref=target,
             send_sem=self.sems.at[0],
             recv_sem=self.sems.at[1],
-            device_id=self.device(peer),
+            device_id=device,
             device_id_type=MESH,
         )
 
     def start(self):
         def step(s, carry):
             peer = lax.rem(self.me + s, self.count)
-            self.copy(self.block(peer), self.slot(self.me), peer).start()
+            self.copy(self.block(peer), self.slot(self.me), {self.axis: peer}).start()
             return carry
 
         lax.fori_loop(1, self.count, step, 0)
 
     def whole(self):
-        return self.copy(self.sent, self.landed, lax.rem(self.me + 1, self.count))
+        return self.copy(self.sent, self.landed, {self.axis: lax.rem(self.me + 1, self.count)})
 
     def arrived(self):
         self.whole().wait_recv()
 
     def done(self):
         self.whole().wait_send()
+
+
+class Everyone(Exchange):
+    def __init__(self, send, recv, em, me, sems):
+        self.send, self.recv, self.em, self.lat, self.sems = send, recv, em, me, sems
+        self.at = em * BANDS + me
+
+    def start(self):
+        owners = [lax.rem(self.em + u, ENS) for u in range(ENS)]
+
+        def one(e, band):
+            self.copy(
+                self.send.at[e * BANDS + band], self.recv.at[self.at], {"ens": e, "lat": band}
+            ).start()
+
+        for u, e in enumerate(owners):
+
+            def step(s, carry, e=e):
+                one(e, lax.rem(self.lat + s, BANDS))
+                return carry
+
+            lax.fori_loop(0 if u else 1, BANDS, step, 0)
+
+    def whole(self):
+        rest = pl.ds(0, WORLD - 1)
+        return self.copy(
+            self.send.at[rest], self.recv.at[rest], {"lat": lax.rem(self.lat + 1, BANDS)}
+        )
 
 
 def kernel(
@@ -328,15 +351,8 @@
     send1[...] = flat[...].reshape(WORLD, 4, 128).astype(BF)
     self_at = em * BANDS + me
 
-    def swap_all(send, recv, sems):
-        exchange = Exchange(
-            None, WORLD, self_at, lambda p: send.at[p], lambda m: recv.at[m],
-            send.at[pl.ds(0, WORLD - 1)], recv.at[pl.ds(0, WORLD - 1)], sems,
-        )
-        return exchange
-
     pl.semaphore_wait(entered, ENS - 1)
-    x1 = swap_all(send1, recv1, sems1)
+    x1 = Everyone(send1, recv1, em, me, sems1)
     x1.start()
     recv1[self_at] = send1[self_at]
 
@@ -454,7 +470,7 @@
             odd = acc[96 + t * 32 : 96 + (t + 1) * 32, e * 128 : (e + 1) * 128]
             flat[tile(e, t), :] = even + pltpu.roll(odd, 60, 1)
     send4[...] = flat[...].reshape(WORLD, 4, 128).astype(BF)
-    x4 = swap_all(send4, recv4, sems4)
+    x4 = Everyone(send4, recv4, em, me, sems4)
     x4.start()
     recv4[self_at] = send4[self_at]
     o = jnp.dot(chosen[...], grads[...], preferred_element_type=F32)
@@ -464,7 +480,7 @@
             flat[tile(e, t), :] = part[2 * t] + pltpu.roll(part[2 * t + 1], 64, 1)
         flat[tile(e, 2), :] = part[4]
     send5[...] = flat[...].reshape(WORLD, 4, 128).astype(BF)
-    x5 = swap_all(send5, recv5, sems5)
+    x5 = Everyone(send5, recv5, em, me, sems5)
     recv5[self_at] = send5[self_at]
 
     spread_weights(taps, flipped, wtmp, True)

time: 82.8 us -> 81.4 us (0.983)
  Pallas kernels: 77.9 us -> 76.5 us
    pallas_call x1, Pallas kernels: 77.9 us -> 76.5 us  [whole(): pl.pallas_call(kernel, out_shape=[jax.ShapeDtypeStruct(HALF, BF), jax.Sha...]
where the time goes in v9:
time: 81.4 us; the launch traced here: 81.2 us
  Pallas kernels  76.5 us (94%)
  local copies, waits for them, and re-layouts  4.11 us (5%)
    pallas_call x1, Pallas kernels, whole(): pl.pallas_call(kernel, out_shape=[jax.ShapeDtypeStruct(HALF, BF), jax.Sha...  76.5 us
    unnamed x2, local copies, waits for them, and re-layouts  4.11 us

profile of v9, /device:TPU:1, one launch (start us, length us, event | category | flops | bytes accessed | tf_op | source)
XLA Modules:
  0.0 81.2 jit_solution(13948943986444739310)
XLA Ops:
  0.6 76.5 %shard_map.104 = (bf16[2,2,72,1440]{3,2,1,0:T(8,128)(2,1)}, f32[2,24,5,2,160]{4,3,2,1,0:T(2,128)}) custom-call(bf16[2,2,72,1440]{3,2,1,0:T(8,128)(2,1)} %bitcast.9, bf16[6,160,160]{2,1,0:T(8,128)(2,1)} %leg_hbm.1, f32[7,7,24]{2,1,0:T(8,128)} %bitcast.12, bf16[320,1440]{1,0:T(8,128)(2,1)} %constant.6.clone.table_hbm, bf16[24,24]{1,0:T(8,128)(2,1)} %mix_hbm.1, ...), custom_call_target="tpu_custom_call" | custom-call | tf_op jit(solution)/shard_map/pallas_call | solution.py:580
  77.1 2.1 %copy.13 = bf16[2,24,6,1440]{3,1,2,0:T(8,128)(2,1)} copy(bf16[2,24,6,1440]{3,1,2,0:T(8,128)(2,1)} %bitcast.10) | data formatting | bytes 1658880
  79.3 2.0 %copy.14 = f32[2,24,2,160,5]{3,2,4,1,0:T(2,128)} copy(f32[2,24,2,160,5]{3,2,4,1,0:T(2,128)} %bitcast.11) | data formatting | bytes 614400
